TPU v7x, 256 devices: a whole 4x4x8 slice. The times are simulated.
256 devices in a mesh: seq: 128 (over y, x, z), head: 2 (over core).
Axes of the slice: x: 4, y: 4, z: 8, core: 2. Of those that a mesh axis runs over, the one named last changes fastest.
Arguments:
- tokens: bfloat16 [65536, 2048], P('seq', 'head'), may hold values from -6 to 6
- q_weight: bfloat16 [2048, 2048], P(None, 'head'), may hold values from -0.125 to 0.125
- key_matrix: bfloat16 [2048, 512], P(None, 'head'), may hold values from -0.125 to 0.125
- value_matrix: bfloat16 [2048, 512], P(None, 'head'), may hold values from -0.125 to 0.125
- norm_gain: float32 [2048], P('head'), may hold values from 0.1 to 1.9
- out_weight: bfloat16 [2048, 2048], P('head'), may hold values from -0.1875 to 0.1875
- doc_ids: int32 [65536], P('seq'), may hold values from 0 to 63, never falling along the last dimension, each value on 1 to 32768 neighbouring positions
Outputs:
- layer_out: bfloat16 [65536, 2048], P('seq', 'head')
Inputs may be any that keep to these rules, and one draw needn't show every extreme that they name: `doc_ids`: document numbers never fall along the window; each of the 64 documents has 1 to 32768 positions, and one has exactly 32768.
All inputs are finite; a program needn't handle non-finite values.
Results may differ from a plain program's by a relative error of at most 0.0095.
Values may be sent and summed in bfloat16 or wider, within the bound.
No kernel may reach another device: no remote copies, remote signals or barrier semaphores. Data moves between devices by JAX's collectives and lax.ppermute only.
A program may use at most 128 MiB of HBM per device.

v0:
```python
import jax
import jax.numpy as jnp
from jax import lax
from jax.sharding import PartitionSpec as P

HEAD_SIZE = 128


epsilon = 1e-05


def prefix(x, axis, join, neutral):
    place = lax.axis_index(axis)
    gathered = jax.tree.map(
        lambda a, kind: lax.all_gather(a.astype(kind), axis),
        x,
        (jnp.bfloat16, jnp.bfloat16, jnp.bfloat16),
    )
    state = jax.tree.map(lambda a, e: jnp.zeros_like(a) + jnp.asarray(e, a.dtype), x, neutral)

    def one(step, state):
        return join(
            state,
            jax.tree.map(
                lambda a, own: lax.dynamic_index_in_dim(a, step, 0, False).astype(own.dtype),
                gathered,
                x,
            ),
        )

    return lax.fori_loop(0, place, one, state)


def features(values_in):
    return jax.nn.elu(values_in) + 1.0


def join_states(earlier, latter):
    early_first, early_last, early_state = earlier
    late_first, late_last, late_state = latter
    joined = (late_first == late_last) & (early_last == late_first) & (late_first >= 0.0)
    passed = jnp.where(joined, early_state, jnp.zeros_like(early_state))
    state_sum = jnp.where(late_first < 0.0, early_state, late_state + passed)
    first_id = jnp.where(early_first < 0.0, late_first, early_first)
    last_id = jnp.where(late_last < 0.0, early_last, late_last)
    return (first_id, last_id, state_sum)


def on_device(tokens, q_weight, key_matrix, value_matrix, norm_gain, out_weight, doc_ids):
    row_count = tokens.shape[0]
    q_heads = q_weight.shape[1] // HEAD_SIZE
    kv_heads = key_matrix.shape[1] // HEAD_SIZE
    query_group_width = q_heads // kv_heads
    part_rows = lax.all_gather(tokens, "head", axis=1, tiled=True)
    raw_query = jnp.dot(part_rows, q_weight, preferred_element_type=jnp.float32)
    raw_key = jnp.dot(part_rows, key_matrix, preferred_element_type=jnp.float32)
    raw_value = jnp.dot(part_rows, value_matrix, preferred_element_type=jnp.float32)
    query_rows = (
        features(raw_query)
        .astype(jnp.bfloat16)
        .reshape(row_count, kv_heads, query_group_width, HEAD_SIZE)
    )
    key_rows = features(raw_key).astype(jnp.bfloat16).reshape(row_count, kv_heads, HEAD_SIZE)
    value_rows = raw_value.astype(jnp.bfloat16).reshape(row_count, kv_heads, HEAD_SIZE)
    first_id = doc_ids[0]
    last_id = doc_ids[row_count - 1]
    offsets = jnp.arange(row_count)
    same_doc = (offsets[:, None] >= offsets[None, :]) & (doc_ids[:, None] == doc_ids[None, :])
    scores = jnp.einsum("tkgd,skd->kgts", query_rows, key_rows, preferred_element_type=jnp.float32)
    scores = jnp.where(same_doc[None, None], scores, 0.0).astype(jnp.bfloat16)
    intra_part = jnp.einsum(
        "kgts,skd->tkgd", scores, value_rows, preferred_element_type=jnp.float32
    )
    tail_keys = jnp.where((doc_ids == last_id)[:, None, None], key_rows, jnp.zeros_like(key_rows))
    tail_state = jnp.einsum(
        "skd,ske->kde", tail_keys, value_rows, preferred_element_type=jnp.float32
    )
    first_float = first_id.astype(jnp.float32)
    last_float = last_id.astype(jnp.float32)
    identity = (jnp.float32(-1.0), jnp.float32(-1.0), jnp.zeros_like(tail_state))
    held_first, held_last, held_state = prefix(
        (first_float, last_float, tail_state), "seq", join_states, identity
    )
    incoming = jnp.where(held_last == first_float, held_state, jnp.zeros_like(held_state))
    carried_part = jnp.einsum(
        "tkgd,kde->tkge",
        query_rows,
        incoming.astype(jnp.bfloat16),
        preferred_element_type=jnp.float32,
    )
    carried_part = jnp.where((doc_ids == first_id)[:, None, None, None], carried_part, 0.0)
    combined = (intra_part + carried_part).reshape(row_count, q_heads, HEAD_SIZE)
    inv_rms = lax.rsqrt(jnp.mean(combined * combined, axis=-1, keepdims=True) + epsilon)
    normed = ((combined * inv_rms).reshape(row_count, q_heads * HEAD_SIZE) * norm_gain).astype(
        jnp.bfloat16
    )
    partial_out = jnp.dot(normed, out_weight, preferred_element_type=jnp.float32)
    return lax.psum_scatter(
        partial_out.astype(jnp.bfloat16), "head", scatter_dimension=1, tiled=True
    )


def solution(mesh):
    return jax.shard_map(
        on_device,
        mesh=mesh,
        in_specs=(
            P("seq", "head"),
            P(None, "head"),
            P(None, "head"),
            P(None, "head"),
            P("head"),
            P("head", None),
            P("seq"),
        ),
        out_specs=P("seq", "head"),
        check_vma=False,
    )
```

profile of v0, /device:TPU:1, one launch (start us, length us, event | category | flops | bytes accessed | tf_op | source)
XLA Modules:
  0.0 1214.5 jit_solution(7048437508417317613)
XLA Ops:
  6.5 0.7 all-gather.4.cloned.1.call-update
  7.3 0.0 all-gather.6.cloned.1.call-start
  7.3 1.4 fusion.33
  8.7 1.9 broadcast_compare_fusion.1
  10.6 19.0 %all-gather.4.cloned.1.call-done = bf16[512,2048]{1,0:T(8,128)(2,1)} async-done(((bf16[512,1024]{1,0:T(8,128)(2,1)}), bf16[512,2048]{1,0:T(8,128)(2,1)}) %all-gather.4.cloned.1.call-update) | async-done | bytes 2097168 | tf_op jit(solution)/shard_map/all_gather | solution.py:54
  29.6 2.6 fusion.22
  32.3 0.0 copy-done.4
  32.3 0.0 copy-done.3
  32.3 0.0 copy-start.5
  32.3 0.0 copy-start.9
  32.3 0.0 copy-start.1
  32.3 0.8 convolution_convert_fusion.1
  33.1 0.0 copy-start.7
  33.1 0.7 copy-done.7
  33.8 0.8 convolution_convert_fusion.2
  34.7 0.0 all-gather.6.cloned.1.call-update
  34.7 0.0 reduce-scatter.2.cloned.1.call-start
  36.0 0.6 dynamic-slice
  36.6 0.7 dynamic-update-slice.1
  37.4 0.7 dynamic-update-slice
  38.1 295.5 %all-reduce.2 = (bf16[128]{0:T(256)(128)(2,1)S(1)}, bf16[128]{0:T(256)(128)(2,1)S(1)}) all-reduce(bf16[128]{0:T(256)(128)(2,1)S(1)} %dynamic-update-slice, bf16[128]{0:T(256)(128)(2,1)S(1)} %dynamic-update-slice.1), channel_id=1, replica_groups=mesh['seq'=128,'head'=2] {'seq'}, use_global_device_ids=true, to_apply=%add | all-reduce | flops 256 | bytes 1024
  333.6 0.2 fusion.15
  333.8 5.8 fusion.10
  339.6 0.8 reshape.83
  340.4 0.0 all-gather.6.cloned.1.call-done
  340.4 0.0 copy-start.8
  340.4 1.8 fusion.18
  342.3 5.6 multiply_reduce_fusion
  347.9 1.8 fusion.12
  349.8 5.9 convolution_convert_fusion
  355.7 0.0 reduce-scatter.2.cloned.1.call-update
  355.7 852.2 %reduce-scatter.2.cloned.1.call-done = bf16[512,1024]{1,0:T(8,128)(2,1)} async-done(((bf16[512,2048]{1,0:T(8,128)(2,1)}), bf16[512,1024]{1,0:T(8,128)(2,1)}) %reduce-scatter.2.cloned.1.call-update) | async-done | bytes 1048592 | tf_op jit(solution)/shard_map/reduce_scatter | solution.py:98
  (19 shorter events, 0.1 us)
Async XLA Ops:
  6.5 23.1 %copy-start = (bf16[2048,256]{1,0:T(8,128)(2,1)S(1)}, bf16[2048,256]{1,0:T(8,128)(2,1)}, u32[]{:S(2)}) copy-start(bf16[2048,256]{1,0:T(8,128)(2,1)} %param.11) | copy-start | bytes 3145732
  6.5 23.1 %all-gather.4.cloned.1.call-start = ((), (), s32[]{:S(2)}) async-start(), calls=%async_computation.1 | async-start | bytes 3145728 | tf_op jit(solution)/shard_map/all_gather | solution.py:54
  7.3 333.1 %all-gather.6.cloned.1.call-start = ((), (), s32[]{:S(2)}) async-start(), calls=%async_computation.3 | async-start | bytes 8454144 | tf_op jit(solution)/shard_map/all_gather | solution.py:15
  10.6 21.7 %copy-start.4 = (bf16[2048,256]{1,0:T(8,128)(2,1)S(1)}, bf16[2048,256]{1,0:T(8,128)(2,1)}, u32[]{:S(2)}) copy-start(bf16[2048,256]{1,0:T(8,128)(2,1)} %param.12) | copy-start | bytes 3145732
  29.6 2.7 copy-start.3
  32.3 0.8 copy-start.5
  32.3 3.7 copy-start.9
  32.3 301.3 %copy-start.1 = (s32[512]{0:T(512)S(1)}, s32[512]{0:T(512)}, u32[]{:S(2)}) copy-start(s32[512]{0:T(512)} %param.15) | copy-start | bytes 6148
  33.1 0.7 copy-start.7
  34.7 1173.3 %reduce-scatter.2.cloned.1.call-start = ((), (), s32[]{:S(2)}) async-start(), calls=%async_computation.2 | async-start | bytes 3145728 | tf_op jit(solution)/shard_map/reduce_scatter | solution.py:98
  340.4 1.9 copy-start.6
  340.4 1.9 copy-start.8
  342.3 5.6 copy-start.2
Sparse Core Ops, SparseCore 0:
  9.2 20.4 all-gather.3
  34.8 121.8 all-gather.5
  355.9 852.0 reduce-scatter.1
where the time goes:
time: 1230 us; the launch traced here: 1210 us
  waiting for transfers between devices  872 us (71%)
  blocking collectives  296 us (24%)
  matrix products  23.4 us (2%)
  between operations  14.5 us (1%)
    reduce_scatter x1, waiting for transfers between devices, on_device(): lax.psum_scatter(partial_out.astype(jnp.bfloat16), 'head', scatter_dimens...  852 us
    unnamed x1, blocking collectives  296 us
  transfers between devices with their start and end apart: 3, of which 2 were waited for; matrix products, arithmetic and copies ran while one was open for 1% of the time, Pallas kernels for 0%

commit v1 on v0

v1 whole, which is shorter than its diff:
```python
import jax
import jax.numpy as jnp
from jax import lax
from jax.sharding import PartitionSpec as P

HEAD_SIZE = 128
ID_ROWS = 16
ROUNDS = ((1,), (2, 4, 6), (8, 16, 24), (32, 64, 96))

epsilon = 1e-05


def features(values_in):
    return jax.nn.elu(values_in) + 1.0


def swap_head(x):
    return lax.ppermute(x, "head", [(0, 1), (1, 0)])


def carried_state(tail_state, first_id, last_id):
    place = lax.axis_index("seq")
    count = lax.axis_size("seq")
    rows = tail_state.shape[0]
    first = jnp.broadcast_to(first_id.astype(jnp.bfloat16), (1, HEAD_SIZE))
    total_id = jnp.broadcast_to(last_id.astype(jnp.bfloat16), (1, HEAD_SIZE))
    total = tail_state.astype(jnp.bfloat16)
    held = jnp.zeros((rows, HEAD_SIZE), jnp.float32)
    for bits in ROUNDS:
        message = jnp.concatenate([total, jnp.broadcast_to(total_id, (ID_ROWS, HEAD_SIZE))])
        got = [lax.ppermute(message, "seq", [(i, i ^ b) for i in range(count)]) for b in bits]
        ids = [g[rows : rows + 1] for g in got]
        top = total_id
        for i in ids:
            top = jnp.maximum(top, i)
        new = jnp.where(total_id == top, total, 0).astype(jnp.float32)
        for b, g, i in zip(bits, got, ids):
            state = g[:rows].astype(jnp.float32)
            earlier = (place & (1 << (b.bit_length() - 1))) != 0
            held = held + jnp.where((i == first) & earlier, state, 0.0)
            new = new + jnp.where(i == top, state, 0.0)
        total, total_id = new.astype(jnp.bfloat16), top
    return held


def on_device(tokens, q_weight, key_matrix, value_matrix, norm_gain, out_weight, doc_ids):
    row_count = tokens.shape[0]
    half = tokens.shape[1]
    q_heads = q_weight.shape[1] // HEAD_SIZE
    kv_heads = key_matrix.shape[1] // HEAD_SIZE
    query_group_width = q_heads // kv_heads
    core = lax.axis_index("head")
    other = swap_head(tokens)
    part_rows = jnp.where(
        core == 0,
        jnp.concatenate([tokens, other], axis=1),
        jnp.concatenate([other, tokens], axis=1),
    )
    raw_key = jnp.dot(part_rows, key_matrix, preferred_element_type=jnp.float32)
    raw_value = jnp.dot(part_rows, value_matrix, preferred_element_type=jnp.float32)
    raw_query = jnp.dot(part_rows, q_weight, preferred_element_type=jnp.float32)
    query_rows = (
        features(raw_query)
        .astype(jnp.bfloat16)
        .reshape(row_count, kv_heads, query_group_width, HEAD_SIZE)
    )
    key_rows = features(raw_key).astype(jnp.bfloat16).reshape(row_count, kv_heads, HEAD_SIZE)
    value_rows = raw_value.astype(jnp.bfloat16).reshape(row_count, kv_heads, HEAD_SIZE)
    first_id = doc_ids[0]
    last_id = doc_ids[row_count - 1]
    tail_keys = jnp.where((doc_ids == last_id)[:, None, None], key_rows, jnp.zeros_like(key_rows))
    tail_state = jnp.einsum(
        "skd,ske->kde", tail_keys, value_rows, preferred_element_type=jnp.float32
    )
    incoming = carried_state(tail_state.reshape(kv_heads * HEAD_SIZE, HEAD_SIZE), first_id, last_id)
    incoming = incoming.reshape(kv_heads, HEAD_SIZE, HEAD_SIZE)
    offsets = jnp.arange(row_count)
    same_doc = (offsets[:, None] >= offsets[None, :]) & (doc_ids[:, None] == doc_ids[None, :])
    scores = jnp.einsum("tkgd,skd->kgts", query_rows, key_rows, preferred_element_type=jnp.float32)
    scores = jnp.where(same_doc[None, None], scores, 0.0).astype(jnp.bfloat16)
    intra_part = jnp.einsum(
        "kgts,skd->tkgd", scores, value_rows, preferred_element_type=jnp.float32
    )
    carried_part = jnp.einsum(
        "tkgd,kde->tkge",
        query_rows,
        incoming.astype(jnp.bfloat16),
        preferred_element_type=jnp.float32,
    )
    carried_part = jnp.where((doc_ids == first_id)[:, None, None, None], carried_part, 0.0)
    combined = (intra_part + carried_part).reshape(row_count, q_heads, HEAD_SIZE)
    inv_rms = lax.rsqrt(jnp.mean(combined * combined, axis=-1, keepdims=True) + epsilon)
    normed = ((combined * inv_rms).reshape(row_count, q_heads * HEAD_SIZE) * norm_gain).astype(
        jnp.bfloat16
    )
    theirs = jnp.dot(
        normed,
        lax.dynamic_slice_in_dim(out_weight, (1 - core) * half, half, 1),
        preferred_element_type=jnp.float32,
    )
    received = swap_head(theirs.astype(jnp.bfloat16))
    mine = jnp.dot(
        normed,
        lax.dynamic_slice_in_dim(out_weight, core * half, half, 1),
        preferred_element_type=jnp.float32,
    )
    return (mine + received.astype(jnp.float32)).astype(jnp.bfloat16)


def solution(mesh):
    return jax.shard_map(
        on_device,
        mesh=mesh,
        in_specs=(
            P("seq", "head"),
            P(None, "head"),
            P(None, "head"),
            P(None, "head"),
            P("head"),
            P("head", None),
            P("seq"),
        ),
        out_specs=P("seq", "head"),
        check_vma=False,
    )
```

time: 1230 us -> 80.1 us (0.07); the launches traced: 1210 us -> 79.7 us
  waiting for transfers between devices: 872 us -> 18.9 us
  blocking collectives: 296 us -> 0 us
  starting transfers between devices: 0.08 us -> 22.4 us
  between operations: 14.5 us -> 1.63 us
    reduce_scatter x1 -> x0, waiting for transfers between devices: 852 us -> none  [on_device(): lax.psum_scatter(partial_out.astype(jnp.bfloat16), 'head', scatter_dimens...]
    unnamed x1 -> x0, blocking collectives: 296 us -> none
    ppermute x0 -> x12, starting transfers between devices: none -> 22.4 us  [the longest x10 13.8 us: carried_state(): lax.ppermute(message, 'seq', [(i, i ^ b) for i in range(count)])]
    all_gather x2 -> x0, waiting for transfers between devices: 19 us -> none  [the longest x1 19 us: on_device(): part_rows = lax.all_gather(tokens, 'head', axis=1, tiled=True)]
    ppermute x0 -> x12, waiting for transfers between devices: none -> 18.9 us  [the longest x10 16.4 us: carried_state(): lax.ppermute(message, 'seq', [(i, i ^ b) for i in range(count)])]
  transfers between devices with their start and end apart: 3 -> 12, of which waited for: 2 -> 7; matrix products, arithmetic and copies ran while one was open for 1% -> 15% of each run, Pallas kernels for 0% -> 0%
where the time goes in v1:
time: 80.1 us; the launch traced here: 79.7 us
  matrix products  25.6 us (32%)
  starting transfers between devices  22.4 us (28%)
  waiting for transfers between devices  18.9 us (24%)
  other arithmetic  8.56 us (11%)
  local copies, waits for them, and re-layouts  2.74 us (3%)
  between operations  1.63 us (2%)
    ppermute x10, waiting for transfers between devices, carried_state(): lax.ppermute(message, 'seq', [(i, i ^ b) for i in range(count)])  16.4 us
    ppermute x10, starting transfers between devices, carried_state(): lax.ppermute(message, 'seq', [(i, i ^ b) for i in range(count)])  13.8 us
    ppermute x2, starting transfers between devices, swap_head(): return lax.ppermute(x, 'head', [(0, 1), (1, 0)])  8.58 us
    dot_general x1, matrix products, on_device(): raw_query = jnp.dot(part_rows, q_weight, preferred_element_type=jnp.float32)  6.4 us
    dot_general x1, matrix products, on_device(): jnp.einsum('kgts,skd->tkgd', scores, value_rows, preferred_element_type=j...  5.57 us
    dot_general x1, matrix products, on_device(): jnp.dot(normed, lax.dynamic_slice_in_dim(out_weight, (1 - core) * half, h...  3.84 us
    dot_general x1, matrix products, on_device(): jnp.dot(normed, lax.dynamic_slice_in_dim(out_weight, core * half, half, 1...  3.83 us
    dot_general x1, matrix products, on_device(): jnp.dot(part_rows, value_matrix, preferred_element_type=jnp.float32)  2.82 us
  transfers between devices with their start and end apart: 12, of which 7 were waited for; matrix products, arithmetic and copies ran while one was open for 15% of the time, Pallas kernels for 0%

profile of v1, /device:TPU:1, one launch (start us, length us, event | category | flops | bytes accessed | tf_op | source)
XLA Modules:
  0.0 79.7 jit_solution(6723903440789947073)
XLA Ops:
  0.0 3.2 %collective-permute-start = (bf16[512,1024]{1,0:T(8,128)(2,1)}, bf16[512,1024]{1,0:T(8,128)(2,1)S(1)}, u32[]{:S(2)}, u32[]{:S(2)}) collective-permute-start(bf16[512,1024]{1,0:T(8,128)(2,1)} %param.7), channel_id=1, source_target_pairs={{0,1},{1,0},{2,3},{3,2},{4,5},{5,4},{6,7},{7,6},{8,9},{9,8},{10,11... | collective-permute-start | bytes 3145736 | tf_op jit(solution)/shard_map/ppermute | solution.py:18
  3.2 1.3 %fusion.60 = (s32[1]{0:T(128)}, s32[1]{0:T(128)}) fusion(s32[512]{0:T(512)} %param.13), kind=kLoop, calls=%fused_computation.107 | loop fusion | bytes 16 | tf_op jit(solution)/shard_map/slice | solution.py:69
  5.2 2.6 %broadcast_compare_fusion.1 = (pred[512]{0:T(512)(128)(4,1)}, pred[512]{0:T(512)(128)(4,1)S(1)}) fusion(s32[512]{0:T(512)} %param.13, s32[]{:T(128)} %bitcast.8, s32[]{:T(128)} %bitcast.9), kind=kLoop, calls=%fused_computation.97 | loop fusion | flops 1024 | bytes 3080 | tf_op jit(solution)/shard_map/eq | solution.py:90
  7.8 2.8 %convolution_convert_fusion = bf16[512,256]{0,1:T(8,128)(2,1)S(1)} fusion(bf16[2048,256]{1,0:T(8,128)(2,1)S(1)} %copy-done, bf16[512,1024]{1,0:T(8,128)(2,1)S(1)} %collective-permute-done, bf16[512,1024]{1,0:T(8,128)(2,1)} %param.7, pred[]{:T(512)S(6)} %eq.92), kind=kOutput, calls=%fused_computation.25 | convolution fusion | flops 546439168 | bytes 3407873 | tf_op jit(solution)/shard_map/dot_general | solution.py:60
  10.7 1.0 %fusion.30 = bf16[512,256]{0,1:T(8,128)(2,1)S(1)} fusion(bf16[2048,256]{1,0:T(8,128)(2,1)S(1)} %copy-done.9, bf16[512,1024]{1,0:T(8,128)(2,1)S(1)} %collective-permute-done, bf16[512,1024]{1,0:T(8,128)(2,1)S(1)} %copy-done.10, pred[]{:T(512)S(6)} %eq.92), kind=kOutput, calls=%fused_computation.34 | convolution fusion | flops 546963456 | bytes 3407873 | tf_op jit(solution)/shard_map/dot_general | solution.py:59
  12.8 3.1 %collective-permute-done.1 = bf16[272,128]{1,0:T(8,128)(2,1)S(1)} collective-permute-done((bf16[272,128]{1,0:T(8,128)(2,1)S(1)}, bf16[272,128]{1,0:T(8,128)(2,1)S(1)}, u32[]{:S(2)}, u32[]{:S(2)}) %collective-permute-start.1) | collective-permute-done | bytes 69664 | tf_op jit(solution)/shard_map/ppermute | solution.py:31
  15.9 0.5 copy-done.5
  16.5 1.5 %collective-permute-start.2 = (bf16[272,128]{1,0:T(8,128)(2,1)S(1)}, bf16[272,128]{1,0:T(8,128)(2,1)S(1)}, u32[]{:S(2)}, u32[]{:S(2)}) collective-permute-start(bf16[272,128]{1,0:T(8,128)(2,1)S(1)} %pad_maximum_fusion), channel_id=1, source_target_pairs={{0,4},{2,6},{4,0},{6,2},{8,12},{10,14},{12,8},{14,10},{16,20},{18,... | collective-permute-start | bytes 208904 | tf_op jit(solution)/shard_map/ppermute | solution.py:31
  18.0 4.8 %collective-permute-start.3 = (bf16[272,128]{1,0:T(8,128)(2,1)S(1)}, bf16[272,128]{1,0:T(8,128)(2,1)S(1)}, u32[]{:S(2)}, u32[]{:S(2)}) collective-permute-start(bf16[272,128]{1,0:T(8,128)(2,1)S(1)} %pad_maximum_fusion), channel_id=1, source_target_pairs={{0,8},{2,10},{4,12},{6,14},{8,0},{10,2},{12,4},{14,6},{16,24},{18,... | collective-permute-start | bytes 208904 | tf_op jit(solution)/shard_map/ppermute | solution.py:31
  22.9 2.7 %collective-permute-done.3 = bf16[272,128]{1,0:T(8,128)(2,1)S(1)} collective-permute-done((bf16[272,128]{1,0:T(8,128)(2,1)S(1)}, bf16[272,128]{1,0:T(8,128)(2,1)S(1)}, u32[]{:S(2)}, u32[]{:S(2)}) %collective-permute-start.3) | collective-permute-done | bytes 69664 | tf_op jit(solution)/shard_map/ppermute | solution.py:31
  25.6 3.0 %collective-permute-done.4 = bf16[272,128]{1,0:T(8,128)(2,1)S(1)} collective-permute-done((bf16[272,128]{1,0:T(8,128)(2,1)S(1)}, bf16[272,128]{1,0:T(8,128)(2,1)S(1)}, u32[]{:S(2)}, u32[]{:S(2)}) %collective-permute-start.4) | collective-permute-done | bytes 69664 | tf_op jit(solution)/shard_map/ppermute | solution.py:31
  28.6 0.6 compare_bitcast_fusion.7
  29.3 1.3 %collective-permute-start.5 = (bf16[272,128]{1,0:T(8,128)(2,1)S(1)}, bf16[272,128]{1,0:T(8,128)(2,1)S(1)}, u32[]{:S(2)}, u32[]{:S(2)}) collective-permute-start(bf16[272,128]{1,0:T(8,128)(2,1)S(1)} %pad_maximum_fusion.1), channel_id=1, source_target_pairs={{0,16},{2,18},{4,20},{6,22},{8,24},{10,26},{12,28},{14,30},{16,0},... | collective-permute-start | bytes 208904 | tf_op jit(solution)/shard_map/ppermute | solution.py:31
  30.6 2.4 %collective-permute-start.6 = (bf16[272,128]{1,0:T(8,128)(2,1)S(1)}, bf16[272,128]{1,0:T(8,128)(2,1)S(1)}, u32[]{:S(2)}, u32[]{:S(2)}) collective-permute-start(bf16[272,128]{1,0:T(8,128)(2,1)S(1)} %pad_maximum_fusion.1), channel_id=1, source_target_pairs={{0,32},{2,34},{4,36},{6,38},{8,40},{10,42},{12,44},{14,46},{16,48}... | collective-permute-start | bytes 208904 | tf_op jit(solution)/shard_map/ppermute | solution.py:31
  33.5 2.0 %collective-permute-done.6 = bf16[272,128]{1,0:T(8,128)(2,1)S(1)} collective-permute-done((bf16[272,128]{1,0:T(8,128)(2,1)S(1)}, bf16[272,128]{1,0:T(8,128)(2,1)S(1)}, u32[]{:S(2)}, u32[]{:S(2)}) %collective-permute-start.6) | collective-permute-done | bytes 69664 | tf_op jit(solution)/shard_map/ppermute | solution.py:31
  35.5 1.9 %collective-permute-done.7 = bf16[272,128]{1,0:T(8,128)(2,1)S(1)} collective-permute-done((bf16[272,128]{1,0:T(8,128)(2,1)S(1)}, bf16[272,128]{1,0:T(8,128)(2,1)S(1)}, u32[]{:S(2)}, u32[]{:S(2)}) %collective-permute-start.7) | collective-permute-done | bytes 69664 | tf_op jit(solution)/shard_map/ppermute | solution.py:31
  37.4 0.6 compare_bitcast_fusion.3
  38.1 0.6 pad_maximum_fusion.2
  38.8 2.7 %collective-permute-start.10 = (bf16[272,128]{1,0:T(8,128)(2,1)}, bf16[272,128]{1,0:T(8,128)(2,1)}, u32[]{:S(2)}, u32[]{:S(2)}) collective-permute-start(bf16[272,128]{1,0:T(8,128)(2,1)} %pad_maximum_fusion.2), channel_id=1, source_target_pairs={{0,192},{2,194},{4,196},{6,198},{8,200},{10,202},{12,204},{14,206}... | collective-permute-start | bytes 208904 | tf_op jit(solution)/shard_map/ppermute | solution.py:31
  41.5 6.4 %fusion.9 = bf16[512,1024]{1,0:T(8,128)(2,1)S(1)} fusion(bf16[2048,1024]{1,0:T(8,128)(2,1)} %param.8, bf16[512,1024]{1,0:T(8,128)(2,1)} %copy-done.11, bf16[512,1024]{1,0:T(8,128)(2,1)} %param.7, pred[]{:T(512)S(6)} %eq.92), kind=kOutput, calls=%fused_computation.10 | convolution fusion | flops 2159542272 | bytes 7340033 | tf_op jit(solution)/shard_map/dot_general | solution.py:61
  47.9 0.8 reshape.81
  48.7 0.4 collective-permute-start.9
  49.4 0.7 and_bitcast_fusion
  50.1 3.6 %collective-permute-done.9 = bf16[272,128]{1,0:T(8,128)(2,1)S(1)} collective-permute-done((bf16[272,128]{1,0:T(8,128)(2,1)}, bf16[272,128]{1,0:T(8,128)(2,1)S(1)}, u32[]{:S(2)}, u32[]{:S(2)}) %collective-permute-start.9) | collective-permute-done | bytes 69664 | tf_op jit(solution)/shard_map/ppermute | solution.py:31
  53.7 1.2 %fusion.42 = bf16[256,128]{1,0:T(8,128)(2,1)S(1)} fusion(bf16[272,128]{1,0:T(8,128)(2,1)} %collective-permute-done.10, bf16[272,128]{1,0:T(8,128)(2,1)S(1)} %collective-permute-done.9, bf16[272,128]{1,0:T(8,128)(2,1)S(1)} %collective-permute-done.8, pred[128]{0:T(512)(128)(4,1)S(1)} %and_bitcast_fusion, pred[128]{0:T(512)(128)(4,1)S(1)} %and_bitcast_fusion.1, ...), kind=kLoop, calls=%fused_computation.60 | loop fusion | flops 983040 | bytes 722176 | tf_op jit(solution)/shard_map/convert_element_type | solution.py:87
  54.9 1.9 %fusion.26 = f32[2,128,512,4]{2,1,3,0:T(8,128)} fusion(bf16[2,128,128,1]{2,1,3,0:T(8,128)(2,1)S(1)} %bitcast.95, bf16[512,2,4,128]{3,2,1,0:T(4,128)(2,1)S(1)} %reshape.81), kind=kOutput, calls=%fused_computation.30 | convolution fusion | flops 134217728 | bytes 3211264 | tf_op jit(solution)/shard_map/tkgd,kde->tkge/dot_general | solution.py:84
  56.7 5.6 %multiply_reduce_fusion = (f32[512,2,4]{0,2,1:T(4,128)S(1)}, f32[512,2,4,128]{0,3,2,1:T(8,128)}) fusion(f32[2,128,512,4]{2,1,3,0:T(8,128)} %fusion.26, pred[512]{0:T(512)(128)(4,1)S(1)} %copy-done.8, bf16[512,2,128,1]{0,2,3,1:T(8,128)(2,1)S(1)} %bitcast.100, pred[512,512]{1,0:T(8,128)(4,1)S(1)} %fusion.23, bf16[512,2,128,1]{0,2,3,1:T(8,128)(2,1)S(1)} %bitcast.102, ...), kind=kOutput, calls=%fused_computation.21 | convolution fusion | flops 1080029184 | bytes 6046208 | tf_op jit(solution)/shard_map/kgts,skd->tkgd/dot_general | solution.py:81
  62.4 1.8 %fusion.11 = bf16[512,1024]{0,1:T(8,128)(2,1)S(1)} fusion(f32[512,2,4,128]{0,3,2,1:T(8,128)} %get-tuple-element.29, f32[1024]{0:T(1024)S(1)} %copy-done.7, f32[512,8]{0,1:T(8,128)S(1)} %rsqrt.12), kind=kLoop, calls=%fused_computation.14 | loop fusion | flops 1572864 | bytes 3166208 | tf_op jit(solution)/shard_map/convert_element_type | solution.py:93
  64.2 3.8 %fusion.18 = bf16[512,1024]{1,0:T(8,128)(2,1)} fusion(bf16[512,1024]{0,1:T(8,128)(2,1)S(1)} %fusion.11, bf16[1024,2048]{1,0:T(8,128)(2,1)} %param.12, s32[]{:T(128)S(6)} %select_n.142), kind=kOutput, calls=%fused_computation.24 | convolution fusion | flops 1074266112 | bytes 4194308 | tf_op jit(solution)/shard_map/dot_general | solution.py:96
  68.1 5.3 %collective-permute-start.11 = (bf16[512,1024]{1,0:T(8,128)(2,1)}, bf16[512,1024]{1,0:T(8,128)(2,1)S(1)}, u32[]{:S(2)}, u32[]{:S(2)}) collective-permute-start(bf16[512,1024]{1,0:T(8,128)(2,1)} %fusion.18), channel_id=1, source_target_pairs={{0,1},{1,0},{2,3},{3,2},{4,5},{5,4},{6,7},{7,6},{8,9},{9,8},{10,11... | collective-permute-start | bytes 3145736 | tf_op jit(solution)/shard_map/ppermute | solution.py:18
  73.4 2.5 %collective-permute-done.11 = bf16[512,1024]{1,0:T(8,128)(2,1)S(1)} collective-permute-done((bf16[512,1024]{1,0:T(8,128)(2,1)}, bf16[512,1024]{1,0:T(8,128)(2,1)S(1)}, u32[]{:S(2)}, u32[]{:S(2)}) %collective-permute-start.11) | collective-permute-done | bytes 1048608 | tf_op jit(solution)/shard_map/ppermute | solution.py:18
  75.9 3.8 %add_convert_fusion = bf16[512,1024]{1,0:T(8,128)(2,1)} fusion(bf16[512,1024]{1,0:T(8,128)(2,1)S(1)} %collective-permute-done.11, bf16[512,1024]{0,1:T(8,128)(2,1)S(1)} %fusion.11, bf16[1024,2048]{1,0:T(8,128)(2,1)} %param.12, s32[]{:T(128)S(6)} %select_n.141), kind=kOutput, calls=%fused_computation.16 | convolution fusion | flops 1075314688 | bytes 5242884 | tf_op jit(solution)/shard_map/dot_general | solution.py:102
  (59 shorter events, 1.3 us)
Async XLA Ops:
  0.0 7.8 %copy-start = (bf16[2048,256]{1,0:T(8,128)(2,1)S(1)}, bf16[2048,256]{1,0:T(8,128)(2,1)}, u32[]{:S(2)}) copy-start(bf16[2048,256]{1,0:T(8,128)(2,1)} %param.10) | copy-start | bytes 3145732
  0.0 7.8 %collective-permute-start = (bf16[512,1024]{1,0:T(8,128)(2,1)}, bf16[512,1024]{1,0:T(8,128)(2,1)S(1)}, u32[]{:S(2)}, u32[]{:S(2)}) collective-permute-start(bf16[512,1024]{1,0:T(8,128)(2,1)} %param.7), channel_id=1, source_target_pairs={{0,1},{1,0},{2,3},{3,2},{4,5},{5,4},{6,7},{7,6},{8,9},{9,8},{10,11... | collective-permute-start | bytes 3145736 | tf_op jit(solution)/shard_map/ppermute | solution.py:18
  7.8 2.9 %copy-start.9 = (bf16[2048,256]{1,0:T(8,128)(2,1)S(1)}, bf16[2048,256]{1,0:T(8,128)(2,1)}, u32[]{:S(2)}) copy-start(bf16[2048,256]{1,0:T(8,128)(2,1)} %param.9) | copy-start | bytes 3145732
  7.8 2.9 %copy-start.10 = (bf16[512,1024]{1,0:T(8,128)(2,1)S(1)}, bf16[512,1024]{1,0:T(8,128)(2,1)}, u32[]{:S(2)}) copy-start(bf16[512,1024]{1,0:T(8,128)(2,1)} %param.7) | copy-start | bytes 3145732
  7.8 2.8 %copy-start.11 = (bf16[512,1024]{1,0:T(8,128)(2,1)}, bf16[512,1024]{1,0:T(8,128)(2,1)S(1)}, u32[]{:S(2)}) copy-start(bf16[512,1024]{1,0:T(8,128)(2,1)S(1)} %collective-permute-done) | copy-start | bytes 3145732
  10.7 1.1 %copy-start.12 = (bf16[512,256]{0,1:T(8,128)(2,1)}, bf16[512,256]{0,1:T(8,128)(2,1)S(1)}, u32[]{:S(2)}) copy-start(bf16[512,256]{0,1:T(8,128)(2,1)S(1)} %convolution_convert_fusion) | copy-start | bytes 786436
  10.7 22.6 %copy-start.6 = (s32[512]{0:T(512)S(1)}, s32[512]{0:T(512)}, u32[]{:S(2)}) copy-start(s32[512]{0:T(512)} %param.13) | copy-start | bytes 6148
  11.7 1.0 %copy-start.14 = (bf16[512,256]{0,1:T(8,128)(2,1)}, bf16[512,256]{0,1:T(8,128)(2,1)S(1)}, u32[]{:S(2)}) copy-start(bf16[512,256]{0,1:T(8,128)(2,1)S(1)} %fusion.30) | copy-start | bytes 786436
  12.0 3.9 %collective-permute-start.1 = (bf16[272,128]{1,0:T(8,128)(2,1)S(1)}, bf16[272,128]{1,0:T(8,128)(2,1)S(1)}, u32[]{:S(2)}, u32[]{:S(2)}) collective-permute-start(bf16[272,128]{1,0:T(8,128)(2,1)S(1)} %concatenate.20), channel_id=1, source_target_pairs={{0,2},{2,0},{4,6},{6,4},{8,10},{10,8},{12,14},{14,12},{16,18},{18,... | collective-permute-start | bytes 208904 | tf_op jit(solution)/shard_map/ppermute | solution.py:31
  15.9 0.6 copy-start.5
  16.5 6.4 %collective-permute-start.2 = (bf16[272,128]{1,0:T(8,128)(2,1)S(1)}, bf16[272,128]{1,0:T(8,128)(2,1)S(1)}, u32[]{:S(2)}, u32[]{:S(2)}) collective-permute-start(bf16[272,128]{1,0:T(8,128)(2,1)S(1)} %pad_maximum_fusion), channel_id=1, source_target_pairs={{0,4},{2,6},{4,0},{6,2},{8,12},{10,14},{12,8},{14,10},{16,20},{18,... | collective-permute-start | bytes 208904 | tf_op jit(solution)/shard_map/ppermute | solution.py:31
  18.0 7.6 %collective-permute-start.3 = (bf16[272,128]{1,0:T(8,128)(2,1)S(1)}, bf16[272,128]{1,0:T(8,128)(2,1)S(1)}, u32[]{:S(2)}, u32[]{:S(2)}) collective-permute-start(bf16[272,128]{1,0:T(8,128)(2,1)S(1)} %pad_maximum_fusion), channel_id=1, source_target_pairs={{0,8},{2,10},{4,12},{6,14},{8,0},{10,2},{12,4},{14,6},{16,24},{18,... | collective-permute-start | bytes 208904 | tf_op jit(solution)/shard_map/ppermute | solution.py:31
  22.8 5.7 %collective-permute-start.4 = (bf16[272,128]{1,0:T(8,128)(2,1)S(1)}, bf16[272,128]{1,0:T(8,128)(2,1)S(1)}, u32[]{:S(2)}, u32[]{:S(2)}) collective-permute-start(bf16[272,128]{1,0:T(8,128)(2,1)S(1)} %pad_maximum_fusion), channel_id=1, source_target_pairs={{0,12},{2,14},{4,8},{6,10},{8,4},{10,6},{12,0},{14,2},{16,28},{18,... | collective-permute-start | bytes 208904 | tf_op jit(solution)/shard_map/ppermute | solution.py:31
  28.6 4.5 %copy-start.1 = (bf16[272,128]{1,0:T(8,128)(2,1)}, bf16[272,128]{1,0:T(8,128)(2,1)S(1)}, u32[]{:S(2)}) copy-start(bf16[272,128]{1,0:T(8,128)(2,1)S(1)} %collective-permute-done.4) | copy-start | bytes 208900
  29.3 4.2 %collective-permute-start.5 = (bf16[272,128]{1,0:T(8,128)(2,1)S(1)}, bf16[272,128]{1,0:T(8,128)(2,1)S(1)}, u32[]{:S(2)}, u32[]{:S(2)}) collective-permute-start(bf16[272,128]{1,0:T(8,128)(2,1)S(1)} %pad_maximum_fusion.1), channel_id=1, source_target_pairs={{0,16},{2,18},{4,20},{6,22},{8,24},{10,26},{12,28},{14,30},{16,0},... | collective-permute-start | bytes 208904 | tf_op jit(solution)/shard_map/ppermute | solution.py:31
  30.6 4.9 %collective-permute-start.6 = (bf16[272,128]{1,0:T(8,128)(2,1)S(1)}, bf16[272,128]{1,0:T(8,128)(2,1)S(1)}, u32[]{:S(2)}, u32[]{:S(2)}) collective-permute-start(bf16[272,128]{1,0:T(8,128)(2,1)S(1)} %pad_maximum_fusion.1), channel_id=1, source_target_pairs={{0,32},{2,34},{4,36},{6,38},{8,40},{10,42},{12,44},{14,46},{16,48}... | collective-permute-start | bytes 208904 | tf_op jit(solution)/shard_map/ppermute | solution.py:31
  33.1 4.4 %collective-permute-start.7 = (bf16[272,128]{1,0:T(8,128)(2,1)S(1)}, bf16[272,128]{1,0:T(8,128)(2,1)S(1)}, u32[]{:S(2)}, u32[]{:S(2)}) collective-permute-start(bf16[272,128]{1,0:T(8,128)(2,1)S(1)} %pad_maximum_fusion.1), channel_id=1, source_target_pairs={{0,48},{2,50},{4,52},{6,54},{8,56},{10,58},{12,60},{14,62},{16,32}... | collective-permute-start | bytes 208904 | tf_op jit(solution)/shard_map/ppermute | solution.py:31
  33.5 8.0 %copy-start.2 = (bf16[272,128]{1,0:T(8,128)(2,1)}, bf16[272,128]{1,0:T(8,128)(2,1)S(1)}, u32[]{:S(2)}) copy-start(bf16[272,128]{1,0:T(8,128)(2,1)S(1)} %collective-permute-done.5) | copy-start | bytes 208900
  35.5 6.0 %copy-start.3 = (bf16[272,128]{1,0:T(8,128)(2,1)}, bf16[272,128]{1,0:T(8,128)(2,1)S(1)}, u32[]{:S(2)}) copy-start(bf16[272,128]{1,0:T(8,128)(2,1)S(1)} %collective-permute-done.6) | copy-start | bytes 208900
  37.4 4.1 %copy-start.4 = (bf16[272,128]{1,0:T(8,128)(2,1)}, bf16[272,128]{1,0:T(8,128)(2,1)S(1)}, u32[]{:S(2)}) copy-start(bf16[272,128]{1,0:T(8,128)(2,1)S(1)} %collective-permute-done.7) | copy-start | bytes 208900
  38.8 10.6 %collective-permute-start.10 = (bf16[272,128]{1,0:T(8,128)(2,1)}, bf16[272,128]{1,0:T(8,128)(2,1)}, u32[]{:S(2)}, u32[]{:S(2)}) collective-permute-start(bf16[272,128]{1,0:T(8,128)(2,1)} %pad_maximum_fusion.2), channel_id=1, source_target_pairs={{0,192},{2,194},{4,196},{6,198},{8,200},{10,202},{12,204},{14,206}... | collective-permute-start | bytes 208904 | tf_op jit(solution)/shard_map/ppermute | solution.py:31
  48.7 8.1 %copy-start.8 = (pred[512]{0:T(512)(128)(4,1)S(1)}, pred[512]{0:T(512)(128)(4,1)}, u32[]{:S(2)}) copy-start(pred[512]{0:T(512)(128)(4,1)} %get-tuple-element.18) | copy-start | bytes 1540
  48.7 8.1 %copy-start.13 = (bf16[512,256]{0,1:T(8,128)(2,1)S(1)}, bf16[512,256]{0,1:T(8,128)(2,1)}, u32[]{:S(2)}) copy-start(bf16[512,256]{0,1:T(8,128)(2,1)} %copy-done.12) | copy-start | bytes 786436
  48.7 8.0 %copy-start.15 = (bf16[512,256]{0,1:T(8,128)(2,1)S(1)}, bf16[512,256]{0,1:T(8,128)(2,1)}, u32[]{:S(2)}) copy-start(bf16[512,256]{0,1:T(8,128)(2,1)} %copy-done.14) | copy-start | bytes 786436
  48.7 5.0 %collective-permute-start.9 = (bf16[272,128]{1,0:T(8,128)(2,1)}, bf16[272,128]{1,0:T(8,128)(2,1)S(1)}, u32[]{:S(2)}, u32[]{:S(2)}) collective-permute-start(bf16[272,128]{1,0:T(8,128)(2,1)} %pad_maximum_fusion.2), channel_id=1, source_target_pairs={{0,128},{2,130},{4,132},{6,134},{8,136},{10,138},{12,140},{14,142}... | collective-permute-start | bytes 208904 | tf_op jit(solution)/shard_map/ppermute | solution.py:31
  49.1 4.5 %collective-permute-start.8 = (bf16[272,128]{1,0:T(8,128)(2,1)}, bf16[272,128]{1,0:T(8,128)(2,1)S(1)}, u32[]{:S(2)}, u32[]{:S(2)}) collective-permute-start(bf16[272,128]{1,0:T(8,128)(2,1)} %pad_maximum_fusion.2), channel_id=1, source_target_pairs={{0,64},{2,66},{4,68},{6,70},{8,72},{10,74},{12,76},{14,78},{16,80}... | collective-permute-start | bytes 208904 | tf_op jit(solution)/shard_map/ppermute | solution.py:31
  56.7 5.6 %copy-start.7 = (f32[1024]{0:T(1024)S(1)}, f32[1024]{0:T(1024)}, u32[]{:S(2)}) copy-start(f32[1024]{0:T(1024)} %param.11) | copy-start | bytes 12292
  68.1 7.8 %collective-permute-start.11 = (bf16[512,1024]{1,0:T(8,128)(2,1)}, bf16[512,1024]{1,0:T(8,128)(2,1)S(1)}, u32[]{:S(2)}, u32[]{:S(2)}) collective-permute-start(bf16[512,1024]{1,0:T(8,128)(2,1)} %fusion.18), channel_id=1, source_target_pairs={{0,1},{1,0},{2,3},{3,2},{4,5},{5,4},{6,7},{7,6},{8,9},{9,8},{10,11... | collective-permute-start | bytes 3145736 | tf_op jit(solution)/shard_map/ppermute | solution.py:18

commit v2 on v1

v2 whole, which is shorter than its diff:
```python
import jax
import jax.numpy as jnp
from jax import lax
from jax.experimental import pallas as pl
from jax.experimental.pallas import tpu as pltpu
from jax.sharding import PartitionSpec as P

HEAD = 128
ID_ROWS = 16
BLOCK = 256
ROUNDS = ((1,), (2, 4, 6), (8, 16, 24), (32, 64, 96))
INTRA_STEPS = (1, 2)
EPSILON = 1e-05
F32 = jnp.float32
BF16 = jnp.bfloat16

SMEM = pl.BlockSpec(memory_space=pltpu.SMEM)
VMEM = pl.BlockSpec(memory_space=pltpu.VMEM)


def params(mib):
    return pltpu.CompilerParams(vmem_limit_bytes=mib << 20)


def dot(a, b):
    return jnp.dot(a, b, preferred_element_type=F32)


def features(x):
    return jnp.where(x > 0.0, x + 1.0, jnp.exp(jnp.minimum(x, 0.0)))


def project(core_ref, own_ref, other_ref, weight_ref):
    half = own_ref.shape[1]
    mine = pl.multiple_of(core_ref[0] * half, half)
    theirs = pl.multiple_of((1 - core_ref[0]) * half, half)
    return dot(own_ref[...], weight_ref[pl.ds(mine, half), :]) + dot(
        other_ref[...], weight_ref[pl.ds(theirs, half), :]
    )


def key_value_kernel(core_ref, own_ref, other_ref, wk_ref, wv_ref, col_ref, k_ref, v_ref, message_ref):
    rows = own_ref.shape[0]
    key = features(project(core_ref, own_ref, other_ref, wk_ref)).astype(BF16)
    value = project(core_ref, own_ref, other_ref, wv_ref).astype(BF16)
    k_ref[...] = key
    v_ref[...] = value
    last = col_ref[rows - 1 : rows, :]
    tail = col_ref[...] == last
    heads = key.shape[1] // HEAD
    for h in range(heads):
        cut = slice(h * HEAD, (h + 1) * HEAD)
        tail_key = jnp.where(tail, key[:, cut].astype(F32), 0.0).astype(BF16)
        state = lax.dot_general(
            tail_key, value[:, cut], (((0,), (0,)), ((), ())), preferred_element_type=F32
        )
        message_ref[cut, :] = state.astype(BF16)
    message_ref[heads * HEAD :, :] = jnp.broadcast_to(last, (ID_ROWS, HEAD)).astype(BF16)


def intra_kernel(core_ref, own_ref, other_ref, wq_ref, k_ref, v_ref, col_ref, row_ref, q_ref, intra_ref):
    rows = own_ref.shape[0]
    group = wq_ref.shape[1] // HEAD
    q_ref[...] = features(project(core_ref, own_ref, other_ref, wq_ref)).astype(BF16)
    for start in range(0, rows, BLOCK):
        seen = start + BLOCK
        here = slice(start, seen)
        key = k_ref[:seen, :]
        value = v_ref[:seen, :]
        t = lax.broadcasted_iota(jnp.int32, (BLOCK, seen), 0) + start
        s = lax.broadcasted_iota(jnp.int32, (BLOCK, seen), 1)
        same = (col_ref[here, :1] == row_ref[:1, :seen]) & (t >= s)
        for g in range(group):
            cut = slice(g * HEAD, (g + 1) * HEAD)
            scores = lax.dot_general(
                q_ref[here, cut], key, (((1,), (1,)), ((), ())), preferred_element_type=F32
            )
            scores = jnp.where(same, scores, 0.0).astype(BF16)
            intra_ref[here, cut] = dot(scores, value)


def combine_kernel(bits, has_held, place_ref, first_ref, message_ref, *refs):
    got = refs[: len(bits)]
    held_in = refs[len(bits)] if has_held else None
    next_ref, held_ref = refs[-2:]
    rows = message_ref.shape[0] - ID_ROWS
    own_id = message_ref[rows : rows + 1, :].astype(F32)
    ids = [g[rows : rows + 1, :].astype(F32) for g in got]
    top = own_id
    for i in ids:
        top = jnp.maximum(top, i)
    first = first_ref[:1, :]
    total = jnp.where(own_id == top, message_ref[:rows, :].astype(F32), 0.0)
    held = held_in[...] if has_held else jnp.zeros((rows, HEAD), F32)
    for b, g, i in zip(bits, got, ids):
        state = g[:rows, :].astype(F32)
        earlier = (place_ref[0] & (1 << (b.bit_length() - 1))) != 0
        held = held + jnp.where((i == first) & earlier, state, 0.0)
        total = total + jnp.where(i == top, state, 0.0)
    next_ref[:rows, :] = total.astype(BF16)
    next_ref[rows:, :] = jnp.broadcast_to(top, (ID_ROWS, HEAD)).astype(BF16)
    held_ref[...] = held


def norm_kernel(bits, groups, core_ref, place_ref, first_ref, held_ref, *refs):
    got = refs[: len(bits)]
    queries = refs[len(bits) : len(bits) + groups]
    intras = refs[len(bits) + groups : len(bits) + 2 * groups]
    col_ref, gain_ref, weight_ref, normed_ref, theirs_ref = refs[len(bits) + 2 * groups :]
    first = first_ref[:1, :]
    rows = held_ref.shape[0]
    held = held_ref[...]
    for b, g in zip(bits, got):
        earlier = (place_ref[0] & (1 << (b.bit_length() - 1))) != 0
        same = (g[rows : rows + 1, :].astype(F32) == first) & earlier
        held = held + jnp.where(same, g[:rows, :].astype(F32), 0.0)
    incoming = held.astype(BF16)
    for start in range(0, col_ref.shape[0], BLOCK):
        here = slice(start, start + BLOCK)
        joins = col_ref[here, :] == first
        for k in range(groups):
            width = queries[k].shape[1]
            for g in range(width // HEAD):
                cut = slice(g * HEAD, (g + 1) * HEAD)
                out = slice(k * width + g * HEAD, k * width + (g + 1) * HEAD)
                carried = dot(queries[k][here, cut], incoming[k * HEAD : (k + 1) * HEAD, :])
                combined = intras[k][here, cut] + jnp.where(joins, carried, 0.0)
                scale = lax.rsqrt(jnp.mean(combined * combined, axis=-1, keepdims=True) + EPSILON)
                normed_ref[here, out] = (combined * scale * gain_ref[:1, out]).astype(BF16)
        theirs_ref[here, :] = dot(normed_ref[here, :], columns(weight_ref, 1 - core_ref[0])).astype(BF16)


def columns(weight_ref, part):
    half = weight_ref.shape[1] // 2
    return weight_ref[:, pl.ds(pl.multiple_of(part * half, half), half)]


def own_kernel(core_ref, normed_ref, weight_ref, out_ref):
    out_ref[...] = dot(normed_ref[...], columns(weight_ref, core_ref[0]))


def shape(dims, dtype):
    return jax.ShapeDtypeStruct(dims, dtype)


def swap_head(x):
    return lax.ppermute(x, "head", [(0, 1), (1, 0)])


def on_device(tokens, q_weight, key_matrix, value_matrix, norm_gain, out_weight, doc_ids):
    rows, half = tokens.shape
    kv_width = key_matrix.shape[1]
    q_width = q_weight.shape[1]
    kv_heads = kv_width // HEAD
    group_width = q_width // kv_heads
    state_rows = kv_heads * HEAD
    count = lax.axis_size("seq")
    core = lax.axis_index("head").astype(jnp.int32).reshape(1)
    place = lax.axis_index("seq").astype(jnp.int32).reshape(1)
    other = swap_head(tokens)
    ids = doc_ids.astype(F32)
    col = jnp.broadcast_to(ids[:, None], (rows, HEAD))
    row = jnp.broadcast_to(ids[None, :], (8, rows))
    first = jnp.broadcast_to(ids[:1, None], (8, HEAD))
    gain = jnp.broadcast_to(norm_gain[None, :], (8, q_width))

    key, value, message = pl.pallas_call(
        key_value_kernel,
        out_shape=(
            shape((rows, kv_width), BF16),
            shape((rows, kv_width), BF16),
            shape((state_rows + ID_ROWS, HEAD), BF16),
        ),
        in_specs=[SMEM] + [VMEM] * 5,
        out_specs=(VMEM, VMEM, VMEM),
        compiler_params=params(24),
        name="key_value",
    )(core, tokens, other, key_matrix, value_matrix, col)

    def intra(k, key, value):
        return pl.pallas_call(
            intra_kernel,
            out_shape=(shape((rows, group_width), BF16), shape((rows, group_width), F32)),
            grid=(1,),
            in_specs=[
                SMEM,
                VMEM,
                VMEM,
                pl.BlockSpec((2 * half, group_width), lambda i: (0, k)),
                pl.BlockSpec((rows, HEAD), lambda i: (0, k)),
                pl.BlockSpec((rows, HEAD), lambda i: (0, k)),
                VMEM,
                VMEM,
            ],
            out_specs=(VMEM, VMEM),
            compiler_params=params(24),
            name=f"intra_{k}",
        )(core, tokens, other, q_weight, key, value, col, row)

    held = None
    queries, intras = [], []
    for step, bits in enumerate(ROUNDS):
        got = [lax.ppermute(message, "seq", [(i, i ^ b) for i in range(count)]) for b in bits]
        if step in INTRA_STEPS:
            (key, value), _ = lax.optimization_barrier(((key, value), message))
            query, part = intra(INTRA_STEPS.index(step), key, value)
            queries.append(query)
            intras.append(part)
        if step == len(ROUNDS) - 1:
            break
        extra = () if held is None else (held,)
        message, held = pl.pallas_call(
            lambda *refs, bits=bits, has=held is not None: combine_kernel(bits, has, *refs),
            out_shape=(shape(message.shape, BF16), shape((state_rows, HEAD), F32)),
            in_specs=[SMEM] + [VMEM] * (2 + len(bits) + len(extra)),
            out_specs=(VMEM, VMEM),
            compiler_params=params(4),
            name="combine",
        )(place, first, message, *got, *extra)
        if step in INTRA_STEPS:
            message, queries[-1] = lax.optimization_barrier((message, queries[-1]))

    normed, theirs = pl.pallas_call(
        lambda *refs: norm_kernel(ROUNDS[-1], kv_heads, *refs),
        out_shape=(shape((rows, q_width), BF16), shape((rows, half), BF16)),
        in_specs=[SMEM, SMEM] + [VMEM] * (2 + len(got) + 2 * kv_heads + 3),
        out_specs=(VMEM, VMEM),
        compiler_params=params(32),
        name="norm",
    )(core, place, first, held, *got, *queries, *intras, col, gain, out_weight)
    received = swap_head(theirs)
    mine = pl.pallas_call(
        own_kernel,
        out_shape=shape((rows, half), F32),
        in_specs=[SMEM, VMEM, VMEM],
        out_specs=VMEM,
        compiler_params=params(32),
        name="own",
    )(core, normed, out_weight)
    return (mine + received.astype(F32)).astype(BF16)


def solution(mesh):
    return jax.shard_map(
        on_device,
        mesh=mesh,
        in_specs=(
            P("seq", "head"),
            P(None, "head"),
            P(None, "head"),
            P(None, "head"),
            P("head"),
            P("head", None),
            P("seq"),
        ),
        out_specs=P("seq", "head"),
        check_vma=False,
    )
```

time: 80.1 us -> 54 us (0.67)
  matrix products: 25.6 us -> 0 us
  Pallas kernels: 0 us -> 10.6 us
  other arithmetic: 8.56 us -> 2.02 us
  waiting for transfers between devices: 18.9 us -> 13.1 us
  local copies, waits for them, and re-layouts: 2.74 us -> 7.09 us
  starting transfers between devices: 22.4 us -> 20.8 us
  between operations: 1.63 us -> 0.14 us
    dot_general x8 -> x0, matrix products: 25.6 us -> none  [the longest x1 6.4 us: on_device(): raw_query = jnp.dot(part_rows, q_weight, preferred_element_type=jnp.float32)]
    pallas_call x0 -> x8, Pallas kernels: none -> 10.6 us  [the longest x2 5.54 us: intra(): pl.pallas_call(intra_kernel, out_shape=(shape((rows, group_width), BF16),...]
    ppermute x10, waiting for transfers between devices: 16.4 us -> 10.3 us  [on_device(): lax.ppermute(message, 'seq', [(i, i ^ b) for i in range(count)])]
    unnamed x32 -> x14, local copies, waits for them, and re-layouts: 0.61 us -> 5.88 us
    eq x1 -> x0, other arithmetic: 2.56 us -> none  [on_device(): doc_ids == first_id]
    broadcast_in_dim x9 -> x0, other arithmetic: 1.96 us -> none  [the longest x3 1.23 us: carried_state(): new = jnp.where(total_id == top, total, 0).astype(jnp.float32)]
    ppermute x2, starting transfers between devices: 8.58 us -> 7.35 us  [swap_head(): return lax.ppermute(x, 'head', [(0, 1), (1, 0)])]
    convert_element_type x5 -> x2, other arithmetic: 3.17 us -> 2.02 us  [the longest x1 1.33 us: on_device(): return (mine + received.astype(F32)).astype(BF16)]
  transfers between devices with their start and end apart: 12 -> 12, of which waited for: 7 -> 8; matrix products, arithmetic and copies ran while one was open for 15% -> 2% of each run, Pallas kernels for 0% -> 13%
where the time goes in v2:
time: 54 us; the launch traced here: 53.8 us
  starting transfers between devices  20.8 us (39%)
  waiting for transfers between devices  13.1 us (24%)
  Pallas kernels  10.6 us (20%)
  local copies, waits for them, and re-layouts  7.09 us (13%)
  other arithmetic  2.02 us (4%)
    ppermute x10, starting transfers between devices, on_device(): lax.ppermute(message, 'seq', [(i, i ^ b) for i in range(count)])  13.5 us
    ppermute x10, waiting for transfers between devices, on_device(): lax.ppermute(message, 'seq', [(i, i ^ b) for i in range(count)])  10.3 us
    ppermute x2, starting transfers between devices, swap_head(): return lax.ppermute(x, 'head', [(0, 1), (1, 0)])  7.35 us
    unnamed x14, local copies, waits for them, and re-layouts  5.88 us
    pallas_call x2, Pallas kernels, intra(): pl.pallas_call(intra_kernel, out_shape=(shape((rows, group_width), BF16),...  5.54 us
    ppermute x2, waiting for transfers between devices, swap_head(): return lax.ppermute(x, 'head', [(0, 1), (1, 0)])  2.84 us
    pallas_call x1, Pallas kernels, on_device(): pl.pallas_call(lambda *refs: norm_kernel(ROUNDS[-1], kv_heads, *refs), ou...  2.05 us
    pallas_call x1, Pallas kernels, on_device(): pl.pallas_call(key_value_kernel, out_shape=(shape((rows, kv_width), BF16)...  1.52 us
  transfers between devices with their start and end apart: 12, of which 8 were waited for; matrix products, arithmetic and copies ran while one was open for 2% of the time, Pallas kernels for 13%

profile of v2, /device:TPU:1, one launch (start us, length us, event | category | flops | bytes accessed | tf_op | source)
XLA Modules:
  0.0 53.8 jit_solution(1777822362808500341)
XLA Ops:
  0.0 3.2 %collective-permute-start = (bf16[512,1024]{1,0:T(8,128)(2,1)}, bf16[512,1024]{1,0:T(8,128)(2,1)S(1)}, u32[]{:S(2)}, u32[]{:S(2)}) collective-permute-start(bf16[512,1024]{1,0:T(8,128)(2,1)} %own_ref.5), channel_id=1, source_target_pairs={{0,1},{1,0},{2,3},{3,2},{4,5},{5,4},{6,7},{7,6},{8,9},{9,8},{10,11... | collective-permute-start | bytes 3145736 | tf_op jit(solution)/shard_map/ppermute | solution.py:147
  3.2 0.7 %convert_element_type.9 = f32[512]{0:T(512)S(1)} convert(s32[512]{0:T(512)} %param.13) | non-fusion elementwise | flops 512 | bytes 4096 | tf_op jit(solution)/shard_map/convert_element_type | solution.py:161
  3.9 1.8 %collective-permute-done.other_ref = bf16[512,1024]{1,0:T(8,128)(2,1)S(1)} collective-permute-done((bf16[512,1024]{1,0:T(8,128)(2,1)}, bf16[512,1024]{1,0:T(8,128)(2,1)S(1)}, u32[]{:S(2)}, u32[]{:S(2)}) %collective-permute-start) | collective-permute-done | bytes 1048608 | tf_op jit(solution)/shard_map/ppermute | solution.py:147
  5.9 1.2 %copy-done.2 = bf16[512,1024]{1,0:T(8,128)(2,1)S(1)} copy-done((bf16[512,1024]{1,0:T(8,128)(2,1)S(1)}, bf16[512,1024]{1,0:T(8,128)(2,1)}, u32[]{:S(2)}) %copy-start.2) | copy-done | bytes 1048600
  7.1 1.2 %copy-done.4 = bf16[2048,256]{1,0:T(8,128)(2,1)S(1)} copy-done((bf16[2048,256]{1,0:T(8,128)(2,1)S(1)}, bf16[2048,256]{1,0:T(8,128)(2,1)}, u32[]{:S(2)}) %copy-start.4) | copy-done | bytes 1048600
  8.3 1.2 %copy-done.5 = bf16[2048,256]{1,0:T(8,128)(2,1)S(1)} copy-done((bf16[2048,256]{1,0:T(8,128)(2,1)S(1)}, bf16[2048,256]{1,0:T(8,128)(2,1)}, u32[]{:S(2)}) %copy-start.5) | copy-done | bytes 1048600
  9.6 1.5 %key_value.1 = (bf16[512,256]{1,0:T(8,128)(2,1)S(1)}, bf16[512,256]{1,0:T(8,128)(2,1)S(1)}, bf16[272,128]{1,0:T(8,128)(2,1)S(1)}) custom-call(s32[1]{0:T(128)} %bitcast.core_ref.refs_0_, bf16[512,1024]{1,0:T(8,128)(2,1)S(1)} %copy-done.2, bf16[512,1024]{1,0:T(8,128)(2,1)S(1)} %collective-permute-done.other_ref, bf16[2048,256]{1,0:T(8,128)(2,1)S(1)} %copy-done.4, ...), custom_call_target="tpu_custom_call" | custom-call | tf_op jit(solution)/shard_map/key_value/pallas_call | solution.py:167
  11.2 0.5 slice.3
  11.7 2.6 %collective-permute-done.1.refs_3_ = bf16[272,128]{1,0:T(8,128)(2,1)S(1)} collective-permute-done((bf16[272,128]{1,0:T(8,128)(2,1)S(1)}, bf16[272,128]{1,0:T(8,128)(2,1)S(1)}, u32[]{:S(2)}, u32[]{:S(2)}) %collective-permute-start.1) | collective-permute-done | bytes 69664 | tf_op jit(solution)/shard_map/ppermute | solution.py:203
  14.3 0.6 %broadcast_in_dim.11.refs_1_.refs_2_ = f32[8,128]{1,0:T(8,128)S(1)} broadcast(f32[]{:T(128)} %bitcast.2), dimensions={} | broadcast | bytes 4100 | tf_op jit(solution)/shard_map/broadcast_in_dim | solution.py:164
  15.0 4.4 %collective-permute-start.4 = (bf16[272,128]{1,0:T(8,128)(2,1)S(1)}, bf16[272,128]{1,0:T(8,128)(2,1)S(1)}, u32[]{:S(2)}, u32[]{:S(2)}) collective-permute-start(bf16[272,128]{1,0:T(8,128)(2,1)S(1)} %get-tuple-element.29.refs_2_), channel_id=1, source_target_pairs={{0,12},{2,14},{4,8},{6,10},{8,4},{10,6},{12,0},{14,2},{16,28},{18,... | collective-permute-start | bytes 208904 | tf_op jit(solution)/shard_map/ppermute | solution.py:203
  19.3 1.0 %collective-permute-start.3 = (bf16[272,128]{1,0:T(8,128)(2,1)S(1)}, bf16[272,128]{1,0:T(8,128)(2,1)S(1)}, u32[]{:S(2)}, u32[]{:S(2)}) collective-permute-start(bf16[272,128]{1,0:T(8,128)(2,1)S(1)} %get-tuple-element.29.refs_2_), channel_id=1, source_target_pairs={{0,8},{2,10},{4,12},{6,14},{8,0},{10,2},{12,4},{14,6},{16,24},{18,... | collective-permute-start | bytes 208904 | tf_op jit(solution)/shard_map/ppermute | solution.py:203
  20.3 1.2 %collective-permute-start.2 = (bf16[272,128]{1,0:T(8,128)(2,1)S(1)}, bf16[272,128]{1,0:T(8,128)(2,1)S(1)}, u32[]{:S(2)}, u32[]{:S(2)}) collective-permute-start(bf16[272,128]{1,0:T(8,128)(2,1)S(1)} %get-tuple-element.29.refs_2_), channel_id=1, source_target_pairs={{0,4},{2,6},{4,0},{6,2},{8,12},{10,14},{12,8},{14,10},{16,20},{18,... | collective-permute-start | bytes 208904 | tf_op jit(solution)/shard_map/ppermute | solution.py:203
  21.5 2.2 %copy-done = bf16[2048,1024]{1,0:T(8,128)(2,1)S(1)} copy-done((bf16[2048,1024]{1,0:T(8,128)(2,1)S(1)}, bf16[2048,1024]{1,0:T(8,128)(2,1)}, u32[]{:S(2)}) %copy-start) | copy-done | bytes 4194328
  23.7 2.8 %intra_0.1 = (bf16[512,512]{1,0:T(8,128)(2,1)S(1)}, f32[512,512]{1,0:T(8,128)S(1)}) custom-call(s32[1]{0:T(128)} %bitcast.core_ref.refs_0_, bf16[512,1024]{1,0:T(8,128)(2,1)S(1)} %copy-done.3, bf16[512,1024]{1,0:T(8,128)(2,1)S(1)} %collective-permute-done.other_ref, bf16[2048,1024]{1,0:T(8,128)(2,1)S(1)} %copy-done, ...), custom_call_target="tpu_custom_call" | custom-call | tf_op jit(solution)/shard_map/intra_0/pallas_call | solution.py:181
  26.5 0.8 %collective-permute-done.3.refs_4_ = bf16[272,128]{1,0:T(8,128)(2,1)S(1)} collective-permute-done((bf16[272,128]{1,0:T(8,128)(2,1)S(1)}, bf16[272,128]{1,0:T(8,128)(2,1)S(1)}, u32[]{:S(2)}, u32[]{:S(2)}) %collective-permute-start.3) | collective-permute-done | bytes 69664 | tf_op jit(solution)/shard_map/ppermute | solution.py:203
  27.3 1.7 %collective-permute-done.2.refs_3_ = bf16[272,128]{1,0:T(8,128)(2,1)S(1)} collective-permute-done((bf16[272,128]{1,0:T(8,128)(2,1)S(1)}, bf16[272,128]{1,0:T(8,128)(2,1)S(1)}, u32[]{:S(2)}, u32[]{:S(2)}) %collective-permute-start.2) | collective-permute-done | bytes 69664 | tf_op jit(solution)/shard_map/ppermute | solution.py:203
  29.1 2.6 %collective-permute-start.7 = (bf16[272,128]{1,0:T(8,128)(2,1)S(1)}, bf16[272,128]{1,0:T(8,128)(2,1)S(1)}, u32[]{:S(2)}, u32[]{:S(2)}) collective-permute-start(bf16[272,128]{1,0:T(8,128)(2,1)S(1)} %get-tuple-element.37.refs_2_), channel_id=1, source_target_pairs={{0,48},{2,50},{4,52},{6,54},{8,56},{10,58},{12,60},{14,62},{16,32}... | collective-permute-start | bytes 208904 | tf_op jit(solution)/shard_map/ppermute | solution.py:203
  31.6 0.5 collective-permute-start.6
  32.1 0.3 collective-permute-start.5
  32.4 2.8 %intra_1.1 = (bf16[512,512]{1,0:T(8,128)(2,1)S(1)}, f32[512,512]{1,0:T(8,128)S(1)}) custom-call(s32[1]{0:T(128)} %bitcast.core_ref.refs_0_, bf16[512,1024]{1,0:T(8,128)(2,1)S(1)} %copy-done.3, bf16[512,1024]{1,0:T(8,128)(2,1)S(1)} %collective-permute-done.other_ref, bf16[2048,1024]{1,0:T(8,128)(2,1)S(1)} %copy-done, ...), custom_call_target="tpu_custom_call" | custom-call | tf_op jit(solution)/shard_map/intra_1/pallas_call | solution.py:181
  35.2 1.1 %collective-permute-done.6.refs_4_ = bf16[272,128]{1,0:T(8,128)(2,1)S(1)} collective-permute-done((bf16[272,128]{1,0:T(8,128)(2,1)S(1)}, bf16[272,128]{1,0:T(8,128)(2,1)S(1)}, u32[]{:S(2)}, u32[]{:S(2)}) %collective-permute-start.6) | collective-permute-done | bytes 69664 | tf_op jit(solution)/shard_map/ppermute | solution.py:203
  36.4 2.8 %collective-permute-start.10 = (bf16[272,128]{1,0:T(8,128)(2,1)S(1)}, bf16[272,128]{1,0:T(8,128)(2,1)S(1)}, u32[]{:S(2)}, u32[]{:S(2)}) collective-permute-start(bf16[272,128]{1,0:T(8,128)(2,1)S(1)} %get-tuple-element.44), channel_id=1, source_target_pairs={{0,192},{2,194},{4,196},{6,198},{8,200},{10,202},{12,204},{14,206}... | collective-permute-start | bytes 208904 | tf_op jit(solution)/shard_map/ppermute | solution.py:203
  39.2 0.4 collective-permute-start.9
  39.6 0.3 collective-permute-start.8
  39.9 1.3 %collective-permute-done.10.refs_6_ = bf16[272,128]{1,0:T(8,128)(2,1)S(1)} collective-permute-done((bf16[272,128]{1,0:T(8,128)(2,1)S(1)}, bf16[272,128]{1,0:T(8,128)(2,1)S(1)}, u32[]{:S(2)}, u32[]{:S(2)}) %collective-permute-start.10) | collective-permute-done | bytes 69664 | tf_op jit(solution)/shard_map/ppermute | solution.py:203
  41.2 2.7 %collective-permute-done.9.refs_5_ = bf16[272,128]{1,0:T(8,128)(2,1)S(1)} collective-permute-done((bf16[272,128]{1,0:T(8,128)(2,1)S(1)}, bf16[272,128]{1,0:T(8,128)(2,1)S(1)}, u32[]{:S(2)}, u32[]{:S(2)}) %collective-permute-start.9) | collective-permute-done | bytes 69664 | tf_op jit(solution)/shard_map/ppermute | solution.py:203
  44.0 2.1 %norm.1 = (bf16[512,1024]{1,0:T(8,128)(2,1)S(1)}, bf16[512,1024]{1,0:T(8,128)(2,1)S(1)}) custom-call(s32[1]{0:T(128)} %bitcast.core_ref.refs_0_, s32[1]{0:T(128)} %bitcast.1.refs_0_.refs_1_, f32[8,128]{1,0:T(8,128)S(1)} %broadcast_in_dim.11.refs_1_.refs_2_, f32[256,128]{1,0:T(8,128)S(1)} %get-tuple-element.39.refs_3_, ...), custom_call_target="tpu_custom_call" | custom-call | tf_op jit(solution)/shard_map/norm/pallas_call | solution.py:223
  46.0 4.1 %collective-permute-start.11 = (bf16[512,1024]{1,0:T(8,128)(2,1)S(1)}, bf16[512,1024]{1,0:T(8,128)(2,1)S(1)}, u32[]{:S(2)}, u32[]{:S(2)}) collective-permute-start(bf16[512,1024]{1,0:T(8,128)(2,1)S(1)} %get-tuple-element.50), channel_id=1, source_target_pairs={{0,1},{1,0},{2,3},{3,2},{4,5},{5,4},{6,7},{7,6},{8,9},{9,8},{10,11... | collective-permute-start | bytes 3145736 | tf_op jit(solution)/shard_map/ppermute | solution.py:147
  50.1 1.3 %own.1 = f32[512,1024]{1,0:T(8,128)S(1)} custom-call(s32[1]{0:T(128)} %bitcast.core_ref.refs_0_, bf16[512,1024]{1,0:T(8,128)(2,1)S(1)} %get-tuple-element.49.normed_ref, bf16[1024,2048]{1,0:T(8,128)(2,1)S(1)} %copy-done.1), custom_call_target="tpu_custom_call" | custom-call | tf_op jit(solution)/shard_map/own/pallas_call | solution.py:232
  51.4 1.0 %collective-permute-done.11 = bf16[512,1024]{1,0:T(8,128)(2,1)S(1)} collective-permute-done((bf16[512,1024]{1,0:T(8,128)(2,1)S(1)}, bf16[512,1024]{1,0:T(8,128)(2,1)S(1)}, u32[]{:S(2)}, u32[]{:S(2)}) %collective-permute-start.11) | collective-permute-done | bytes 1048608 | tf_op jit(solution)/shard_map/ppermute | solution.py:147
  52.4 1.3 %add_convert_fusion = bf16[512,1024]{1,0:T(8,128)(2,1)} fusion(f32[512,1024]{1,0:T(8,128)S(1)} %own.1, bf16[512,1024]{1,0:T(8,128)(2,1)S(1)} %collective-permute-done.11), kind=kLoop, calls=%fused_computation | loop fusion | flops 1572864 | bytes 4194304 | tf_op jit(solution)/shard_map/convert_element_type | solution.py:240
  (21 shorter events, 0.5 us)
Async XLA Ops:
  0.0 5.7 %collective-permute-start = (bf16[512,1024]{1,0:T(8,128)(2,1)}, bf16[512,1024]{1,0:T(8,128)(2,1)S(1)}, u32[]{:S(2)}, u32[]{:S(2)}) collective-permute-start(bf16[512,1024]{1,0:T(8,128)(2,1)} %own_ref.5), channel_id=1, source_target_pairs={{0,1},{1,0},{2,3},{3,2},{4,5},{5,4},{6,7},{7,6},{8,9},{9,8},{10,11... | collective-permute-start | bytes 3145736 | tf_op jit(solution)/shard_map/ppermute | solution.py:147
  5.9 1.2 %copy-start.2 = (bf16[512,1024]{1,0:T(8,128)(2,1)S(1)}, bf16[512,1024]{1,0:T(8,128)(2,1)}, u32[]{:S(2)}) copy-start(bf16[512,1024]{1,0:T(8,128)(2,1)} %own_ref.5) | copy-start | bytes 3145732
  7.1 1.2 %copy-start.4 = (bf16[2048,256]{1,0:T(8,128)(2,1)S(1)}, bf16[2048,256]{1,0:T(8,128)(2,1)}, u32[]{:S(2)}) copy-start(bf16[2048,256]{1,0:T(8,128)(2,1)} %wk_ref.1) | copy-start | bytes 3145732
  8.3 1.2 %copy-start.5 = (bf16[2048,256]{1,0:T(8,128)(2,1)S(1)}, bf16[2048,256]{1,0:T(8,128)(2,1)}, u32[]{:S(2)}) copy-start(bf16[2048,256]{1,0:T(8,128)(2,1)} %wv_ref.1) | copy-start | bytes 3145732
  9.6 12.0 %copy-start.3 = (bf16[512,1024]{1,0:T(8,128)(2,1)S(1)}, bf16[512,1024]{1,0:T(8,128)(2,1)}, u32[]{:S(2)}) copy-start(bf16[512,1024]{1,0:T(8,128)(2,1)} %own_ref.5) | copy-start | bytes 3145732
  11.1 3.2 %collective-permute-start.1 = (bf16[272,128]{1,0:T(8,128)(2,1)S(1)}, bf16[272,128]{1,0:T(8,128)(2,1)S(1)}, u32[]{:S(2)}, u32[]{:S(2)}) collective-permute-start(bf16[272,128]{1,0:T(8,128)(2,1)S(1)} %get-tuple-element.28.refs_2_), channel_id=1, source_target_pairs={{0,2},{2,0},{4,6},{6,4},{8,10},{10,8},{12,14},{14,12},{16,18},{18,... | collective-permute-start | bytes 208904 | tf_op jit(solution)/shard_map/ppermute | solution.py:203
  15.0 11.5 %collective-permute-start.4 = (bf16[272,128]{1,0:T(8,128)(2,1)S(1)}, bf16[272,128]{1,0:T(8,128)(2,1)S(1)}, u32[]{:S(2)}, u32[]{:S(2)}) collective-permute-start(bf16[272,128]{1,0:T(8,128)(2,1)S(1)} %get-tuple-element.29.refs_2_), channel_id=1, source_target_pairs={{0,12},{2,14},{4,8},{6,10},{8,4},{10,6},{12,0},{14,2},{16,28},{18,... | collective-permute-start | bytes 208904 | tf_op jit(solution)/shard_map/ppermute | solution.py:203
  19.3 8.0 %collective-permute-start.3 = (bf16[272,128]{1,0:T(8,128)(2,1)S(1)}, bf16[272,128]{1,0:T(8,128)(2,1)S(1)}, u32[]{:S(2)}, u32[]{:S(2)}) collective-permute-start(bf16[272,128]{1,0:T(8,128)(2,1)S(1)} %get-tuple-element.29.refs_2_), channel_id=1, source_target_pairs={{0,8},{2,10},{4,12},{6,14},{8,0},{10,2},{12,4},{14,6},{16,24},{18,... | collective-permute-start | bytes 208904 | tf_op jit(solution)/shard_map/ppermute | solution.py:203
  20.3 8.6 %collective-permute-start.2 = (bf16[272,128]{1,0:T(8,128)(2,1)S(1)}, bf16[272,128]{1,0:T(8,128)(2,1)S(1)}, u32[]{:S(2)}, u32[]{:S(2)}) collective-permute-start(bf16[272,128]{1,0:T(8,128)(2,1)S(1)} %get-tuple-element.29.refs_2_), channel_id=1, source_target_pairs={{0,4},{2,6},{4,0},{6,2},{8,12},{10,14},{12,8},{14,10},{16,20},{18,... | collective-permute-start | bytes 208904 | tf_op jit(solution)/shard_map/ppermute | solution.py:203
  21.5 2.2 %copy-start = (bf16[2048,1024]{1,0:T(8,128)(2,1)S(1)}, bf16[2048,1024]{1,0:T(8,128)(2,1)}, u32[]{:S(2)}) copy-start(bf16[2048,1024]{1,0:T(8,128)(2,1)} %wq_ref.3) | copy-start | bytes 12582916
  29.1 14.9 %copy-start.6 = (f32[1024]{0:T(1024)S(1)}, f32[1024]{0:T(1024)}, u32[]{:S(2)}) copy-start(f32[1024]{0:T(1024)} %param.11) | copy-start | bytes 12292
  29.1 14.9 %copy-start.1 = (bf16[1024,2048]{1,0:T(8,128)(2,1)S(1)}, bf16[1024,2048]{1,0:T(8,128)(2,1)}, u32[]{:S(2)}) copy-start(bf16[1024,2048]{1,0:T(8,128)(2,1)} %weight_ref.1) | copy-start | bytes 12582916
  29.1 6.1 %collective-permute-start.7 = (bf16[272,128]{1,0:T(8,128)(2,1)S(1)}, bf16[272,128]{1,0:T(8,128)(2,1)S(1)}, u32[]{:S(2)}, u32[]{:S(2)}) collective-permute-start(bf16[272,128]{1,0:T(8,128)(2,1)S(1)} %get-tuple-element.37.refs_2_), channel_id=1, source_target_pairs={{0,48},{2,50},{4,52},{6,54},{8,56},{10,58},{12,60},{14,62},{16,32}... | collective-permute-start | bytes 208904 | tf_op jit(solution)/shard_map/ppermute | solution.py:203
  31.6 4.7 %collective-permute-start.6 = (bf16[272,128]{1,0:T(8,128)(2,1)S(1)}, bf16[272,128]{1,0:T(8,128)(2,1)S(1)}, u32[]{:S(2)}, u32[]{:S(2)}) collective-permute-start(bf16[272,128]{1,0:T(8,128)(2,1)S(1)} %get-tuple-element.37.refs_2_), channel_id=1, source_target_pairs={{0,32},{2,34},{4,36},{6,38},{8,40},{10,42},{12,44},{14,46},{16,48}... | collective-permute-start | bytes 208904 | tf_op jit(solution)/shard_map/ppermute | solution.py:203
  32.1 4.2 %collective-permute-start.5 = (bf16[272,128]{1,0:T(8,128)(2,1)S(1)}, bf16[272,128]{1,0:T(8,128)(2,1)S(1)}, u32[]{:S(2)}, u32[]{:S(2)}) collective-permute-start(bf16[272,128]{1,0:T(8,128)(2,1)S(1)} %get-tuple-element.37.refs_2_), channel_id=1, source_target_pairs={{0,16},{2,18},{4,20},{6,22},{8,24},{10,26},{12,28},{14,30},{16,0},... | collective-permute-start | bytes 208904 | tf_op jit(solution)/shard_map/ppermute | solution.py:203
  36.4 4.8 %collective-permute-start.10 = (bf16[272,128]{1,0:T(8,128)(2,1)S(1)}, bf16[272,128]{1,0:T(8,128)(2,1)S(1)}, u32[]{:S(2)}, u32[]{:S(2)}) collective-permute-start(bf16[272,128]{1,0:T(8,128)(2,1)S(1)} %get-tuple-element.44), channel_id=1, source_target_pairs={{0,192},{2,194},{4,196},{6,198},{8,200},{10,202},{12,204},{14,206}... | collective-permute-start | bytes 208904 | tf_op jit(solution)/shard_map/ppermute | solution.py:203
  39.2 4.7 %collective-permute-start.9 = (bf16[272,128]{1,0:T(8,128)(2,1)S(1)}, bf16[272,128]{1,0:T(8,128)(2,1)S(1)}, u32[]{:S(2)}, u32[]{:S(2)}) collective-permute-start(bf16[272,128]{1,0:T(8,128)(2,1)S(1)} %get-tuple-element.44), channel_id=1, source_target_pairs={{0,128},{2,130},{4,132},{6,134},{8,136},{10,138},{12,140},{14,142}... | collective-permute-start | bytes 208904 | tf_op jit(solution)/shard_map/ppermute | solution.py:203
  39.6 4.4 %collective-permute-start.8 = (bf16[272,128]{1,0:T(8,128)(2,1)S(1)}, bf16[272,128]{1,0:T(8,128)(2,1)S(1)}, u32[]{:S(2)}, u32[]{:S(2)}) collective-permute-start(bf16[272,128]{1,0:T(8,128)(2,1)S(1)} %get-tuple-element.44), channel_id=1, source_target_pairs={{0,64},{2,66},{4,68},{6,70},{8,72},{10,74},{12,76},{14,78},{16,80}... | collective-permute-start | bytes 208904 | tf_op jit(solution)/shard_map/ppermute | solution.py:203
  46.0 6.4 %collective-permute-start.11 = (bf16[512,1024]{1,0:T(8,128)(2,1)S(1)}, bf16[512,1024]{1,0:T(8,128)(2,1)S(1)}, u32[]{:S(2)}, u32[]{:S(2)}) collective-permute-start(bf16[512,1024]{1,0:T(8,128)(2,1)S(1)} %get-tuple-element.50), channel_id=1, source_target_pairs={{0,1},{1,0},{2,3},{3,2},{4,5},{5,4},{6,7},{7,6},{8,9},{9,8},{10,11... | collective-permute-start | bytes 3145736 | tf_op jit(solution)/shard_map/ppermute | solution.py:147

commit v3 on v2

--- a/solution.py
+++ b/solution.py
@@ -8,14 +8,16 @@
 HEAD = 128
 ID_ROWS = 16
 BLOCK = 256
-ROUNDS = ((1,), (2, 4, 6), (8, 16, 24), (32, 64, 96))
+ROUNDS = ((1,), (2, 6, 4), (8, 24, 16), (32, 96, 64))
 INTRA_STEPS = (1, 2)
+CHUNKS = 2
 EPSILON = 1e-05
 F32 = jnp.float32
 BF16 = jnp.bfloat16
 
 SMEM = pl.BlockSpec(memory_space=pltpu.SMEM)
 VMEM = pl.BlockSpec(memory_space=pltpu.VMEM)
+HBM = pl.BlockSpec(memory_space=pltpu.HBM)
 
 
 def params(mib):
@@ -39,10 +41,51 @@
     )
 
 
-def key_value_kernel(core_ref, own_ref, other_ref, wk_ref, wv_ref, col_ref, k_ref, v_ref, message_ref):
-    rows = own_ref.shape[0]
-    key = features(project(core_ref, own_ref, other_ref, wk_ref)).astype(BF16)
-    value = project(core_ref, own_ref, other_ref, wv_ref).astype(BF16)
+def own_half_kernel(core_ref, ids_ref, own_hbm, wk_hbm, wv_hbm, *refs):
+    own_ref, wk_ref, wv_ref, k_ref, v_ref, col_ref, row_ref, sems = refs
+    half = own_hbm.shape[1]
+    chunk = half // CHUNKS
+    near = core_ref[0] * half
+    far = pl.multiple_of((1 - core_ref[0]) * half, half)
+    copies = []
+    for c in range(CHUNKS):
+        cut = pl.ds(pl.multiple_of(near + c * chunk, chunk), chunk)
+        copies.append((own_hbm.at[:, c * chunk : (c + 1) * chunk], own_ref.at[:, c * chunk : (c + 1) * chunk]))
+        copies.append((wk_hbm.at[cut, :], wk_ref.at[cut, :]))
+        copies.append((wv_hbm.at[cut, :], wv_ref.at[cut, :]))
+    cut = pl.ds(far, half)
+    copies.append((wk_hbm.at[cut, :], wk_ref.at[cut, :]))
+    copies.append((wv_hbm.at[cut, :], wv_ref.at[cut, :]))
+    copies = [pltpu.make_async_copy(a, b, sems.at[i]) for i, (a, b) in enumerate(copies)]
+    for copy in copies:
+        copy.start()
+    ids = ids_ref[...].astype(F32)
+    row_ref[...] = jnp.broadcast_to(ids, row_ref.shape)
+    col_ref[...] = jnp.broadcast_to(ids, (HEAD, ids.shape[1])).T
+    for c in range(CHUNKS):
+        for copy in copies[3 * c : 3 * c + 3]:
+            copy.wait()
+        own = own_ref[:, c * chunk : (c + 1) * chunk]
+        cut = pl.ds(pl.multiple_of(near + c * chunk, chunk), chunk)
+        key = dot(own, wk_ref[cut, :])
+        value = dot(own, wv_ref[cut, :])
+        if c == 0:
+            k_ref[...] = key
+            v_ref[...] = value
+        else:
+            k_ref[...] += key
+            v_ref[...] += value
+    for copy in copies[3 * CHUNKS :]:
+        copy.wait()
+
+
+def key_value_kernel(core_ref, other_ref, k_part_ref, v_part_ref, wk_ref, wv_ref, col_ref, *outs):
+    k_ref, v_ref, message_ref = outs
+    rows, half = other_ref.shape
+    other = other_ref[...]
+    far = pl.ds(pl.multiple_of((1 - core_ref[0]) * half, half), half)
+    key = features(k_part_ref[...] + dot(other, wk_ref[far, :])).astype(BF16)
+    value = (v_part_ref[...] + dot(other, wv_ref[far, :])).astype(BF16)
     k_ref[...] = key
     v_ref[...] = value
     last = col_ref[rows - 1 : rows, :]
@@ -79,7 +122,7 @@
             intra_ref[here, cut] = dot(scores, value)
 
 
-def combine_kernel(bits, has_held, place_ref, first_ref, message_ref, *refs):
+def combine_kernel(bits, has_held, place_ref, col_ref, message_ref, *refs):
     got = refs[: len(bits)]
     held_in = refs[len(bits)] if has_held else None
     next_ref, held_ref = refs[-2:]
@@ -89,7 +132,7 @@
     top = own_id
     for i in ids:
         top = jnp.maximum(top, i)
-    first = first_ref[:1, :]
+    first = col_ref[:1, :]
     total = jnp.where(own_id == top, message_ref[:rows, :].astype(F32), 0.0)
     held = held_in[...] if has_held else jnp.zeros((rows, HEAD), F32)
     for b, g, i in zip(bits, got, ids):
@@ -102,22 +145,25 @@
     held_ref[...] = held
 
 
-def norm_kernel(bits, groups, core_ref, place_ref, first_ref, held_ref, *refs):
-    got = refs[: len(bits)]
-    queries = refs[len(bits) : len(bits) + groups]
-    intras = refs[len(bits) + groups : len(bits) + 2 * groups]
-    col_ref, gain_ref, weight_ref, normed_ref, theirs_ref = refs[len(bits) + 2 * groups :]
-    first = first_ref[:1, :]
+def incoming_of(bits, place_ref, col_ref, held_ref, got):
+    first = col_ref[:1, :]
     rows = held_ref.shape[0]
     held = held_ref[...]
     for b, g in zip(bits, got):
         earlier = (place_ref[0] & (1 << (b.bit_length() - 1))) != 0
         same = (g[rows : rows + 1, :].astype(F32) == first) & earlier
         held = held + jnp.where(same, g[:rows, :].astype(F32), 0.0)
-    incoming = held.astype(BF16)
+    return held.astype(BF16)
+
+
+def norm_kernel(bits, groups, core_ref, place_ref, held_ref, *refs):
+    got, refs = refs[: len(bits)], refs[len(bits) :]
+    queries, intras, refs = refs[:groups], refs[groups : 2 * groups], refs[2 * groups :]
+    col_ref, gain_ref, weight_ref, normed_ref, theirs_ref = refs
+    incoming = incoming_of(bits, place_ref, col_ref, held_ref, got)
     for start in range(0, col_ref.shape[0], BLOCK):
         here = slice(start, start + BLOCK)
-        joins = col_ref[here, :] == first
+        joins = col_ref[here, :] == col_ref[:1, :]
         for k in range(groups):
             width = queries[k].shape[1]
             for g in range(width // HEAD):
@@ -139,8 +185,18 @@
     out_ref[...] = dot(normed_ref[...], columns(weight_ref, core_ref[0]))
 
 
+def add_kernel(mine_ref, theirs_ref, out_ref):
+    size = out_ref.shape[0]
+    here = pl.ds(pl.multiple_of(pl.program_id(0) * size, size), size)
+    out_ref[...] = (mine_ref[here, :] + theirs_ref[here, :].astype(F32)).astype(BF16)
+
+
 def shape(dims, dtype):
     return jax.ShapeDtypeStruct(dims, dtype)
+
+
+def in_hbm(x):
+    return pltpu.with_memory_space_constraint(x, pltpu.HBM)
 
 
 def swap_head(x):
@@ -158,11 +214,24 @@
     core = lax.axis_index("head").astype(jnp.int32).reshape(1)
     place = lax.axis_index("seq").astype(jnp.int32).reshape(1)
     other = swap_head(tokens)
-    ids = doc_ids.astype(F32)
-    col = jnp.broadcast_to(ids[:, None], (rows, HEAD))
-    row = jnp.broadcast_to(ids[None, :], (8, rows))
-    first = jnp.broadcast_to(ids[:1, None], (8, HEAD))
-    gain = jnp.broadcast_to(norm_gain[None, :], (8, q_width))
+    gain = norm_gain.reshape(1, q_width)
+    own, wk, wv, k_part, v_part, col, row = pl.pallas_call(
+        own_half_kernel,
+        out_shape=(
+            shape(tokens.shape, BF16),
+            shape(key_matrix.shape, BF16),
+            shape(value_matrix.shape, BF16),
+            shape((rows, kv_width), F32),
+            shape((rows, kv_width), F32),
+            shape((rows, HEAD), F32),
+            shape((8, rows), F32),
+        ),
+        in_specs=[SMEM, VMEM, HBM, HBM, HBM],
+        out_specs=(VMEM,) * 7,
+        scratch_shapes=[pltpu.SemaphoreType.DMA((3 * CHUNKS + 2,))],
+        compiler_params=params(8),
+        name="own_half",
+    )(core, doc_ids.reshape(1, rows), *(in_hbm(x) for x in (tokens, key_matrix, value_matrix)))
 
     key, value, message = pl.pallas_call(
         key_value_kernel,
@@ -171,11 +240,11 @@
             shape((rows, kv_width), BF16),
             shape((state_rows + ID_ROWS, HEAD), BF16),
         ),
-        in_specs=[SMEM] + [VMEM] * 5,
+        in_specs=[SMEM] + [VMEM] * 6,
         out_specs=(VMEM, VMEM, VMEM),
-        compiler_params=params(24),
+        compiler_params=params(16),
         name="key_value",
-    )(core, tokens, other, key_matrix, value_matrix, col)
+    )(core, other, k_part, v_part, wk, wv, col)
 
     def intra(k, key, value):
         return pl.pallas_call(
@@ -195,18 +264,22 @@
             out_specs=(VMEM, VMEM),
             compiler_params=params(24),
             name=f"intra_{k}",
-        )(core, tokens, other, q_weight, key, value, col, row)
+        )(core, own, other, q_weight, key, value, col, row)
 
     held = None
     queries, intras = [], []
     for step, bits in enumerate(ROUNDS):
-        got = [lax.ppermute(message, "seq", [(i, i ^ b) for i in range(count)]) for b in bits]
+        final = step == len(ROUNDS) - 1
+        got = [
+            lax.ppermute(message, "seq", [(i, i ^ b) for i in range(count) if i < i ^ b or not final])
+            for b in bits
+        ]
         if step in INTRA_STEPS:
             (key, value), _ = lax.optimization_barrier(((key, value), message))
             query, part = intra(INTRA_STEPS.index(step), key, value)
             queries.append(query)
             intras.append(part)
-        if step == len(ROUNDS) - 1:
+        if final:
             break
         extra = () if held is None else (held,)
         message, held = pl.pallas_call(
@@ -216,28 +289,36 @@
             out_specs=(VMEM, VMEM),
             compiler_params=params(4),
             name="combine",
-        )(place, first, message, *got, *extra)
+        )(place, col, message, *got, *extra)
         if step in INTRA_STEPS:
             message, queries[-1] = lax.optimization_barrier((message, queries[-1]))
 
     normed, theirs = pl.pallas_call(
         lambda *refs: norm_kernel(ROUNDS[-1], kv_heads, *refs),
         out_shape=(shape((rows, q_width), BF16), shape((rows, half), BF16)),
-        in_specs=[SMEM, SMEM] + [VMEM] * (2 + len(got) + 2 * kv_heads + 3),
+        in_specs=[SMEM, SMEM] + [VMEM] * (1 + len(got) + 2 * kv_heads + 3),
         out_specs=(VMEM, VMEM),
-        compiler_params=params(32),
+        compiler_params=params(16),
         name="norm",
-    )(core, place, first, held, *got, *queries, *intras, col, gain, out_weight)
+    )(core, place, held, *got, *queries, *intras, col, gain, out_weight)
     received = swap_head(theirs)
     mine = pl.pallas_call(
         own_kernel,
         out_shape=shape((rows, half), F32),
         in_specs=[SMEM, VMEM, VMEM],
         out_specs=VMEM,
-        compiler_params=params(32),
+        compiler_params=params(16),
         name="own",
     )(core, normed, out_weight)
-    return (mine + received.astype(F32)).astype(BF16)
+    return pl.pallas_call(
+        add_kernel,
+        grid=(4,),
+        out_shape=shape((rows, half), BF16),
+        in_specs=[VMEM, VMEM],
+        out_specs=pl.BlockSpec((rows // 4, half), lambda i: (i, 0)),
+        compiler_params=params(8),
+        name="add",
+    )(mine, received)
 
 
 def solution(mesh):

time: 54 us -> 50.5 us (0.935)
  waiting for transfers between devices: 13.1 us -> 8.47 us
  local copies, waits for them, and re-layouts: 7.09 us -> 2.88 us
  starting transfers between devices: 20.8 us -> 25 us
  Pallas kernels: 10.6 us -> 13.8 us
  other arithmetic: 2.02 us -> 0 us
    ppermute x10, starting transfers between devices: 13.5 us -> 18.7 us  [on_device(): lax.ppermute(message, 'seq', [(i, i ^ b) for i in range(count) if i < i ^...]
    pallas_call x0 -> x2, Pallas kernels: none -> 3.61 us  [the longest x1 2.03 us: on_device(): pl.pallas_call(own_half_kernel, out_shape=(shape(tokens.shape, BF16), sha...]
    unnamed x14 -> x8, local copies, waits for them, and re-layouts: 5.88 us -> 2.88 us
    ppermute x10, waiting for transfers between devices: 10.3 us -> 7.45 us  [on_device(): lax.ppermute(message, 'seq', [(i, i ^ b) for i in range(count) if i < i ^...]
    convert_element_type x2 -> x0, other arithmetic: 2.02 us -> none  [the longest x1 1.33 us: on_device(): return (mine + received.astype(F32)).astype(BF16)]
    ppermute x2, waiting for transfers between devices: 2.84 us -> 1.03 us  [swap_head(): return lax.ppermute(x, 'head', [(0, 1), (1, 0)])]
    ppermute x2, starting transfers between devices: 7.35 us -> 6.38 us  [swap_head(): return lax.ppermute(x, 'head', [(0, 1), (1, 0)])]
    broadcast_in_dim x4 -> x0, local copies, waits for them, and re-layouts: 0.7 us -> none  [the longest x1 0.57 us: on_device(): first = jnp.broadcast_to(ids[:1, None], (8, HEAD))]
  transfers between devices with their start and end apart: 12 -> 12, of which waited for: 8 -> 5; matrix products, arithmetic and copies ran while one was open for 2% -> 0% of each run, Pallas kernels for 13% -> 18%
where the time goes in v3:
time: 50.5 us; the launch traced here: 50.3 us
  starting transfers between devices  25 us (50%)
  Pallas kernels  13.8 us (27%)
  waiting for transfers between devices  8.47 us (17%)
  local copies, waits for them, and re-layouts  2.88 us (6%)
    ppermute x10, starting transfers between devices, on_device(): lax.ppermute(message, 'seq', [(i, i ^ b) for i in range(count) if i < i ^...  18.7 us
    ppermute x10, waiting for transfers between devices, on_device(): lax.ppermute(message, 'seq', [(i, i ^ b) for i in range(count) if i < i ^...  7.45 us
    ppermute x2, starting transfers between devices, swap_head(): return lax.ppermute(x, 'head', [(0, 1), (1, 0)])  6.38 us
    pallas_call x2, Pallas kernels, intra(): pl.pallas_call(intra_kernel, out_shape=(shape((rows, group_width), BF16),...  5.54 us
    unnamed x8, local copies, waits for them, and re-layouts  2.88 us
    pallas_call x1, Pallas kernels, on_device(): pl.pallas_call(lambda *refs: norm_kernel(ROUNDS[-1], kv_heads, *refs), ou...  2.08 us
    pallas_call x1, Pallas kernels, on_device(): pl.pallas_call(own_half_kernel, out_shape=(shape(tokens.shape, BF16), sha...  2.03 us
    pallas_call x1, Pallas kernels, on_device(): pl.pallas_call(add_kernel, grid=(4,), out_shape=shape((rows, half), BF16)...  1.58 us
  transfers between devices with their start and end apart: 12, of which 5 were waited for; matrix products, arithmetic and copies ran while one was open for 0% of the time, Pallas kernels for 18%

profile of v3, /device:TPU:1, one launch (start us, length us, event | category | flops | bytes accessed | tf_op | source)
XLA Modules:
  0.0 50.3 jit_solution(13752144119701859339)
XLA Ops:
  0.0 3.2 %collective-permute-start = (bf16[512,1024]{1,0:T(8,128)(2,1)}, bf16[512,1024]{1,0:T(8,128)(2,1)S(1)}, u32[]{:S(2)}, u32[]{:S(2)}) collective-permute-start(bf16[512,1024]{1,0:T(8,128)(2,1)} %own_hbm.1), channel_id=1, source_target_pairs={{0,1},{1,0},{2,3},{3,2},{4,5},{5,4},{6,7},{7,6},{8,9},{9,8},{10,11... | collective-permute-start | bytes 3145736 | tf_op jit(solution)/shard_map/ppermute | solution.py:203
  3.2 0.7 %copy-done.3 = s32[512]{0:T(512)S(1)} copy-done((s32[512]{0:T(512)S(1)}, s32[512]{0:T(512)}, u32[]{:S(2)}) %copy-start.3) | copy-done | bytes 2072
  3.9 2.0 %own_half.1 = (bf16[512,1024]{1,0:T(8,128)(2,1)S(1)}, bf16[2048,256]{1,0:T(8,128)(2,1)S(1)}, bf16[2048,256]{1,0:T(8,128)(2,1)S(1)}, f32[512,256]{1,0:T(8,128)S(1...) custom-call(s32[1]{0:T(128)} %bitcast.core_ref.refs_0_, s32[1,512]{1,0:T(1,128)S(1)} %bitcast.5, ...), custom_call_target="tpu_custom_call" | custom-call | tf_op jit(solution)/shard_map/own_half/pallas_call | solution.py:218
  6.0 0.0 collective-permute-done.other_ref
  6.0 1.0 %key_value.1 = (bf16[512,256]{1,0:T(8,128)(2,1)S(1)}, bf16[512,256]{1,0:T(8,128)(2,1)S(1)}, bf16[272,128]{1,0:T(8,128)(2,1)S(1)}) custom-call(s32[1]{0:T(128)} %bitcast.core_ref.refs_0_, bf16[512,1024]{1,0:T(8,128)(2,1)S(1)} %collective-permute-done.other_ref, f32[512,256]{1,0:T(8,128)S(1)} %get-tuple-element.36.k_part_ref, ...), custom_call_target="tpu_custom_call" | custom-call | tf_op jit(solution)/shard_map/key_value/pallas_call | solution.py:236
  7.0 0.1 collective-permute-start.1
  7.1 3.6 %collective-permute-done.1.refs_3_ = bf16[272,128]{1,0:T(8,128)(2,1)S(1)} collective-permute-done((bf16[272,128]{1,0:T(8,128)(2,1)S(1)}, bf16[272,128]{1,0:T(8,128)(2,1)S(1)}, u32[]{:S(2)}, u32[]{:S(2)}) %collective-permute-start.1) | collective-permute-done | bytes 69664 | tf_op jit(solution)/shard_map/ppermute | solution.py:274
  10.8 5.3 %collective-permute-start.4 = (bf16[272,128]{1,0:T(8,128)(2,1)S(1)}, bf16[272,128]{1,0:T(8,128)(2,1)S(1)}, u32[]{:S(2)}, u32[]{:S(2)}) collective-permute-start(bf16[272,128]{1,0:T(8,128)(2,1)S(1)} %get-tuple-element.41.refs_2_), channel_id=1, source_target_pairs={{0,8},{2,10},{4,12},{6,14},{8,0},{10,2},{12,4},{14,6},{16,24},{18,... | collective-permute-start | bytes 208904 | tf_op jit(solution)/shard_map/ppermute | solution.py:274
  16.1 0.0 collective-permute-start.3
  16.1 1.2 %collective-permute-start.2 = (bf16[272,128]{1,0:T(8,128)(2,1)S(1)}, bf16[272,128]{1,0:T(8,128)(2,1)S(1)}, u32[]{:S(2)}, u32[]{:S(2)}) collective-permute-start(bf16[272,128]{1,0:T(8,128)(2,1)S(1)} %get-tuple-element.41.refs_2_), channel_id=1, source_target_pairs={{0,4},{2,6},{4,0},{6,2},{8,12},{10,14},{12,8},{14,10},{16,20},{18,... | collective-permute-start | bytes 208904 | tf_op jit(solution)/shard_map/ppermute | solution.py:274
  17.3 2.2 %copy-done = bf16[2048,1024]{1,0:T(8,128)(2,1)S(1)} copy-done((bf16[2048,1024]{1,0:T(8,128)(2,1)S(1)}, bf16[2048,1024]{1,0:T(8,128)(2,1)}, u32[]{:S(2)}) %copy-start) | copy-done | bytes 4194328
  19.4 2.8 %intra_0.1 = (bf16[512,512]{1,0:T(8,128)(2,1)S(1)}, f32[512,512]{1,0:T(8,128)S(1)}) custom-call(s32[1]{0:T(128)} %bitcast.core_ref.refs_0_, bf16[512,1024]{1,0:T(8,128)(2,1)S(1)} %get-tuple-element.44.own_ref, bf16[512,1024]{1,0:T(8,128)(2,1)S(1)} %collective-permute-done.other_ref, bf16[2048,1024]{1,0:T(8,128)(2,1)S(1)} %copy-done, ...), custom_call_target="tpu_custom_call" | custom-call | tf_op jit(solution)/shard_map/intra_0/pallas_call | solution.py:250
  22.2 0.0 collective-permute-done.4.refs_5_
  22.2 0.0 collective-permute-done.3.refs_4_
  22.2 1.7 %collective-permute-done.2.refs_3_ = bf16[272,128]{1,0:T(8,128)(2,1)S(1)} collective-permute-done((bf16[272,128]{1,0:T(8,128)(2,1)S(1)}, bf16[272,128]{1,0:T(8,128)(2,1)S(1)}, u32[]{:S(2)}, u32[]{:S(2)}) %collective-permute-start.2) | collective-permute-done | bytes 69664 | tf_op jit(solution)/shard_map/ppermute | solution.py:274
  24.0 0.1 combine.4
  24.1 2.8 %collective-permute-start.7 = (bf16[272,128]{1,0:T(8,128)(2,1)S(1)}, bf16[272,128]{1,0:T(8,128)(2,1)S(1)}, u32[]{:S(2)}, u32[]{:S(2)}) collective-permute-start(bf16[272,128]{1,0:T(8,128)(2,1)S(1)} %get-tuple-element.51.refs_2_), channel_id=1, source_target_pairs={{0,32},{2,34},{4,36},{6,38},{8,40},{10,42},{12,44},{14,46},{16,48}... | collective-permute-start | bytes 208904 | tf_op jit(solution)/shard_map/ppermute | solution.py:274
  26.9 0.9 %collective-permute-start.6 = (bf16[272,128]{1,0:T(8,128)(2,1)S(1)}, bf16[272,128]{1,0:T(8,128)(2,1)S(1)}, u32[]{:S(2)}, u32[]{:S(2)}) collective-permute-start(bf16[272,128]{1,0:T(8,128)(2,1)S(1)} %get-tuple-element.51.refs_2_), channel_id=1, source_target_pairs={{0,48},{2,50},{4,52},{6,54},{8,56},{10,58},{12,60},{14,62},{16,32}... | collective-permute-start | bytes 208904 | tf_op jit(solution)/shard_map/ppermute | solution.py:274
  27.8 2.8 %intra_1.1 = (bf16[512,512]{1,0:T(8,128)(2,1)S(1)}, f32[512,512]{1,0:T(8,128)S(1)}) custom-call(s32[1]{0:T(128)} %bitcast.core_ref.refs_0_, bf16[512,1024]{1,0:T(8,128)(2,1)S(1)} %get-tuple-element.44.own_ref, bf16[512,1024]{1,0:T(8,128)(2,1)S(1)} %collective-permute-done.other_ref, bf16[2048,1024]{1,0:T(8,128)(2,1)S(1)} %copy-done, ...), custom_call_target="tpu_custom_call" | custom-call | tf_op jit(solution)/shard_map/intra_1/pallas_call | solution.py:250
  30.6 0.0 collective-permute-done.7.refs_5_
  30.6 0.7 %collective-permute-done.6.refs_4_ = bf16[272,128]{1,0:T(8,128)(2,1)S(1)} collective-permute-done((bf16[272,128]{1,0:T(8,128)(2,1)S(1)}, bf16[272,128]{1,0:T(8,128)(2,1)S(1)}, u32[]{:S(2)}, u32[]{:S(2)}) %collective-permute-start.6) | collective-permute-done | bytes 69664 | tf_op jit(solution)/shard_map/ppermute | solution.py:274
  31.3 0.0 collective-permute-done.5.refs_3_
  31.3 0.1 combine.5
  31.4 4.8 %collective-permute-start.10 = (bf16[272,128]{1,0:T(8,128)(2,1)S(1)}, bf16[272,128]{1,0:T(8,128)(2,1)S(1)}, u32[]{:S(2)}, u32[]{:S(2)}) collective-permute-start(bf16[272,128]{1,0:T(8,128)(2,1)S(1)} %get-tuple-element.58), channel_id=1, source_target_pairs={{0,128},{2,130},{4,132},{6,134},{8,136},{10,138},{12,140},{14,142}... | collective-permute-start | bytes 208904 | tf_op jit(solution)/shard_map/ppermute | solution.py:274
  36.2 1.3 %collective-permute-start.9 = (bf16[272,128]{1,0:T(8,128)(2,1)S(1)}, bf16[272,128]{1,0:T(8,128)(2,1)S(1)}, u32[]{:S(2)}, u32[]{:S(2)}) collective-permute-start(bf16[272,128]{1,0:T(8,128)(2,1)S(1)} %get-tuple-element.58), channel_id=1, source_target_pairs={{0,192},{2,194},{4,196},{6,198},{8,200},{10,202},{12,204},{14,206}... | collective-permute-start | bytes 208904 | tf_op jit(solution)/shard_map/ppermute | solution.py:274
  37.5 2.3 %collective-permute-start.8 = (bf16[272,128]{1,0:T(8,128)(2,1)S(1)}, bf16[272,128]{1,0:T(8,128)(2,1)S(1)}, u32[]{:S(2)}, u32[]{:S(2)}) collective-permute-start(bf16[272,128]{1,0:T(8,128)(2,1)S(1)} %get-tuple-element.58), channel_id=1, source_target_pairs={{0,64},{2,66},{4,68},{6,70},{8,72},{10,74},{12,76},{14,78},{16,80}... | collective-permute-start | bytes 208904 | tf_op jit(solution)/shard_map/ppermute | solution.py:274
  39.9 1.3 %collective-permute-done.8.refs_3_ = bf16[272,128]{1,0:T(8,128)(2,1)S(1)} collective-permute-done((bf16[272,128]{1,0:T(8,128)(2,1)S(1)}, bf16[272,128]{1,0:T(8,128)(2,1)S(1)}, u32[]{:S(2)}, u32[]{:S(2)}) %collective-permute-start.8) | collective-permute-done | bytes 69664 | tf_op jit(solution)/shard_map/ppermute | solution.py:274
  41.2 2.1 %norm.1 = (bf16[512,1024]{1,0:T(8,128)(2,1)S(1)}, bf16[512,1024]{1,0:T(8,128)(2,1)S(1)}) custom-call(s32[1]{0:T(128)} %bitcast.core_ref.refs_0_, s32[1]{0:T(128)} %bitcast.1.refs_0_.refs_1_, f32[256,128]{1,0:T(8,128)S(1)} %get-tuple-element.53.refs_2_, bf16[272,128]{1,0:T(8,128)(2,1)S(1)} %collective-permute-done.8.refs_3_, ...), custom_call_target="tpu_custom_call" | custom-call | tf_op jit(solution)/shard_map/norm/pallas_call | solution.py:296
  43.3 3.1 %collective-permute-start.11 = (bf16[512,1024]{1,0:T(8,128)(2,1)S(1)}, bf16[512,1024]{1,0:T(8,128)(2,1)S(1)}, u32[]{:S(2)}, u32[]{:S(2)}) collective-permute-start(bf16[512,1024]{1,0:T(8,128)(2,1)S(1)} %get-tuple-element.64), channel_id=1, source_target_pairs={{0,1},{1,0},{2,3},{3,2},{4,5},{5,4},{6,7},{7,6},{8,9},{9,8},{10,11... | collective-permute-start | bytes 3145736 | tf_op jit(solution)/shard_map/ppermute | solution.py:203
  46.4 1.3 %own.1.mine_ref = f32[512,1024]{1,0:T(8,128)S(1)} custom-call(s32[1]{0:T(128)} %bitcast.core_ref.refs_0_, bf16[512,1024]{1,0:T(8,128)(2,1)S(1)} %get-tuple-element.63.normed_ref, bf16[1024,2048]{1,0:T(8,128)(2,1)S(1)} %copy-done.1), custom_call_target="tpu_custom_call" | custom-call | tf_op jit(solution)/shard_map/own/pallas_call | solution.py:305
  47.7 1.0 %collective-permute-done.11.theirs_ref = bf16[512,1024]{1,0:T(8,128)(2,1)S(1)} collective-permute-done((bf16[512,1024]{1,0:T(8,128)(2,1)S(1)}, bf16[512,1024]{1,0:T(8,128)(2,1)S(1)}, u32[]{:S(2)}, u32[]{:S(2)}) %collective-permute-start.11) | collective-permute-done | bytes 1048608 | tf_op jit(solution)/shard_map/ppermute | solution.py:203
  48.7 1.6 %add.1 = bf16[512,1024]{1,0:T(8,128)(2,1)} custom-call(f32[512,1024]{1,0:T(8,128)S(1)} %own.1.mine_ref, bf16[512,1024]{1,0:T(8,128)(2,1)S(1)} %collective-permute-done.11.theirs_ref), custom_call_target="tpu_custom_call" | custom-call | tf_op jit(solution)/shard_map/add/pallas_call | solution.py:313
  (10 shorter events, 0.1 us)
Async XLA Ops:
  0.0 6.0 %collective-permute-start = (bf16[512,1024]{1,0:T(8,128)(2,1)}, bf16[512,1024]{1,0:T(8,128)(2,1)S(1)}, u32[]{:S(2)}, u32[]{:S(2)}) collective-permute-start(bf16[512,1024]{1,0:T(8,128)(2,1)} %own_hbm.1), channel_id=1, source_target_pairs={{0,1},{1,0},{2,3},{3,2},{4,5},{5,4},{6,7},{7,6},{8,9},{9,8},{10,11... | collective-permute-start | bytes 3145736 | tf_op jit(solution)/shard_map/ppermute | solution.py:203
  3.2 0.7 %copy-start.3 = (s32[512]{0:T(512)S(1)}, s32[512]{0:T(512)}, u32[]{:S(2)}) copy-start(s32[512]{0:T(512)} %param.13) | copy-start | bytes 6148
  7.0 3.7 %collective-permute-start.1 = (bf16[272,128]{1,0:T(8,128)(2,1)S(1)}, bf16[272,128]{1,0:T(8,128)(2,1)S(1)}, u32[]{:S(2)}, u32[]{:S(2)}) collective-permute-start(bf16[272,128]{1,0:T(8,128)(2,1)S(1)} %get-tuple-element.40.refs_2_), channel_id=1, source_target_pairs={{0,2},{2,0},{4,6},{6,4},{8,10},{10,8},{12,14},{14,12},{16,18},{18,... | collective-permute-start | bytes 208904 | tf_op jit(solution)/shard_map/ppermute | solution.py:274
  10.8 11.4 %collective-permute-start.4 = (bf16[272,128]{1,0:T(8,128)(2,1)S(1)}, bf16[272,128]{1,0:T(8,128)(2,1)S(1)}, u32[]{:S(2)}, u32[]{:S(2)}) collective-permute-start(bf16[272,128]{1,0:T(8,128)(2,1)S(1)} %get-tuple-element.41.refs_2_), channel_id=1, source_target_pairs={{0,8},{2,10},{4,12},{6,14},{8,0},{10,2},{12,4},{14,6},{16,24},{18,... | collective-permute-start | bytes 208904 | tf_op jit(solution)/shard_map/ppermute | solution.py:274
  16.1 6.2 %collective-permute-start.3 = (bf16[272,128]{1,0:T(8,128)(2,1)S(1)}, bf16[272,128]{1,0:T(8,128)(2,1)S(1)}, u32[]{:S(2)}, u32[]{:S(2)}) collective-permute-start(bf16[272,128]{1,0:T(8,128)(2,1)S(1)} %get-tuple-element.41.refs_2_), channel_id=1, source_target_pairs={{0,12},{2,14},{4,8},{6,10},{8,4},{10,6},{12,0},{14,2},{16,28},{18,... | collective-permute-start | bytes 208904 | tf_op jit(solution)/shard_map/ppermute | solution.py:274
  16.1 7.9 %collective-permute-start.2 = (bf16[272,128]{1,0:T(8,128)(2,1)S(1)}, bf16[272,128]{1,0:T(8,128)(2,1)S(1)}, u32[]{:S(2)}, u32[]{:S(2)}) collective-permute-start(bf16[272,128]{1,0:T(8,128)(2,1)S(1)} %get-tuple-element.41.refs_2_), channel_id=1, source_target_pairs={{0,4},{2,6},{4,0},{6,2},{8,12},{10,14},{12,8},{14,10},{16,20},{18,... | collective-permute-start | bytes 208904 | tf_op jit(solution)/shard_map/ppermute | solution.py:274
  17.3 2.2 %copy-start = (bf16[2048,1024]{1,0:T(8,128)(2,1)S(1)}, bf16[2048,1024]{1,0:T(8,128)(2,1)}, u32[]{:S(2)}) copy-start(bf16[2048,1024]{1,0:T(8,128)(2,1)} %wq_ref.3) | copy-start | bytes 12582916
  24.0 17.2 %copy-start.1 = (bf16[1024,2048]{1,0:T(8,128)(2,1)S(1)}, bf16[1024,2048]{1,0:T(8,128)(2,1)}, u32[]{:S(2)}) copy-start(bf16[1024,2048]{1,0:T(8,128)(2,1)} %weight_ref.1) | copy-start | bytes 12582916
  24.0 17.2 %copy-start.2 = (f32[1024]{0:T(1024)S(1)}, f32[1024]{0:T(1024)}, u32[]{:S(2)}) copy-start(f32[1024]{0:T(1024)} %param.11) | copy-start | bytes 12292
  24.1 6.5 %collective-permute-start.7 = (bf16[272,128]{1,0:T(8,128)(2,1)S(1)}, bf16[272,128]{1,0:T(8,128)(2,1)S(1)}, u32[]{:S(2)}, u32[]{:S(2)}) collective-permute-start(bf16[272,128]{1,0:T(8,128)(2,1)S(1)} %get-tuple-element.51.refs_2_), channel_id=1, source_target_pairs={{0,32},{2,34},{4,36},{6,38},{8,40},{10,42},{12,44},{14,46},{16,48}... | collective-permute-start | bytes 208904 | tf_op jit(solution)/shard_map/ppermute | solution.py:274
  26.9 4.4 %collective-permute-start.6 = (bf16[272,128]{1,0:T(8,128)(2,1)S(1)}, bf16[272,128]{1,0:T(8,128)(2,1)S(1)}, u32[]{:S(2)}, u32[]{:S(2)}) collective-permute-start(bf16[272,128]{1,0:T(8,128)(2,1)S(1)} %get-tuple-element.51.refs_2_), channel_id=1, source_target_pairs={{0,48},{2,50},{4,52},{6,54},{8,56},{10,58},{12,60},{14,62},{16,32}... | collective-permute-start | bytes 208904 | tf_op jit(solution)/shard_map/ppermute | solution.py:274
  27.8 3.5 %collective-permute-start.5 = (bf16[272,128]{1,0:T(8,128)(2,1)S(1)}, bf16[272,128]{1,0:T(8,128)(2,1)S(1)}, u32[]{:S(2)}, u32[]{:S(2)}) collective-permute-start(bf16[272,128]{1,0:T(8,128)(2,1)S(1)} %get-tuple-element.51.refs_2_), channel_id=1, source_target_pairs={{0,16},{2,18},{4,20},{6,22},{8,24},{10,26},{12,28},{14,30},{16,0},... | collective-permute-start | bytes 208904 | tf_op jit(solution)/shard_map/ppermute | solution.py:274
  31.4 8.4 %collective-permute-start.10 = (bf16[272,128]{1,0:T(8,128)(2,1)S(1)}, bf16[272,128]{1,0:T(8,128)(2,1)S(1)}, u32[]{:S(2)}, u32[]{:S(2)}) collective-permute-start(bf16[272,128]{1,0:T(8,128)(2,1)S(1)} %get-tuple-element.58), channel_id=1, source_target_pairs={{0,128},{2,130},{4,132},{6,134},{8,136},{10,138},{12,140},{14,142}... | collective-permute-start | bytes 208904 | tf_op jit(solution)/shard_map/ppermute | solution.py:274
  36.2 3.6 %collective-permute-start.9 = (bf16[272,128]{1,0:T(8,128)(2,1)S(1)}, bf16[272,128]{1,0:T(8,128)(2,1)S(1)}, u32[]{:S(2)}, u32[]{:S(2)}) collective-permute-start(bf16[272,128]{1,0:T(8,128)(2,1)S(1)} %get-tuple-element.58), channel_id=1, source_target_pairs={{0,192},{2,194},{4,196},{6,198},{8,200},{10,202},{12,204},{14,206}... | collective-permute-start | bytes 208904 | tf_op jit(solution)/shard_map/ppermute | solution.py:274
  37.5 3.7 %collective-permute-start.8 = (bf16[272,128]{1,0:T(8,128)(2,1)S(1)}, bf16[272,128]{1,0:T(8,128)(2,1)S(1)}, u32[]{:S(2)}, u32[]{:S(2)}) collective-permute-start(bf16[272,128]{1,0:T(8,128)(2,1)S(1)} %get-tuple-element.58), channel_id=1, source_target_pairs={{0,64},{2,66},{4,68},{6,70},{8,72},{10,74},{12,76},{14,78},{16,80}... | collective-permute-start | bytes 208904 | tf_op jit(solution)/shard_map/ppermute | solution.py:274
  43.3 5.4 %collective-permute-start.11 = (bf16[512,1024]{1,0:T(8,128)(2,1)S(1)}, bf16[512,1024]{1,0:T(8,128)(2,1)S(1)}, u32[]{:S(2)}, u32[]{:S(2)}) collective-permute-start(bf16[512,1024]{1,0:T(8,128)(2,1)S(1)} %get-tuple-element.64), channel_id=1, source_target_pairs={{0,1},{1,0},{2,3},{3,2},{4,5},{5,4},{6,7},{7,6},{8,9},{9,8},{10,11... | collective-permute-start | bytes 3145736 | tf_op jit(solution)/shard_map/ppermute | solution.py:203

commit v4 on v3

--- a/solution.py
+++ b/solution.py
@@ -11,6 +11,8 @@
 ROUNDS = ((1,), (2, 6, 4), (8, 24, 16), (32, 96, 64))
 INTRA_STEPS = (1, 2)
 CHUNKS = 2
+STAGE_COPIES = 4
+ADD_STEPS = 2
 EPSILON = 1e-05
 F32 = jnp.float32
 BF16 = jnp.bfloat16
@@ -41,8 +43,8 @@
     )
 
 
-def own_half_kernel(core_ref, ids_ref, own_hbm, wk_hbm, wv_hbm, *refs):
-    own_ref, wk_ref, wv_ref, k_ref, v_ref, col_ref, row_ref, sems = refs
+def own_half_kernel(core_ref, ids_hbm, own_hbm, wk_hbm, wv_hbm, *refs):
+    own_ref, wk_ref, wv_ref, k_ref, v_ref, col_ref, row_ref, ids_vmem, sems = refs
     half = own_hbm.shape[1]
     chunk = half // CHUNKS
     near = core_ref[0] * half
@@ -56,14 +58,16 @@
     cut = pl.ds(far, half)
     copies.append((wk_hbm.at[cut, :], wk_ref.at[cut, :]))
     copies.append((wv_hbm.at[cut, :], wv_ref.at[cut, :]))
+    copies.insert(0, (ids_hbm, ids_vmem))
     copies = [pltpu.make_async_copy(a, b, sems.at[i]) for i, (a, b) in enumerate(copies)]
     for copy in copies:
         copy.start()
-    ids = ids_ref[...].astype(F32)
+    copies[0].wait()
+    ids = ids_vmem[...].astype(F32)
     row_ref[...] = jnp.broadcast_to(ids, row_ref.shape)
     col_ref[...] = jnp.broadcast_to(ids, (HEAD, ids.shape[1])).T
     for c in range(CHUNKS):
-        for copy in copies[3 * c : 3 * c + 3]:
+        for copy in copies[3 * c + 1 : 3 * c + 4]:
             copy.wait()
         own = own_ref[:, c * chunk : (c + 1) * chunk]
         cut = pl.ds(pl.multiple_of(near + c * chunk, chunk), chunk)
@@ -75,7 +79,7 @@
         else:
             k_ref[...] += key
             v_ref[...] += value
-    for copy in copies[3 * CHUNKS :]:
+    for copy in copies[3 * CHUNKS + 1 :]:
         copy.wait()
 
 
@@ -99,6 +103,18 @@
         )
         message_ref[cut, :] = state.astype(BF16)
     message_ref[heads * HEAD :, :] = jnp.broadcast_to(last, (ID_ROWS, HEAD)).astype(BF16)
+
+
+def stage_kernel(after_ref, weight_hbm, weight_ref, sems):
+    size = weight_ref.shape[0] // STAGE_COPIES
+    copies = []
+    for i in range(STAGE_COPIES):
+        cut = slice(i * size, (i + 1) * size)
+        copies.append(pltpu.make_async_copy(weight_hbm.at[cut, :], weight_ref.at[cut, :], sems.at[i]))
+    for copy in copies:
+        copy.start()
+    for copy in copies:
+        copy.wait()
 
 
 def intra_kernel(core_ref, own_ref, other_ref, wq_ref, k_ref, v_ref, col_ref, row_ref, q_ref, intra_ref):
@@ -159,7 +175,7 @@
 def norm_kernel(bits, groups, core_ref, place_ref, held_ref, *refs):
     got, refs = refs[: len(bits)], refs[len(bits) :]
     queries, intras, refs = refs[:groups], refs[groups : 2 * groups], refs[2 * groups :]
-    col_ref, gain_ref, weight_ref, normed_ref, theirs_ref = refs
+    col_ref, gain_ref, weight_ref, normed_ref, *theirs = refs
     incoming = incoming_of(bits, place_ref, col_ref, held_ref, got)
     for start in range(0, col_ref.shape[0], BLOCK):
         here = slice(start, start + BLOCK)
@@ -173,7 +189,7 @@
                 combined = intras[k][here, cut] + jnp.where(joins, carried, 0.0)
                 scale = lax.rsqrt(jnp.mean(combined * combined, axis=-1, keepdims=True) + EPSILON)
                 normed_ref[here, out] = (combined * scale * gain_ref[:1, out]).astype(BF16)
-        theirs_ref[here, :] = dot(normed_ref[here, :], columns(weight_ref, 1 - core_ref[0])).astype(BF16)
+        theirs[start // BLOCK][...] = dot(normed_ref[here, :], columns(weight_ref, 1 - core_ref[0])).astype(BF16)
 
 
 def columns(weight_ref, part):
@@ -185,10 +201,13 @@
     out_ref[...] = dot(normed_ref[...], columns(weight_ref, core_ref[0]))
 
 
-def add_kernel(mine_ref, theirs_ref, out_ref):
+def add_kernel(mine_ref, theirs_ref, *refs):
+    out_ref = refs[-1]
     size = out_ref.shape[0]
-    here = pl.ds(pl.multiple_of(pl.program_id(0) * size, size), size)
-    out_ref[...] = (mine_ref[here, :] + theirs_ref[here, :].astype(F32)).astype(BF16)
+    step = pl.program_id(0)
+    first = pl.multiple_of((step + (pl.num_programs(0) if len(refs) > 1 else 0)) * size, size)
+    here = pl.ds(pl.multiple_of(step * size, size), size)
+    out_ref[...] = (mine_ref[pl.ds(first, size), :] + theirs_ref[here, :].astype(F32)).astype(BF16)
 
 
 def shape(dims, dtype):
@@ -226,12 +245,12 @@
             shape((rows, HEAD), F32),
             shape((8, rows), F32),
         ),
-        in_specs=[SMEM, VMEM, HBM, HBM, HBM],
+        in_specs=[SMEM, HBM, HBM, HBM, HBM],
         out_specs=(VMEM,) * 7,
-        scratch_shapes=[pltpu.SemaphoreType.DMA((3 * CHUNKS + 2,))],
+        scratch_shapes=[pltpu.VMEM((1, rows), jnp.int32), pltpu.SemaphoreType.DMA((3 * CHUNKS + 3,))],
         compiler_params=params(8),
         name="own_half",
-    )(core, doc_ids.reshape(1, rows), *(in_hbm(x) for x in (tokens, key_matrix, value_matrix)))
+    )(core, *(in_hbm(x) for x in (doc_ids.reshape(1, rows), tokens, key_matrix, value_matrix)))
 
     key, value, message = pl.pallas_call(
         key_value_kernel,
@@ -264,16 +283,23 @@
             out_specs=(VMEM, VMEM),
             compiler_params=params(24),
             name=f"intra_{k}",
-        )(core, own, other, q_weight, key, value, col, row)
+        )(core, own, other, wq, key, value, col, row)
 
     held = None
     queries, intras = [], []
     for step, bits in enumerate(ROUNDS):
         final = step == len(ROUNDS) - 1
-        got = [
-            lax.ppermute(message, "seq", [(i, i ^ b) for i in range(count) if i < i ^ b or not final])
-            for b in bits
-        ]
+        got = [lax.ppermute(message, "seq", [(i, i ^ b) for i in range(count)]) for b in bits]
+        if step == 0:
+            wq = pl.pallas_call(
+                stage_kernel,
+                out_shape=shape(q_weight.shape, BF16),
+                in_specs=[VMEM, HBM],
+                out_specs=VMEM,
+                scratch_shapes=[pltpu.SemaphoreType.DMA((STAGE_COPIES,))],
+                compiler_params=params(2),
+                name="stage",
+            )(message, in_hbm(q_weight))
         if step in INTRA_STEPS:
             (key, value), _ = lax.optimization_barrier(((key, value), message))
             query, part = intra(INTRA_STEPS.index(step), key, value)
@@ -290,18 +316,20 @@
             compiler_params=params(4),
             name="combine",
         )(place, col, message, *got, *extra)
+        if step == 0:
+            message, wq = lax.optimization_barrier((message, wq))
         if step in INTRA_STEPS:
             message, queries[-1] = lax.optimization_barrier((message, queries[-1]))
 
-    normed, theirs = pl.pallas_call(
+    normed, *theirs = pl.pallas_call(
         lambda *refs: norm_kernel(ROUNDS[-1], kv_heads, *refs),
-        out_shape=(shape((rows, q_width), BF16), shape((rows, half), BF16)),
+        out_shape=(shape((rows, q_width), BF16),) + (shape((BLOCK, half), BF16),) * (rows // BLOCK),
         in_specs=[SMEM, SMEM] + [VMEM] * (1 + len(got) + 2 * kv_heads + 3),
-        out_specs=(VMEM, VMEM),
+        out_specs=(VMEM,) * (1 + rows // BLOCK),
         compiler_params=params(16),
         name="norm",
     )(core, place, held, *got, *queries, *intras, col, gain, out_weight)
-    received = swap_head(theirs)
+    received = [swap_head(part) for part in theirs]
     mine = pl.pallas_call(
         own_kernel,
         out_shape=shape((rows, half), F32),
@@ -310,15 +338,23 @@
         compiler_params=params(16),
         name="own",
     )(core, normed, out_weight)
-    return pl.pallas_call(
-        add_kernel,
-        grid=(4,),
-        out_shape=shape((rows, half), BF16),
-        in_specs=[VMEM, VMEM],
-        out_specs=pl.BlockSpec((rows // 4, half), lambda i: (i, 0)),
-        compiler_params=params(8),
-        name="add",
-    )(mine, received)
+    out = ()
+    for part in range(rows // BLOCK):
+        out = (
+            pl.pallas_call(
+                add_kernel,
+                grid=(ADD_STEPS,),
+                out_shape=shape((rows, half), BF16),
+                in_specs=[VMEM, VMEM] + [HBM] * len(out),
+                out_specs=pl.BlockSpec(
+                    (BLOCK // ADD_STEPS, half), lambda i, part=part: (i + part * ADD_STEPS, 0)
+                ),
+                input_output_aliases={2: 0} if out else {},
+                compiler_params=params(8),
+                name=f"add_{part}",
+            )(mine, received[part], *out),
+        )
+    return out[0]
 
 
 def solution(mesh):

time: 50.5 us -> 46.9 us (0.929)
  starting transfers between devices: 25 us -> 20.3 us
  local copies, waits for them, and re-layouts: 2.88 us -> 0.01 us
  Pallas kernels: 13.8 us -> 16.1 us
  waiting for transfers between devices: 8.47 us -> 10.3 us
    ppermute x10, starting transfers between devices: 18.7 us -> 14 us  [on_device(): lax.ppermute(message, 'seq', [(i, i ^ b) for i in range(count)])]
    unnamed x8 -> x4, local copies, waits for them, and re-layouts: 2.88 us -> 0.01 us
    pallas_call x1 -> x3, Pallas kernels: 1.58 us -> 3.9 us  [the longest x1 2.21 us: on_device(): pl.pallas_call(stage_kernel, out_shape=shape(q_weight.shape, BF16), in_sp...]
    ppermute x10, waiting for transfers between devices: 7.45 us -> 9.67 us  [on_device(): lax.ppermute(message, 'seq', [(i, i ^ b) for i in range(count)])]
    ppermute x2 -> x3, waiting for transfers between devices: 1.03 us -> 0.61 us  [swap_head(): return lax.ppermute(x, 'head', [(0, 1), (1, 0)])]
    ppermute x2 -> x3, starting transfers between devices: 6.38 us -> 6.3 us  [swap_head(): return lax.ppermute(x, 'head', [(0, 1), (1, 0)])]
  transfers between devices with their start and end apart: 12 -> 13, of which waited for: 5 -> 8; matrix products, arithmetic and copies ran while one was open for 0% -> 0% of each run, Pallas kernels for 18% -> 25%
where the time goes in v4:
time: 46.9 us; the launch traced here: 46.8 us
  starting transfers between devices  20.3 us (43%)
  Pallas kernels  16.1 us (34%)
  waiting for transfers between devices  10.3 us (22%)
    ppermute x10, starting transfers between devices, on_device(): lax.ppermute(message, 'seq', [(i, i ^ b) for i in range(count)])  14 us
    ppermute x10, waiting for transfers between devices, on_device(): lax.ppermute(message, 'seq', [(i, i ^ b) for i in range(count)])  9.67 us
    ppermute x3, starting transfers between devices, swap_head(): return lax.ppermute(x, 'head', [(0, 1), (1, 0)])  6.3 us
    pallas_call x2, Pallas kernels, intra(): pl.pallas_call(intra_kernel, out_shape=(shape((rows, group_width), BF16),...  5.52 us
    pallas_call x1, Pallas kernels, on_device(): pl.pallas_call(stage_kernel, out_shape=shape(q_weight.shape, BF16), in_sp...  2.21 us
    pallas_call x1, Pallas kernels, on_device(): pl.pallas_call(lambda *refs: norm_kernel(ROUNDS[-1], kv_heads, *refs), ou...  2.07 us
    pallas_call x1, Pallas kernels, on_device(): pl.pallas_call(own_half_kernel, out_shape=(shape(tokens.shape, BF16), sha...  2.06 us
    pallas_call x2, Pallas kernels, on_device(): pl.pallas_call(add_kernel, grid=(ADD_STEPS,), out_shape=shape((rows, half...  1.69 us
  transfers between devices with their start and end apart: 13, of which 8 were waited for; matrix products, arithmetic and copies ran while one was open for 0% of the time, Pallas kernels for 25%

profile of v4, /device:TPU:1, one launch (start us, length us, event | category | flops | bytes accessed | tf_op | source)
XLA Modules:
  0.0 46.8 jit_solution(2198800048482781314)
XLA Ops:
  0.0 3.2 %collective-permute-start = (bf16[512,1024]{1,0:T(8,128)(2,1)}, bf16[512,1024]{1,0:T(8,128)(2,1)S(1)}, u32[]{:S(2)}, u32[]{:S(2)}) collective-permute-start(bf16[512,1024]{1,0:T(8,128)(2,1)} %own_hbm.1), channel_id=1, source_target_pairs={{0,1},{1,0},{2,3},{3,2},{4,5},{5,4},{6,7},{7,6},{8,9},{9,8},{10,11... | collective-permute-start | bytes 3145736 | tf_op jit(solution)/shard_map/ppermute | solution.py:222
  3.2 2.1 %own_half.1 = (bf16[512,1024]{1,0:T(8,128)(2,1)S(1)}, bf16[2048,256]{1,0:T(8,128)(2,1)S(1)}, bf16[2048,256]{1,0:T(8,128)(2,1)S(1)}, f32[512,256]{1,0:T(8,128)S(1...) custom-call(s32[1]{0:T(128)} %bitcast.core_ref.refs_0_, s32[1,512]{1,0:T(1,128)} %bitcast.5, ...), custom_call_target="tpu_custom_call" | custom-call | tf_op jit(solution)/shard_map/own_half/pallas_call | solution.py:237
  5.3 0.4 collective-permute-done.other_ref
  5.7 1.0 %key_value.1 = (bf16[512,256]{1,0:T(8,128)(2,1)S(1)}, bf16[512,256]{1,0:T(8,128)(2,1)S(1)}, bf16[272,128]{1,0:T(8,128)(2,1)S(1)}) custom-call(s32[1]{0:T(128)} %bitcast.core_ref.refs_0_, bf16[512,1024]{1,0:T(8,128)(2,1)S(1)} %collective-permute-done.other_ref, f32[512,256]{1,0:T(8,128)S(1)} %get-tuple-element.39.k_part_ref, ...), custom_call_target="tpu_custom_call" | custom-call | tf_op jit(solution)/shard_map/key_value/pallas_call | solution.py:255
  6.8 0.1 collective-permute-start.1
  6.9 2.2 %stage.1.wq_ref = bf16[2048,1024]{1,0:T(8,128)(2,1)S(1)} custom-call(bf16[272,128]{1,0:T(8,128)(2,1)S(1)} %get-tuple-element.43.refs_2_.after_ref, bf16[2048,1024]{1,0:T(8,128)(2,1)} %weight_hbm.1), custom_call_target="tpu_custom_call" | custom-call | tf_op jit(solution)/shard_map/stage/pallas_call | solution.py:294
  9.1 0.9 %collective-permute-done.1.refs_3_ = bf16[272,128]{1,0:T(8,128)(2,1)S(1)} collective-permute-done((bf16[272,128]{1,0:T(8,128)(2,1)S(1)}, bf16[272,128]{1,0:T(8,128)(2,1)S(1)}, u32[]{:S(2)}, u32[]{:S(2)}) %collective-permute-start.1) | collective-permute-done | bytes 69664 | tf_op jit(solution)/shard_map/ppermute | solution.py:292
  10.1 5.3 %collective-permute-start.4 = (bf16[272,128]{1,0:T(8,128)(2,1)S(1)}, bf16[272,128]{1,0:T(8,128)(2,1)S(1)}, u32[]{:S(2)}, u32[]{:S(2)}) collective-permute-start(bf16[272,128]{1,0:T(8,128)(2,1)S(1)} %get-tuple-element.45.refs_2_), channel_id=1, source_target_pairs={{0,8},{2,10},{4,12},{6,14},{8,0},{10,2},{12,4},{14,6},{16,24},{18,... | collective-permute-start | bytes 208904 | tf_op jit(solution)/shard_map/ppermute | solution.py:292
  15.3 0.1 collective-permute-start.3
  15.4 1.1 %collective-permute-start.2 = (bf16[272,128]{1,0:T(8,128)(2,1)S(1)}, bf16[272,128]{1,0:T(8,128)(2,1)S(1)}, u32[]{:S(2)}, u32[]{:S(2)}) collective-permute-start(bf16[272,128]{1,0:T(8,128)(2,1)S(1)} %get-tuple-element.45.refs_2_), channel_id=1, source_target_pairs={{0,4},{2,6},{4,0},{6,2},{8,12},{10,14},{12,8},{14,10},{16,20},{18,... | collective-permute-start | bytes 208904 | tf_op jit(solution)/shard_map/ppermute | solution.py:292
  16.5 2.8 %intra_0.1 = (bf16[512,512]{1,0:T(8,128)(2,1)S(1)}, f32[512,512]{1,0:T(8,128)S(1)}) custom-call(s32[1]{0:T(128)} %bitcast.core_ref.refs_0_, bf16[512,1024]{1,0:T(8,128)(2,1)S(1)} %get-tuple-element.48.own_ref, bf16[512,1024]{1,0:T(8,128)(2,1)S(1)} %collective-permute-done.other_ref, bf16[2048,1024]{1,0:T(8,128)(2,1)S(1)} %stage.1.wq_ref, ...), custom_call_target="tpu_custom_call" | custom-call | tf_op jit(solution)/shard_map/intra_0/pallas_call | solution.py:269
  19.3 1.4 %collective-permute-done.3.refs_4_ = bf16[272,128]{1,0:T(8,128)(2,1)S(1)} collective-permute-done((bf16[272,128]{1,0:T(8,128)(2,1)S(1)}, bf16[272,128]{1,0:T(8,128)(2,1)S(1)}, u32[]{:S(2)}, u32[]{:S(2)}) %collective-permute-start.3) | collective-permute-done | bytes 69664 | tf_op jit(solution)/shard_map/ppermute | solution.py:292
  20.7 2.3 %collective-permute-done.2.refs_3_ = bf16[272,128]{1,0:T(8,128)(2,1)S(1)} collective-permute-done((bf16[272,128]{1,0:T(8,128)(2,1)S(1)}, bf16[272,128]{1,0:T(8,128)(2,1)S(1)}, u32[]{:S(2)}, u32[]{:S(2)}) %collective-permute-start.2) | collective-permute-done | bytes 69664 | tf_op jit(solution)/shard_map/ppermute | solution.py:292
  23.0 0.1 combine.4
  23.1 2.8 %collective-permute-start.7 = (bf16[272,128]{1,0:T(8,128)(2,1)S(1)}, bf16[272,128]{1,0:T(8,128)(2,1)S(1)}, u32[]{:S(2)}, u32[]{:S(2)}) collective-permute-start(bf16[272,128]{1,0:T(8,128)(2,1)S(1)} %get-tuple-element.56.refs_2_), channel_id=1, source_target_pairs={{0,32},{2,34},{4,36},{6,38},{8,40},{10,42},{12,44},{14,46},{16,48}... | collective-permute-start | bytes 208904 | tf_op jit(solution)/shard_map/ppermute | solution.py:292
  25.9 0.8 %collective-permute-start.6 = (bf16[272,128]{1,0:T(8,128)(2,1)S(1)}, bf16[272,128]{1,0:T(8,128)(2,1)S(1)}, u32[]{:S(2)}, u32[]{:S(2)}) collective-permute-start(bf16[272,128]{1,0:T(8,128)(2,1)S(1)} %get-tuple-element.56.refs_2_), channel_id=1, source_target_pairs={{0,48},{2,50},{4,52},{6,54},{8,56},{10,58},{12,60},{14,62},{16,32}... | collective-permute-start | bytes 208904 | tf_op jit(solution)/shard_map/ppermute | solution.py:292
  26.8 2.8 %intra_1.1 = (bf16[512,512]{1,0:T(8,128)(2,1)S(1)}, f32[512,512]{1,0:T(8,128)S(1)}) custom-call(s32[1]{0:T(128)} %bitcast.core_ref.refs_0_, bf16[512,1024]{1,0:T(8,128)(2,1)S(1)} %get-tuple-element.48.own_ref, bf16[512,1024]{1,0:T(8,128)(2,1)S(1)} %collective-permute-done.other_ref, bf16[2048,1024]{1,0:T(8,128)(2,1)S(1)} %stage.1.wq_ref, ...), custom_call_target="tpu_custom_call" | custom-call | tf_op jit(solution)/shard_map/intra_1/pallas_call | solution.py:269
  29.5 0.0 collective-permute-done.7.refs_5_
  29.5 0.7 %collective-permute-done.6.refs_4_ = bf16[272,128]{1,0:T(8,128)(2,1)S(1)} collective-permute-done((bf16[272,128]{1,0:T(8,128)(2,1)S(1)}, bf16[272,128]{1,0:T(8,128)(2,1)S(1)}, u32[]{:S(2)}, u32[]{:S(2)}) %collective-permute-start.6) | collective-permute-done | bytes 69664 | tf_op jit(solution)/shard_map/ppermute | solution.py:292
  30.3 0.1 combine.5
  30.4 3.0 %collective-permute-start.10 = (bf16[272,128]{1,0:T(8,128)(2,1)S(1)}, bf16[272,128]{1,0:T(8,128)(2,1)S(1)}, u32[]{:S(2)}, u32[]{:S(2)}) collective-permute-start(bf16[272,128]{1,0:T(8,128)(2,1)S(1)} %get-tuple-element.63), channel_id=1, source_target_pairs={{0,128},{2,130},{4,132},{6,134},{8,136},{10,138},{12,140},{14,142}... | collective-permute-start | bytes 208904 | tf_op jit(solution)/shard_map/ppermute | solution.py:292
  33.4 0.8 %collective-permute-start.9 = (bf16[272,128]{1,0:T(8,128)(2,1)S(1)}, bf16[272,128]{1,0:T(8,128)(2,1)S(1)}, u32[]{:S(2)}, u32[]{:S(2)}) collective-permute-start(bf16[272,128]{1,0:T(8,128)(2,1)S(1)} %get-tuple-element.63), channel_id=1, source_target_pairs={{0,192},{2,194},{4,196},{6,198},{8,200},{10,202},{12,204},{14,206}... | collective-permute-start | bytes 208904 | tf_op jit(solution)/shard_map/ppermute | solution.py:292
  34.2 0.0 collective-permute-start.8
  34.2 1.0 %collective-permute-done.10.refs_5_ = bf16[272,128]{1,0:T(8,128)(2,1)S(1)} collective-permute-done((bf16[272,128]{1,0:T(8,128)(2,1)S(1)}, bf16[272,128]{1,0:T(8,128)(2,1)S(1)}, u32[]{:S(2)}, u32[]{:S(2)}) %collective-permute-start.10) | collective-permute-done | bytes 69664 | tf_op jit(solution)/shard_map/ppermute | solution.py:292
  35.1 3.4 %collective-permute-done.9.refs_4_ = bf16[272,128]{1,0:T(8,128)(2,1)S(1)} collective-permute-done((bf16[272,128]{1,0:T(8,128)(2,1)S(1)}, bf16[272,128]{1,0:T(8,128)(2,1)S(1)}, u32[]{:S(2)}, u32[]{:S(2)}) %collective-permute-start.9) | collective-permute-done | bytes 69664 | tf_op jit(solution)/shard_map/ppermute | solution.py:292
  38.5 2.1 %norm.1 = (bf16[512,1024]{1,0:T(8,128)(2,1)S(1)}, bf16[256,1024]{1,0:T(8,128)(2,1)S(1)}, bf16[256,1024]{1,0:T(8,128)(2,1)S(1)}) custom-call(s32[1]{0:T(128)} %bitcast.core_ref.refs_0_, s32[1]{0:T(128)} %bitcast.1.refs_0_.refs_1_, f32[256,128]{1,0:T(8,128)S(1)} %get-tuple-element.58.refs_2_, bf16[272,128]{1,0:T(8,128)(2,1)S(1)} %collective-permute-done.8.refs_3_, ...), custom_call_target="tpu_custom_call" | custom-call | tf_op jit(solution)/shard_map/norm/pallas_call | solution.py:324
  40.6 3.0 %collective-permute-start.12 = (bf16[256,1024]{1,0:T(8,128)(2,1)S(1)}, bf16[256,1024]{1,0:T(8,128)(2,1)S(1)}, u32[]{:S(2)}, u32[]{:S(2)}) collective-permute-start(bf16[256,1024]{1,0:T(8,128)(2,1)S(1)} %get-tuple-element.70), channel_id=1, source_target_pairs={{0,1},{1,0},{2,3},{3,2},{4,5},{5,4},{6,7},{7,6},{8,9},{9,8},{10,11... | collective-permute-start | bytes 1572872 | tf_op jit(solution)/shard_map/ppermute | solution.py:222
  43.5 0.1 collective-permute-start.11
  43.7 1.3 %own.1.mine_ref = f32[512,1024]{1,0:T(8,128)S(1)} custom-call(s32[1]{0:T(128)} %bitcast.core_ref.refs_0_, bf16[512,1024]{1,0:T(8,128)(2,1)S(1)} %get-tuple-element.68.normed_ref, bf16[1024,2048]{1,0:T(8,128)(2,1)S(1)} %copy-done), custom_call_target="tpu_custom_call" | custom-call | tf_op jit(solution)/shard_map/own/pallas_call | solution.py:333
  44.9 0.2 collective-permute-done.12.theirs_ref
  45.1 0.9 %add_0.1.refs_0_ = bf16[512,1024]{1,0:T(8,128)(2,1)} custom-call(f32[512,1024]{1,0:T(8,128)S(1)} %own.1.mine_ref, bf16[256,1024]{1,0:T(8,128)(2,1)S(1)} %collective-permute-done.12.theirs_ref), custom_call_target="tpu_custom_call" | custom-call | tf_op jit(solution)/shard_map/add_0/pallas_call | solution.py:344
  45.9 0.8 %add_1.1 = bf16[512,1024]{1,0:T(8,128)(2,1)} custom-call(f32[512,1024]{1,0:T(8,128)S(1)} %own.1.mine_ref, bf16[256,1024]{1,0:T(8,128)(2,1)S(1)} %collective-permute-done.11.theirs_ref, bf16[512,1024]{1,0:T(8,128)(2,1)} %add_0.1.refs_0_), custom_call_target="tpu_custom_call", output_to_operand_aliasing={{}: (2, {})} | custom-call | tf_op jit(solution)/shard_map/add_1/pallas_call | solution.py:344
  (10 shorter events, 0.1 us)
Async XLA Ops:
  0.0 5.7 %collective-permute-start = (bf16[512,1024]{1,0:T(8,128)(2,1)}, bf16[512,1024]{1,0:T(8,128)(2,1)S(1)}, u32[]{:S(2)}, u32[]{:S(2)}) collective-permute-start(bf16[512,1024]{1,0:T(8,128)(2,1)} %own_hbm.1), channel_id=1, source_target_pairs={{0,1},{1,0},{2,3},{3,2},{4,5},{5,4},{6,7},{7,6},{8,9},{9,8},{10,11... | collective-permute-start | bytes 3145736 | tf_op jit(solution)/shard_map/ppermute | solution.py:222
  6.8 3.2 %collective-permute-start.1 = (bf16[272,128]{1,0:T(8,128)(2,1)S(1)}, bf16[272,128]{1,0:T(8,128)(2,1)S(1)}, u32[]{:S(2)}, u32[]{:S(2)}) collective-permute-start(bf16[272,128]{1,0:T(8,128)(2,1)S(1)} %get-tuple-element.43.refs_2_.after_ref), channel_id=1, source_target_pairs={{0,2},{2,0},{4,6},{6,4},{8,10},{10,8},{12,14},{14,12},{16,18},{18,... | collective-permute-start | bytes 208904 | tf_op jit(solution)/shard_map/ppermute | solution.py:292
  10.1 9.2 %collective-permute-start.4 = (bf16[272,128]{1,0:T(8,128)(2,1)S(1)}, bf16[272,128]{1,0:T(8,128)(2,1)S(1)}, u32[]{:S(2)}, u32[]{:S(2)}) collective-permute-start(bf16[272,128]{1,0:T(8,128)(2,1)S(1)} %get-tuple-element.45.refs_2_), channel_id=1, source_target_pairs={{0,8},{2,10},{4,12},{6,14},{8,0},{10,2},{12,4},{14,6},{16,24},{18,... | collective-permute-start | bytes 208904 | tf_op jit(solution)/shard_map/ppermute | solution.py:292
  15.3 5.4 %collective-permute-start.3 = (bf16[272,128]{1,0:T(8,128)(2,1)S(1)}, bf16[272,128]{1,0:T(8,128)(2,1)S(1)}, u32[]{:S(2)}, u32[]{:S(2)}) collective-permute-start(bf16[272,128]{1,0:T(8,128)(2,1)S(1)} %get-tuple-element.45.refs_2_), channel_id=1, source_target_pairs={{0,12},{2,14},{4,8},{6,10},{8,4},{10,6},{12,0},{14,2},{16,28},{18,... | collective-permute-start | bytes 208904 | tf_op jit(solution)/shard_map/ppermute | solution.py:292
  15.4 7.6 %collective-permute-start.2 = (bf16[272,128]{1,0:T(8,128)(2,1)S(1)}, bf16[272,128]{1,0:T(8,128)(2,1)S(1)}, u32[]{:S(2)}, u32[]{:S(2)}) collective-permute-start(bf16[272,128]{1,0:T(8,128)(2,1)S(1)} %get-tuple-element.45.refs_2_), channel_id=1, source_target_pairs={{0,4},{2,6},{4,0},{6,2},{8,12},{10,14},{12,8},{14,10},{16,20},{18,... | collective-permute-start | bytes 208904 | tf_op jit(solution)/shard_map/ppermute | solution.py:292
  23.0 15.5 %copy-start = (bf16[1024,2048]{1,0:T(8,128)(2,1)S(1)}, bf16[1024,2048]{1,0:T(8,128)(2,1)}, u32[]{:S(2)}) copy-start(bf16[1024,2048]{1,0:T(8,128)(2,1)} %weight_ref.1) | copy-start | bytes 12582916
  23.0 15.5 %copy-start.1 = (f32[1024]{0:T(1024)S(1)}, f32[1024]{0:T(1024)}, u32[]{:S(2)}) copy-start(f32[1024]{0:T(1024)} %param.11) | copy-start | bytes 12292
  23.1 6.5 %collective-permute-start.7 = (bf16[272,128]{1,0:T(8,128)(2,1)S(1)}, bf16[272,128]{1,0:T(8,128)(2,1)S(1)}, u32[]{:S(2)}, u32[]{:S(2)}) collective-permute-start(bf16[272,128]{1,0:T(8,128)(2,1)S(1)} %get-tuple-element.56.refs_2_), channel_id=1, source_target_pairs={{0,32},{2,34},{4,36},{6,38},{8,40},{10,42},{12,44},{14,46},{16,48}... | collective-permute-start | bytes 208904 | tf_op jit(solution)/shard_map/ppermute | solution.py:292
  25.9 4.4 %collective-permute-start.6 = (bf16[272,128]{1,0:T(8,128)(2,1)S(1)}, bf16[272,128]{1,0:T(8,128)(2,1)S(1)}, u32[]{:S(2)}, u32[]{:S(2)}) collective-permute-start(bf16[272,128]{1,0:T(8,128)(2,1)S(1)} %get-tuple-element.56.refs_2_), channel_id=1, source_target_pairs={{0,48},{2,50},{4,52},{6,54},{8,56},{10,58},{12,60},{14,62},{16,32}... | collective-permute-start | bytes 208904 | tf_op jit(solution)/shard_map/ppermute | solution.py:292
  26.8 3.5 %collective-permute-start.5 = (bf16[272,128]{1,0:T(8,128)(2,1)S(1)}, bf16[272,128]{1,0:T(8,128)(2,1)S(1)}, u32[]{:S(2)}, u32[]{:S(2)}) collective-permute-start(bf16[272,128]{1,0:T(8,128)(2,1)S(1)} %get-tuple-element.56.refs_2_), channel_id=1, source_target_pairs={{0,16},{2,18},{4,20},{6,22},{8,24},{10,26},{12,28},{14,30},{16,0},... | collective-permute-start | bytes 208904 | tf_op jit(solution)/shard_map/ppermute | solution.py:292
  30.4 4.8 %collective-permute-start.10 = (bf16[272,128]{1,0:T(8,128)(2,1)S(1)}, bf16[272,128]{1,0:T(8,128)(2,1)S(1)}, u32[]{:S(2)}, u32[]{:S(2)}) collective-permute-start(bf16[272,128]{1,0:T(8,128)(2,1)S(1)} %get-tuple-element.63), channel_id=1, source_target_pairs={{0,128},{2,130},{4,132},{6,134},{8,136},{10,138},{12,140},{14,142}... | collective-permute-start | bytes 208904 | tf_op jit(solution)/shard_map/ppermute | solution.py:292
  33.4 5.1 %collective-permute-start.9 = (bf16[272,128]{1,0:T(8,128)(2,1)S(1)}, bf16[272,128]{1,0:T(8,128)(2,1)S(1)}, u32[]{:S(2)}, u32[]{:S(2)}) collective-permute-start(bf16[272,128]{1,0:T(8,128)(2,1)S(1)} %get-tuple-element.63), channel_id=1, source_target_pairs={{0,192},{2,194},{4,196},{6,198},{8,200},{10,202},{12,204},{14,206}... | collective-permute-start | bytes 208904 | tf_op jit(solution)/shard_map/ppermute | solution.py:292
  34.2 4.3 %collective-permute-start.8 = (bf16[272,128]{1,0:T(8,128)(2,1)S(1)}, bf16[272,128]{1,0:T(8,128)(2,1)S(1)}, u32[]{:S(2)}, u32[]{:S(2)}) collective-permute-start(bf16[272,128]{1,0:T(8,128)(2,1)S(1)} %get-tuple-element.63), channel_id=1, source_target_pairs={{0,64},{2,66},{4,68},{6,70},{8,72},{10,74},{12,76},{14,78},{16,80}... | collective-permute-start | bytes 208904 | tf_op jit(solution)/shard_map/ppermute | solution.py:292
  40.6 4.5 %collective-permute-start.12 = (bf16[256,1024]{1,0:T(8,128)(2,1)S(1)}, bf16[256,1024]{1,0:T(8,128)(2,1)S(1)}, u32[]{:S(2)}, u32[]{:S(2)}) collective-permute-start(bf16[256,1024]{1,0:T(8,128)(2,1)S(1)} %get-tuple-element.70), channel_id=1, source_target_pairs={{0,1},{1,0},{2,3},{3,2},{4,5},{5,4},{6,7},{7,6},{8,9},{9,8},{10,11... | collective-permute-start | bytes 1572872 | tf_op jit(solution)/shard_map/ppermute | solution.py:222
  43.5 2.4 %collective-permute-start.11 = (bf16[256,1024]{1,0:T(8,128)(2,1)S(1)}, bf16[256,1024]{1,0:T(8,128)(2,1)S(1)}, u32[]{:S(2)}, u32[]{:S(2)}) collective-permute-start(bf16[256,1024]{1,0:T(8,128)(2,1)S(1)} %get-tuple-element.69), channel_id=1, source_target_pairs={{0,1},{1,0},{2,3},{3,2},{4,5},{5,4},{6,7},{7,6},{8,9},{9,8},{10,11... | collective-permute-start | bytes 1572872 | tf_op jit(solution)/shard_map/ppermute | solution.py:222

commit v5 on v4

--- a/solution.py
+++ b/solution.py
@@ -8,7 +8,7 @@
 HEAD = 128
 ID_ROWS = 16
 BLOCK = 256
-ROUNDS = ((1,), (2, 6, 4), (8, 24, 16), (32, 96, 64))
+ROUNDS = ((1,), (2, 6, 5), (8, 24, 16), (32, 96, 64))
 INTRA_STEPS = (1, 2)
 CHUNKS = 2
 STAGE_COPIES = 4

time: 46.9 us -> 46.7 us (level)
  transfers between devices with their start and end apart: 13 -> 13, of which waited for: 8 -> 9; matrix products, arithmetic and copies ran while one was open for 0% -> 0% of each run, Pallas kernels for 25% -> 25%
where the time goes in v5:
time: 46.7 us
  starting transfers between devices  20.3 us (43%)
  Pallas kernels  16.1 us (34%)
  waiting for transfers between devices  10.2 us (22%)
    ppermute x10, starting transfers between devices, on_device(): lax.ppermute(message, 'seq', [(i, i ^ b) for i in range(count)])  13.6 us
    ppermute x10, waiting for transfers between devices, on_device(): lax.ppermute(message, 'seq', [(i, i ^ b) for i in range(count)])  9.56 us
    ppermute x3, starting transfers between devices, swap_head(): return lax.ppermute(x, 'head', [(0, 1), (1, 0)])  6.7 us
    pallas_call x2, Pallas kernels, intra(): pl.pallas_call(intra_kernel, out_shape=(shape((rows, group_width), BF16),...  5.52 us
    pallas_call x1, Pallas kernels, on_device(): pl.pallas_call(stage_kernel, out_shape=shape(q_weight.shape, BF16), in_sp...  2.21 us
    pallas_call x1, Pallas kernels, on_device(): pl.pallas_call(lambda *refs: norm_kernel(ROUNDS[-1], kv_heads, *refs), ou...  2.08 us
    pallas_call x1, Pallas kernels, on_device(): pl.pallas_call(own_half_kernel, out_shape=(shape(tokens.shape, BF16), sha...  2.06 us
    pallas_call x2, Pallas kernels, on_device(): pl.pallas_call(add_kernel, grid=(ADD_STEPS,), out_shape=shape((rows, half...  1.69 us
  transfers between devices with their start and end apart: 13, of which 9 were waited for; matrix products, arithmetic and copies ran while one was open for 0% of the time, Pallas kernels for 25%

profile of v5, /device:TPU:1, one launch (start us, length us, event | category | flops | bytes accessed | tf_op | source)
XLA Modules:
  0.0 46.7 jit_solution(18351536342435277979)
XLA Ops:
  0.0 3.2 %collective-permute-start = (bf16[512,1024]{1,0:T(8,128)(2,1)}, bf16[512,1024]{1,0:T(8,128)(2,1)S(1)}, u32[]{:S(2)}, u32[]{:S(2)}) collective-permute-start(bf16[512,1024]{1,0:T(8,128)(2,1)} %own_hbm.1), channel_id=1, source_target_pairs={{0,1},{1,0},{2,3},{3,2},{4,5},{5,4},{6,7},{7,6},{8,9},{9,8},{10,11... | collective-permute-start | bytes 3145736 | tf_op jit(solution)/shard_map/ppermute | solution.py:222
  3.2 2.1 %own_half.1 = (bf16[512,1024]{1,0:T(8,128)(2,1)S(1)}, bf16[2048,256]{1,0:T(8,128)(2,1)S(1)}, bf16[2048,256]{1,0:T(8,128)(2,1)S(1)}, f32[512,256]{1,0:T(8,128)S(1...) custom-call(s32[1]{0:T(128)} %bitcast.core_ref.refs_0_, s32[1,512]{1,0:T(1,128)} %bitcast.5, ...), custom_call_target="tpu_custom_call" | custom-call | tf_op jit(solution)/shard_map/own_half/pallas_call | solution.py:237
  5.3 0.4 collective-permute-done.other_ref
  5.7 1.0 %key_value.1 = (bf16[512,256]{1,0:T(8,128)(2,1)S(1)}, bf16[512,256]{1,0:T(8,128)(2,1)S(1)}, bf16[272,128]{1,0:T(8,128)(2,1)S(1)}) custom-call(s32[1]{0:T(128)} %bitcast.core_ref.refs_0_, bf16[512,1024]{1,0:T(8,128)(2,1)S(1)} %collective-permute-done.other_ref, f32[512,256]{1,0:T(8,128)S(1)} %get-tuple-element.39.k_part_ref, ...), custom_call_target="tpu_custom_call" | custom-call | tf_op jit(solution)/shard_map/key_value/pallas_call | solution.py:255
  6.8 0.1 collective-permute-start.1
  6.9 2.2 %stage.1.wq_ref = bf16[2048,1024]{1,0:T(8,128)(2,1)S(1)} custom-call(bf16[272,128]{1,0:T(8,128)(2,1)S(1)} %get-tuple-element.43.refs_2_.after_ref, bf16[2048,1024]{1,0:T(8,128)(2,1)} %weight_hbm.1), custom_call_target="tpu_custom_call" | custom-call | tf_op jit(solution)/shard_map/stage/pallas_call | solution.py:294
  9.1 0.9 %collective-permute-done.1.refs_3_ = bf16[272,128]{1,0:T(8,128)(2,1)S(1)} collective-permute-done((bf16[272,128]{1,0:T(8,128)(2,1)S(1)}, bf16[272,128]{1,0:T(8,128)(2,1)S(1)}, u32[]{:S(2)}, u32[]{:S(2)}) %collective-permute-start.1) | collective-permute-done | bytes 69664 | tf_op jit(solution)/shard_map/ppermute | solution.py:292
  10.1 4.8 %collective-permute-start.4 = (bf16[272,128]{1,0:T(8,128)(2,1)S(1)}, bf16[272,128]{1,0:T(8,128)(2,1)S(1)}, u32[]{:S(2)}, u32[]{:S(2)}) collective-permute-start(bf16[272,128]{1,0:T(8,128)(2,1)S(1)} %get-tuple-element.45.refs_2_), channel_id=1, source_target_pairs={{0,10},{2,8},{4,14},{6,12},{8,2},{10,0},{12,6},{14,4},{16,26},{18,... | collective-permute-start | bytes 208904 | tf_op jit(solution)/shard_map/ppermute | solution.py:292
  14.9 0.3 collective-permute-start.3
  15.2 0.9 %collective-permute-start.2 = (bf16[272,128]{1,0:T(8,128)(2,1)S(1)}, bf16[272,128]{1,0:T(8,128)(2,1)S(1)}, u32[]{:S(2)}, u32[]{:S(2)}) collective-permute-start(bf16[272,128]{1,0:T(8,128)(2,1)S(1)} %get-tuple-element.45.refs_2_), channel_id=1, source_target_pairs={{0,4},{2,6},{4,0},{6,2},{8,12},{10,14},{12,8},{14,10},{16,20},{18,... | collective-permute-start | bytes 208904 | tf_op jit(solution)/shard_map/ppermute | solution.py:292
  16.1 2.8 %intra_0.1 = (bf16[512,512]{1,0:T(8,128)(2,1)S(1)}, f32[512,512]{1,0:T(8,128)S(1)}) custom-call(s32[1]{0:T(128)} %bitcast.core_ref.refs_0_, bf16[512,1024]{1,0:T(8,128)(2,1)S(1)} %get-tuple-element.48.own_ref, bf16[512,1024]{1,0:T(8,128)(2,1)S(1)} %collective-permute-done.other_ref, bf16[2048,1024]{1,0:T(8,128)(2,1)S(1)} %stage.1.wq_ref, ...), custom_call_target="tpu_custom_call" | custom-call | tf_op jit(solution)/shard_map/intra_0/pallas_call | solution.py:269
  18.9 1.4 %collective-permute-done.3.refs_4_ = bf16[272,128]{1,0:T(8,128)(2,1)S(1)} collective-permute-done((bf16[272,128]{1,0:T(8,128)(2,1)S(1)}, bf16[272,128]{1,0:T(8,128)(2,1)S(1)}, u32[]{:S(2)}, u32[]{:S(2)}) %collective-permute-start.3) | collective-permute-done | bytes 69664 | tf_op jit(solution)/shard_map/ppermute | solution.py:292
  20.3 1.8 %collective-permute-done.2.refs_3_ = bf16[272,128]{1,0:T(8,128)(2,1)S(1)} collective-permute-done((bf16[272,128]{1,0:T(8,128)(2,1)S(1)}, bf16[272,128]{1,0:T(8,128)(2,1)S(1)}, u32[]{:S(2)}, u32[]{:S(2)}) %collective-permute-start.2) | collective-permute-done | bytes 69664 | tf_op jit(solution)/shard_map/ppermute | solution.py:292
  22.1 0.1 combine.4
  22.2 2.8 %collective-permute-start.7 = (bf16[272,128]{1,0:T(8,128)(2,1)S(1)}, bf16[272,128]{1,0:T(8,128)(2,1)S(1)}, u32[]{:S(2)}, u32[]{:S(2)}) collective-permute-start(bf16[272,128]{1,0:T(8,128)(2,1)S(1)} %get-tuple-element.56.refs_2_), channel_id=1, source_target_pairs={{0,32},{2,34},{4,36},{6,38},{8,40},{10,42},{12,44},{14,46},{16,48}... | collective-permute-start | bytes 208904 | tf_op jit(solution)/shard_map/ppermute | solution.py:292
  25.0 0.9 %collective-permute-start.6 = (bf16[272,128]{1,0:T(8,128)(2,1)S(1)}, bf16[272,128]{1,0:T(8,128)(2,1)S(1)}, u32[]{:S(2)}, u32[]{:S(2)}) collective-permute-start(bf16[272,128]{1,0:T(8,128)(2,1)S(1)} %get-tuple-element.56.refs_2_), channel_id=1, source_target_pairs={{0,48},{2,50},{4,52},{6,54},{8,56},{10,58},{12,60},{14,62},{16,32}... | collective-permute-start | bytes 208904 | tf_op jit(solution)/shard_map/ppermute | solution.py:292
  25.9 2.8 %intra_1.1 = (bf16[512,512]{1,0:T(8,128)(2,1)S(1)}, f32[512,512]{1,0:T(8,128)S(1)}) custom-call(s32[1]{0:T(128)} %bitcast.core_ref.refs_0_, bf16[512,1024]{1,0:T(8,128)(2,1)S(1)} %get-tuple-element.48.own_ref, bf16[512,1024]{1,0:T(8,128)(2,1)S(1)} %collective-permute-done.other_ref, bf16[2048,1024]{1,0:T(8,128)(2,1)S(1)} %stage.1.wq_ref, ...), custom_call_target="tpu_custom_call" | custom-call | tf_op jit(solution)/shard_map/intra_1/pallas_call | solution.py:269
  28.7 1.0 %collective-permute-done.6.refs_4_ = bf16[272,128]{1,0:T(8,128)(2,1)S(1)} collective-permute-done((bf16[272,128]{1,0:T(8,128)(2,1)S(1)}, bf16[272,128]{1,0:T(8,128)(2,1)S(1)}, u32[]{:S(2)}, u32[]{:S(2)}) %collective-permute-start.6) | collective-permute-done | bytes 69664 | tf_op jit(solution)/shard_map/ppermute | solution.py:292
  29.7 0.1 collective-permute-done.5.refs_3_
  29.7 0.1 combine.5
  29.8 3.0 %collective-permute-start.10 = (bf16[272,128]{1,0:T(8,128)(2,1)S(1)}, bf16[272,128]{1,0:T(8,128)(2,1)S(1)}, u32[]{:S(2)}, u32[]{:S(2)}) collective-permute-start(bf16[272,128]{1,0:T(8,128)(2,1)S(1)} %get-tuple-element.63), channel_id=1, source_target_pairs={{0,128},{2,130},{4,132},{6,134},{8,136},{10,138},{12,140},{14,142}... | collective-permute-start | bytes 208904 | tf_op jit(solution)/shard_map/ppermute | solution.py:292
  32.8 0.8 %collective-permute-start.9 = (bf16[272,128]{1,0:T(8,128)(2,1)S(1)}, bf16[272,128]{1,0:T(8,128)(2,1)S(1)}, u32[]{:S(2)}, u32[]{:S(2)}) collective-permute-start(bf16[272,128]{1,0:T(8,128)(2,1)S(1)} %get-tuple-element.63), channel_id=1, source_target_pairs={{0,192},{2,194},{4,196},{6,198},{8,200},{10,202},{12,204},{14,206}... | collective-permute-start | bytes 208904 | tf_op jit(solution)/shard_map/ppermute | solution.py:292
  33.6 0.0 collective-permute-start.8
  33.6 1.0 %collective-permute-done.10.refs_5_ = bf16[272,128]{1,0:T(8,128)(2,1)S(1)} collective-permute-done((bf16[272,128]{1,0:T(8,128)(2,1)S(1)}, bf16[272,128]{1,0:T(8,128)(2,1)S(1)}, u32[]{:S(2)}, u32[]{:S(2)}) %collective-permute-start.10) | collective-permute-done | bytes 69664 | tf_op jit(solution)/shard_map/ppermute | solution.py:292
  34.6 3.4 %collective-permute-done.9.refs_4_ = bf16[272,128]{1,0:T(8,128)(2,1)S(1)} collective-permute-done((bf16[272,128]{1,0:T(8,128)(2,1)S(1)}, bf16[272,128]{1,0:T(8,128)(2,1)S(1)}, u32[]{:S(2)}, u32[]{:S(2)}) %collective-permute-start.9) | collective-permute-done | bytes 69664 | tf_op jit(solution)/shard_map/ppermute | solution.py:292
  38.0 2.1 %norm.1 = (bf16[512,1024]{1,0:T(8,128)(2,1)S(1)}, bf16[256,1024]{1,0:T(8,128)(2,1)S(1)}, bf16[256,1024]{1,0:T(8,128)(2,1)S(1)}) custom-call(s32[1]{0:T(128)} %bitcast.core_ref.refs_0_, s32[1]{0:T(128)} %bitcast.1.refs_0_.refs_1_, f32[256,128]{1,0:T(8,128)S(1)} %get-tuple-element.58.refs_2_, bf16[272,128]{1,0:T(8,128)(2,1)S(1)} %collective-permute-done.8.refs_3_, ...), custom_call_target="tpu_custom_call" | custom-call | tf_op jit(solution)/shard_map/norm/pallas_call | solution.py:324
  40.1 3.4 %collective-permute-start.12 = (bf16[256,1024]{1,0:T(8,128)(2,1)S(1)}, bf16[256,1024]{1,0:T(8,128)(2,1)S(1)}, u32[]{:S(2)}, u32[]{:S(2)}) collective-permute-start(bf16[256,1024]{1,0:T(8,128)(2,1)S(1)} %get-tuple-element.70), channel_id=1, source_target_pairs={{0,1},{1,0},{2,3},{3,2},{4,5},{5,4},{6,7},{7,6},{8,9},{9,8},{10,11... | collective-permute-start | bytes 1572872 | tf_op jit(solution)/shard_map/ppermute | solution.py:222
  43.4 0.1 collective-permute-start.11
  43.5 1.3 %own.1.mine_ref = f32[512,1024]{1,0:T(8,128)S(1)} custom-call(s32[1]{0:T(128)} %bitcast.core_ref.refs_0_, bf16[512,1024]{1,0:T(8,128)(2,1)S(1)} %get-tuple-element.68.normed_ref, bf16[1024,2048]{1,0:T(8,128)(2,1)S(1)} %copy-done), custom_call_target="tpu_custom_call" | custom-call | tf_op jit(solution)/shard_map/own/pallas_call | solution.py:333
  44.8 0.2 collective-permute-done.12.theirs_ref
  45.0 0.9 %add_0.1.refs_0_ = bf16[512,1024]{1,0:T(8,128)(2,1)} custom-call(f32[512,1024]{1,0:T(8,128)S(1)} %own.1.mine_ref, bf16[256,1024]{1,0:T(8,128)(2,1)S(1)} %collective-permute-done.12.theirs_ref), custom_call_target="tpu_custom_call" | custom-call | tf_op jit(solution)/shard_map/add_0/pallas_call | solution.py:344
  45.8 0.8 %add_1.1 = bf16[512,1024]{1,0:T(8,128)(2,1)} custom-call(f32[512,1024]{1,0:T(8,128)S(1)} %own.1.mine_ref, bf16[256,1024]{1,0:T(8,128)(2,1)S(1)} %collective-permute-done.11.theirs_ref, bf16[512,1024]{1,0:T(8,128)(2,1)} %add_0.1.refs_0_), custom_call_target="tpu_custom_call", output_to_operand_aliasing={{}: (2, {})} | custom-call | tf_op jit(solution)/shard_map/add_1/pallas_call | solution.py:344
  (10 shorter events, 0.1 us)
Async XLA Ops:
  0.0 5.7 %collective-permute-start = (bf16[512,1024]{1,0:T(8,128)(2,1)}, bf16[512,1024]{1,0:T(8,128)(2,1)S(1)}, u32[]{:S(2)}, u32[]{:S(2)}) collective-permute-start(bf16[512,1024]{1,0:T(8,128)(2,1)} %own_hbm.1), channel_id=1, source_target_pairs={{0,1},{1,0},{2,3},{3,2},{4,5},{5,4},{6,7},{7,6},{8,9},{9,8},{10,11... | collective-permute-start | bytes 3145736 | tf_op jit(solution)/shard_map/ppermute | solution.py:222
  6.8 3.2 %collective-permute-start.1 = (bf16[272,128]{1,0:T(8,128)(2,1)S(1)}, bf16[272,128]{1,0:T(8,128)(2,1)S(1)}, u32[]{:S(2)}, u32[]{:S(2)}) collective-permute-start(bf16[272,128]{1,0:T(8,128)(2,1)S(1)} %get-tuple-element.43.refs_2_.after_ref), channel_id=1, source_target_pairs={{0,2},{2,0},{4,6},{6,4},{8,10},{10,8},{12,14},{14,12},{16,18},{18,... | collective-permute-start | bytes 208904 | tf_op jit(solution)/shard_map/ppermute | solution.py:292
  10.1 8.8 %collective-permute-start.4 = (bf16[272,128]{1,0:T(8,128)(2,1)S(1)}, bf16[272,128]{1,0:T(8,128)(2,1)S(1)}, u32[]{:S(2)}, u32[]{:S(2)}) collective-permute-start(bf16[272,128]{1,0:T(8,128)(2,1)S(1)} %get-tuple-element.45.refs_2_), channel_id=1, source_target_pairs={{0,10},{2,8},{4,14},{6,12},{8,2},{10,0},{12,6},{14,4},{16,26},{18,... | collective-permute-start | bytes 208904 | tf_op jit(solution)/shard_map/ppermute | solution.py:292
  14.9 5.4 %collective-permute-start.3 = (bf16[272,128]{1,0:T(8,128)(2,1)S(1)}, bf16[272,128]{1,0:T(8,128)(2,1)S(1)}, u32[]{:S(2)}, u32[]{:S(2)}) collective-permute-start(bf16[272,128]{1,0:T(8,128)(2,1)S(1)} %get-tuple-element.45.refs_2_), channel_id=1, source_target_pairs={{0,12},{2,14},{4,8},{6,10},{8,4},{10,6},{12,0},{14,2},{16,28},{18,... | collective-permute-start | bytes 208904 | tf_op jit(solution)/shard_map/ppermute | solution.py:292
  15.2 6.9 %collective-permute-start.2 = (bf16[272,128]{1,0:T(8,128)(2,1)S(1)}, bf16[272,128]{1,0:T(8,128)(2,1)S(1)}, u32[]{:S(2)}, u32[]{:S(2)}) collective-permute-start(bf16[272,128]{1,0:T(8,128)(2,1)S(1)} %get-tuple-element.45.refs_2_), channel_id=1, source_target_pairs={{0,4},{2,6},{4,0},{6,2},{8,12},{10,14},{12,8},{14,10},{16,20},{18,... | collective-permute-start | bytes 208904 | tf_op jit(solution)/shard_map/ppermute | solution.py:292
  22.1 15.9 %copy-start = (bf16[1024,2048]{1,0:T(8,128)(2,1)S(1)}, bf16[1024,2048]{1,0:T(8,128)(2,1)}, u32[]{:S(2)}) copy-start(bf16[1024,2048]{1,0:T(8,128)(2,1)} %weight_ref.1) | copy-start | bytes 12582916
  22.1 15.9 %copy-start.1 = (f32[1024]{0:T(1024)S(1)}, f32[1024]{0:T(1024)}, u32[]{:S(2)}) copy-start(f32[1024]{0:T(1024)} %param.11) | copy-start | bytes 12292
  22.2 6.5 %collective-permute-start.7 = (bf16[272,128]{1,0:T(8,128)(2,1)S(1)}, bf16[272,128]{1,0:T(8,128)(2,1)S(1)}, u32[]{:S(2)}, u32[]{:S(2)}) collective-permute-start(bf16[272,128]{1,0:T(8,128)(2,1)S(1)} %get-tuple-element.56.refs_2_), channel_id=1, source_target_pairs={{0,32},{2,34},{4,36},{6,38},{8,40},{10,42},{12,44},{14,46},{16,48}... | collective-permute-start | bytes 208904 | tf_op jit(solution)/shard_map/ppermute | solution.py:292
  25.0 4.6 %collective-permute-start.6 = (bf16[272,128]{1,0:T(8,128)(2,1)S(1)}, bf16[272,128]{1,0:T(8,128)(2,1)S(1)}, u32[]{:S(2)}, u32[]{:S(2)}) collective-permute-start(bf16[272,128]{1,0:T(8,128)(2,1)S(1)} %get-tuple-element.56.refs_2_), channel_id=1, source_target_pairs={{0,48},{2,50},{4,52},{6,54},{8,56},{10,58},{12,60},{14,62},{16,32}... | collective-permute-start | bytes 208904 | tf_op jit(solution)/shard_map/ppermute | solution.py:292
  25.9 3.9 %collective-permute-start.5 = (bf16[272,128]{1,0:T(8,128)(2,1)S(1)}, bf16[272,128]{1,0:T(8,128)(2,1)S(1)}, u32[]{:S(2)}, u32[]{:S(2)}) collective-permute-start(bf16[272,128]{1,0:T(8,128)(2,1)S(1)} %get-tuple-element.56.refs_2_), channel_id=1, source_target_pairs={{0,16},{2,18},{4,20},{6,22},{8,24},{10,26},{12,28},{14,30},{16,0},... | collective-permute-start | bytes 208904 | tf_op jit(solution)/shard_map/ppermute | solution.py:292
  29.8 4.8 %collective-permute-start.10 = (bf16[272,128]{1,0:T(8,128)(2,1)S(1)}, bf16[272,128]{1,0:T(8,128)(2,1)S(1)}, u32[]{:S(2)}, u32[]{:S(2)}) collective-permute-start(bf16[272,128]{1,0:T(8,128)(2,1)S(1)} %get-tuple-element.63), channel_id=1, source_target_pairs={{0,128},{2,130},{4,132},{6,134},{8,136},{10,138},{12,140},{14,142}... | collective-permute-start | bytes 208904 | tf_op jit(solution)/shard_map/ppermute | solution.py:292
  32.8 5.1 %collective-permute-start.9 = (bf16[272,128]{1,0:T(8,128)(2,1)S(1)}, bf16[272,128]{1,0:T(8,128)(2,1)S(1)}, u32[]{:S(2)}, u32[]{:S(2)}) collective-permute-start(bf16[272,128]{1,0:T(8,128)(2,1)S(1)} %get-tuple-element.63), channel_id=1, source_target_pairs={{0,192},{2,194},{4,196},{6,198},{8,200},{10,202},{12,204},{14,206}... | collective-permute-start | bytes 208904 | tf_op jit(solution)/shard_map/ppermute | solution.py:292
  33.6 4.3 %collective-permute-start.8 = (bf16[272,128]{1,0:T(8,128)(2,1)S(1)}, bf16[272,128]{1,0:T(8,128)(2,1)S(1)}, u32[]{:S(2)}, u32[]{:S(2)}) collective-permute-start(bf16[272,128]{1,0:T(8,128)(2,1)S(1)} %get-tuple-element.63), channel_id=1, source_target_pairs={{0,64},{2,66},{4,68},{6,70},{8,72},{10,74},{12,76},{14,78},{16,80}... | collective-permute-start | bytes 208904 | tf_op jit(solution)/shard_map/ppermute | solution.py:292
  40.1 4.9 %collective-permute-start.12 = (bf16[256,1024]{1,0:T(8,128)(2,1)S(1)}, bf16[256,1024]{1,0:T(8,128)(2,1)S(1)}, u32[]{:S(2)}, u32[]{:S(2)}) collective-permute-start(bf16[256,1024]{1,0:T(8,128)(2,1)S(1)} %get-tuple-element.70), channel_id=1, source_target_pairs={{0,1},{1,0},{2,3},{3,2},{4,5},{5,4},{6,7},{7,6},{8,9},{9,8},{10,11... | collective-permute-start | bytes 1572872 | tf_op jit(solution)/shard_map/ppermute | solution.py:222
  43.4 2.4 %collective-permute-start.11 = (bf16[256,1024]{1,0:T(8,128)(2,1)S(1)}, bf16[256,1024]{1,0:T(8,128)(2,1)S(1)}, u32[]{:S(2)}, u32[]{:S(2)}) collective-permute-start(bf16[256,1024]{1,0:T(8,128)(2,1)S(1)} %get-tuple-element.69), channel_id=1, source_target_pairs={{0,1},{1,0},{2,3},{3,2},{4,5},{5,4},{6,7},{7,6},{8,9},{9,8},{10,11... | collective-permute-start | bytes 1572872 | tf_op jit(solution)/shard_map/ppermute | solution.py:222

commit v6 on v5

--- a/solution.py
+++ b/solution.py
@@ -8,7 +8,7 @@
 HEAD = 128
 ID_ROWS = 16
 BLOCK = 256
-ROUNDS = ((1,), (2, 6, 5), (8, 24, 16), (32, 96, 64))
+ROUNDS = ((1, 2, 3), (6,), (8, 24, 16), (32, 96, 64))
 INTRA_STEPS = (1, 2)
 CHUNKS = 2
 STAGE_COPIES = 4

time: 46.7 us -> 46 us (0.985)
  waiting for transfers between devices: 10.2 us -> 9.1 us
    ppermute x10, waiting for transfers between devices: 9.56 us -> 8.49 us  [on_device(): lax.ppermute(message, 'seq', [(i, i ^ b) for i in range(count)])]
  transfers between devices with their start and end apart: 13 -> 13, of which waited for: 9 -> 7; matrix products, arithmetic and copies ran while one was open for 0% -> 0% of each run, Pallas kernels for 25% -> 26%
where the time goes in v6:
time: 46 us; the launch traced here: 45.9 us
  starting transfers between devices  20.6 us (45%)
  Pallas kernels  16.1 us (35%)
  waiting for transfers between devices  9.1 us (20%)
    ppermute x10, starting transfers between devices, on_device(): lax.ppermute(message, 'seq', [(i, i ^ b) for i in range(count)])  13.9 us
    ppermute x10, waiting for transfers between devices, on_device(): lax.ppermute(message, 'seq', [(i, i ^ b) for i in range(count)])  8.49 us
    ppermute x3, starting transfers between devices, swap_head(): return lax.ppermute(x, 'head', [(0, 1), (1, 0)])  6.7 us
    pallas_call x2, Pallas kernels, intra(): pl.pallas_call(intra_kernel, out_shape=(shape((rows, group_width), BF16),...  5.53 us
    pallas_call x1, Pallas kernels, on_device(): pl.pallas_call(stage_kernel, out_shape=shape(q_weight.shape, BF16), in_sp...  2.2 us
    pallas_call x1, Pallas kernels, on_device(): pl.pallas_call(lambda *refs: norm_kernel(ROUNDS[-1], kv_heads, *refs), ou...  2.08 us
    pallas_call x1, Pallas kernels, on_device(): pl.pallas_call(own_half_kernel, out_shape=(shape(tokens.shape, BF16), sha...  2.06 us
    pallas_call x2, Pallas kernels, on_device(): pl.pallas_call(add_kernel, grid=(ADD_STEPS,), out_shape=shape((rows, half...  1.69 us
  transfers between devices with their start and end apart: 13, of which 7 were waited for; matrix products, arithmetic and copies ran while one was open for 0% of the time, Pallas kernels for 26%

profile of v6, /device:TPU:1, one launch (start us, length us, event | category | flops | bytes accessed | tf_op | source)
XLA Modules:
  0.0 45.9 jit_solution(9513828369948570377)
XLA Ops:
  0.0 3.2 %collective-permute-start = (bf16[512,1024]{1,0:T(8,128)(2,1)}, bf16[512,1024]{1,0:T(8,128)(2,1)S(1)}, u32[]{:S(2)}, u32[]{:S(2)}) collective-permute-start(bf16[512,1024]{1,0:T(8,128)(2,1)} %own_hbm.1), channel_id=1, source_target_pairs={{0,1},{1,0},{2,3},{3,2},{4,5},{5,4},{6,7},{7,6},{8,9},{9,8},{10,11... | collective-permute-start | bytes 3145736 | tf_op jit(solution)/shard_map/ppermute | solution.py:222
  3.2 2.1 %own_half.1 = (bf16[512,1024]{1,0:T(8,128)(2,1)S(1)}, bf16[2048,256]{1,0:T(8,128)(2,1)S(1)}, bf16[2048,256]{1,0:T(8,128)(2,1)S(1)}, f32[512,256]{1,0:T(8,128)S(1...) custom-call(s32[1]{0:T(128)} %bitcast.core_ref.refs_0_, s32[1,512]{1,0:T(1,128)} %bitcast.5, ...), custom_call_target="tpu_custom_call" | custom-call | tf_op jit(solution)/shard_map/own_half/pallas_call | solution.py:237
  5.3 0.4 collective-permute-done.other_ref
  5.7 1.0 %key_value.1 = (bf16[512,256]{1,0:T(8,128)(2,1)S(1)}, bf16[512,256]{1,0:T(8,128)(2,1)S(1)}, bf16[272,128]{1,0:T(8,128)(2,1)S(1)}) custom-call(s32[1]{0:T(128)} %bitcast.core_ref.refs_0_, bf16[512,1024]{1,0:T(8,128)(2,1)S(1)} %collective-permute-done.other_ref, f32[512,256]{1,0:T(8,128)S(1)} %get-tuple-element.39.k_part_ref, ...), custom_call_target="tpu_custom_call" | custom-call | tf_op jit(solution)/shard_map/key_value/pallas_call | solution.py:255
  6.8 2.7 %collective-permute-start.3 = (bf16[272,128]{1,0:T(8,128)(2,1)S(1)}, bf16[272,128]{1,0:T(8,128)(2,1)S(1)}, u32[]{:S(2)}, u32[]{:S(2)}) collective-permute-start(bf16[272,128]{1,0:T(8,128)(2,1)S(1)} %get-tuple-element.43.refs_2_.after_ref), channel_id=1, source_target_pairs={{0,6},{2,4},{4,2},{6,0},{8,14},{10,12},{12,10},{14,8},{16,22},{18,... | collective-permute-start | bytes 208904 | tf_op jit(solution)/shard_map/ppermute | solution.py:292
  9.5 0.0 collective-permute-start.2
  9.5 0.9 %collective-permute-start.1 = (bf16[272,128]{1,0:T(8,128)(2,1)S(1)}, bf16[272,128]{1,0:T(8,128)(2,1)S(1)}, u32[]{:S(2)}, u32[]{:S(2)}) collective-permute-start(bf16[272,128]{1,0:T(8,128)(2,1)S(1)} %get-tuple-element.43.refs_2_.after_ref), channel_id=1, source_target_pairs={{0,2},{2,0},{4,6},{6,4},{8,10},{10,8},{12,14},{14,12},{16,18},{18,... | collective-permute-start | bytes 208904 | tf_op jit(solution)/shard_map/ppermute | solution.py:292
  10.4 2.2 %stage.1.wq_ref = bf16[2048,1024]{1,0:T(8,128)(2,1)S(1)} custom-call(bf16[272,128]{1,0:T(8,128)(2,1)S(1)} %get-tuple-element.43.refs_2_.after_ref, bf16[2048,1024]{1,0:T(8,128)(2,1)} %weight_hbm.1), custom_call_target="tpu_custom_call" | custom-call | tf_op jit(solution)/shard_map/stage/pallas_call | solution.py:294
  12.6 3.1 %collective-permute-done.2.refs_4_ = bf16[272,128]{1,0:T(8,128)(2,1)S(1)} collective-permute-done((bf16[272,128]{1,0:T(8,128)(2,1)S(1)}, bf16[272,128]{1,0:T(8,128)(2,1)S(1)}, u32[]{:S(2)}, u32[]{:S(2)}) %collective-permute-start.2) | collective-permute-done | bytes 69664 | tf_op jit(solution)/shard_map/ppermute | solution.py:292
  15.8 0.1 combine.3
  15.8 2.8 %collective-permute-start.4 = (bf16[272,128]{1,0:T(8,128)(2,1)S(1)}, bf16[272,128]{1,0:T(8,128)(2,1)S(1)}, u32[]{:S(2)}, u32[]{:S(2)}) collective-permute-start(bf16[272,128]{1,0:T(8,128)(2,1)S(1)} %get-tuple-element.45.refs_2_), channel_id=1, source_target_pairs={{0,12},{2,14},{4,8},{6,10},{8,4},{10,6},{12,0},{14,2},{16,28},{18,... | collective-permute-start | bytes 208904 | tf_op jit(solution)/shard_map/ppermute | solution.py:292
  18.6 2.8 %intra_0.1 = (bf16[512,512]{1,0:T(8,128)(2,1)S(1)}, f32[512,512]{1,0:T(8,128)S(1)}) custom-call(s32[1]{0:T(128)} %bitcast.core_ref.refs_0_, bf16[512,1024]{1,0:T(8,128)(2,1)S(1)} %get-tuple-element.48.own_ref, bf16[512,1024]{1,0:T(8,128)(2,1)S(1)} %collective-permute-done.other_ref, bf16[2048,1024]{1,0:T(8,128)(2,1)S(1)} %stage.1.wq_ref, ...), custom_call_target="tpu_custom_call" | custom-call | tf_op jit(solution)/shard_map/intra_0/pallas_call | solution.py:269
  21.4 0.0 copy-start
  21.4 0.0 copy-start.1
  21.5 2.8 %collective-permute-start.7 = (bf16[272,128]{1,0:T(8,128)(2,1)S(1)}, bf16[272,128]{1,0:T(8,128)(2,1)S(1)}, u32[]{:S(2)}, u32[]{:S(2)}) collective-permute-start(bf16[272,128]{1,0:T(8,128)(2,1)S(1)} %get-tuple-element.56.refs_2_), channel_id=1, source_target_pairs={{0,32},{2,34},{4,36},{6,38},{8,40},{10,42},{12,44},{14,46},{16,48}... | collective-permute-start | bytes 208904 | tf_op jit(solution)/shard_map/ppermute | solution.py:292
  24.3 0.9 %collective-permute-start.6 = (bf16[272,128]{1,0:T(8,128)(2,1)S(1)}, bf16[272,128]{1,0:T(8,128)(2,1)S(1)}, u32[]{:S(2)}, u32[]{:S(2)}) collective-permute-start(bf16[272,128]{1,0:T(8,128)(2,1)S(1)} %get-tuple-element.56.refs_2_), channel_id=1, source_target_pairs={{0,48},{2,50},{4,52},{6,54},{8,56},{10,58},{12,60},{14,62},{16,32}... | collective-permute-start | bytes 208904 | tf_op jit(solution)/shard_map/ppermute | solution.py:292
  25.2 2.8 %intra_1.1 = (bf16[512,512]{1,0:T(8,128)(2,1)S(1)}, f32[512,512]{1,0:T(8,128)S(1)}) custom-call(s32[1]{0:T(128)} %bitcast.core_ref.refs_0_, bf16[512,1024]{1,0:T(8,128)(2,1)S(1)} %get-tuple-element.48.own_ref, bf16[512,1024]{1,0:T(8,128)(2,1)S(1)} %collective-permute-done.other_ref, bf16[2048,1024]{1,0:T(8,128)(2,1)S(1)} %stage.1.wq_ref, ...), custom_call_target="tpu_custom_call" | custom-call | tf_op jit(solution)/shard_map/intra_1/pallas_call | solution.py:269
  28.0 1.0 %collective-permute-done.6.refs_4_ = bf16[272,128]{1,0:T(8,128)(2,1)S(1)} collective-permute-done((bf16[272,128]{1,0:T(8,128)(2,1)S(1)}, bf16[272,128]{1,0:T(8,128)(2,1)S(1)}, u32[]{:S(2)}, u32[]{:S(2)}) %collective-permute-start.6) | collective-permute-done | bytes 69664 | tf_op jit(solution)/shard_map/ppermute | solution.py:292
  28.9 0.1 collective-permute-done.5.refs_3_
  29.0 0.1 combine.5
  29.1 3.0 %collective-permute-start.10 = (bf16[272,128]{1,0:T(8,128)(2,1)S(1)}, bf16[272,128]{1,0:T(8,128)(2,1)S(1)}, u32[]{:S(2)}, u32[]{:S(2)}) collective-permute-start(bf16[272,128]{1,0:T(8,128)(2,1)S(1)} %get-tuple-element.63), channel_id=1, source_target_pairs={{0,128},{2,130},{4,132},{6,134},{8,136},{10,138},{12,140},{14,142}... | collective-permute-start | bytes 208904 | tf_op jit(solution)/shard_map/ppermute | solution.py:292
  32.1 0.8 %collective-permute-start.9 = (bf16[272,128]{1,0:T(8,128)(2,1)S(1)}, bf16[272,128]{1,0:T(8,128)(2,1)S(1)}, u32[]{:S(2)}, u32[]{:S(2)}) collective-permute-start(bf16[272,128]{1,0:T(8,128)(2,1)S(1)} %get-tuple-element.63), channel_id=1, source_target_pairs={{0,192},{2,194},{4,196},{6,198},{8,200},{10,202},{12,204},{14,206}... | collective-permute-start | bytes 208904 | tf_op jit(solution)/shard_map/ppermute | solution.py:292
  32.9 0.0 collective-permute-start.8
  32.9 1.0 %collective-permute-done.10.refs_5_ = bf16[272,128]{1,0:T(8,128)(2,1)S(1)} collective-permute-done((bf16[272,128]{1,0:T(8,128)(2,1)S(1)}, bf16[272,128]{1,0:T(8,128)(2,1)S(1)}, u32[]{:S(2)}, u32[]{:S(2)}) %collective-permute-start.10) | collective-permute-done | bytes 69664 | tf_op jit(solution)/shard_map/ppermute | solution.py:292
  33.9 3.4 %collective-permute-done.9.refs_4_ = bf16[272,128]{1,0:T(8,128)(2,1)S(1)} collective-permute-done((bf16[272,128]{1,0:T(8,128)(2,1)S(1)}, bf16[272,128]{1,0:T(8,128)(2,1)S(1)}, u32[]{:S(2)}, u32[]{:S(2)}) %collective-permute-start.9) | collective-permute-done | bytes 69664 | tf_op jit(solution)/shard_map/ppermute | solution.py:292
  37.3 2.1 %norm.1 = (bf16[512,1024]{1,0:T(8,128)(2,1)S(1)}, bf16[256,1024]{1,0:T(8,128)(2,1)S(1)}, bf16[256,1024]{1,0:T(8,128)(2,1)S(1)}) custom-call(s32[1]{0:T(128)} %bitcast.core_ref.refs_0_, s32[1]{0:T(128)} %bitcast.1.refs_0_.refs_1_, f32[256,128]{1,0:T(8,128)S(1)} %get-tuple-element.58.refs_2_, bf16[272,128]{1,0:T(8,128)(2,1)S(1)} %collective-permute-done.8.refs_3_, ...), custom_call_target="tpu_custom_call" | custom-call | tf_op jit(solution)/shard_map/norm/pallas_call | solution.py:324
  39.3 3.4 %collective-permute-start.12 = (bf16[256,1024]{1,0:T(8,128)(2,1)S(1)}, bf16[256,1024]{1,0:T(8,128)(2,1)S(1)}, u32[]{:S(2)}, u32[]{:S(2)}) collective-permute-start(bf16[256,1024]{1,0:T(8,128)(2,1)S(1)} %get-tuple-element.70), channel_id=1, source_target_pairs={{0,1},{1,0},{2,3},{3,2},{4,5},{5,4},{6,7},{7,6},{8,9},{9,8},{10,11... | collective-permute-start | bytes 1572872 | tf_op jit(solution)/shard_map/ppermute | solution.py:222
  42.7 0.1 collective-permute-start.11
  42.8 1.3 %own.1.mine_ref = f32[512,1024]{1,0:T(8,128)S(1)} custom-call(s32[1]{0:T(128)} %bitcast.core_ref.refs_0_, bf16[512,1024]{1,0:T(8,128)(2,1)S(1)} %get-tuple-element.68.normed_ref, bf16[1024,2048]{1,0:T(8,128)(2,1)S(1)} %copy-done), custom_call_target="tpu_custom_call" | custom-call | tf_op jit(solution)/shard_map/own/pallas_call | solution.py:333
  44.1 0.2 collective-permute-done.12.theirs_ref
  44.2 0.9 %add_0.1.refs_0_ = bf16[512,1024]{1,0:T(8,128)(2,1)} custom-call(f32[512,1024]{1,0:T(8,128)S(1)} %own.1.mine_ref, bf16[256,1024]{1,0:T(8,128)(2,1)S(1)} %collective-permute-done.12.theirs_ref), custom_call_target="tpu_custom_call" | custom-call | tf_op jit(solution)/shard_map/add_0/pallas_call | solution.py:344
  45.1 0.8 %add_1.1 = bf16[512,1024]{1,0:T(8,128)(2,1)} custom-call(f32[512,1024]{1,0:T(8,128)S(1)} %own.1.mine_ref, bf16[256,1024]{1,0:T(8,128)(2,1)S(1)} %collective-permute-done.11.theirs_ref, bf16[512,1024]{1,0:T(8,128)(2,1)} %add_0.1.refs_0_), custom_call_target="tpu_custom_call", output_to_operand_aliasing={{}: (2, {})} | custom-call | tf_op jit(solution)/shard_map/add_1/pallas_call | solution.py:344
  (10 shorter events, 0.1 us)
Async XLA Ops:
  0.0 5.7 %collective-permute-start = (bf16[512,1024]{1,0:T(8,128)(2,1)}, bf16[512,1024]{1,0:T(8,128)(2,1)S(1)}, u32[]{:S(2)}, u32[]{:S(2)}) collective-permute-start(bf16[512,1024]{1,0:T(8,128)(2,1)} %own_hbm.1), channel_id=1, source_target_pairs={{0,1},{1,0},{2,3},{3,2},{4,5},{5,4},{6,7},{7,6},{8,9},{9,8},{10,11... | collective-permute-start | bytes 3145736 | tf_op jit(solution)/shard_map/ppermute | solution.py:222
  6.8 5.9 %collective-permute-start.3 = (bf16[272,128]{1,0:T(8,128)(2,1)S(1)}, bf16[272,128]{1,0:T(8,128)(2,1)S(1)}, u32[]{:S(2)}, u32[]{:S(2)}) collective-permute-start(bf16[272,128]{1,0:T(8,128)(2,1)S(1)} %get-tuple-element.43.refs_2_.after_ref), channel_id=1, source_target_pairs={{0,6},{2,4},{4,2},{6,0},{8,14},{10,12},{12,10},{14,8},{16,22},{18,... | collective-permute-start | bytes 208904 | tf_op jit(solution)/shard_map/ppermute | solution.py:292
  9.5 6.3 %collective-permute-start.2 = (bf16[272,128]{1,0:T(8,128)(2,1)S(1)}, bf16[272,128]{1,0:T(8,128)(2,1)S(1)}, u32[]{:S(2)}, u32[]{:S(2)}) collective-permute-start(bf16[272,128]{1,0:T(8,128)(2,1)S(1)} %get-tuple-element.43.refs_2_.after_ref), channel_id=1, source_target_pairs={{0,4},{2,6},{4,0},{6,2},{8,12},{10,14},{12,8},{14,10},{16,20},{18,... | collective-permute-start | bytes 208904 | tf_op jit(solution)/shard_map/ppermute | solution.py:292
  9.5 6.3 %collective-permute-start.1 = (bf16[272,128]{1,0:T(8,128)(2,1)S(1)}, bf16[272,128]{1,0:T(8,128)(2,1)S(1)}, u32[]{:S(2)}, u32[]{:S(2)}) collective-permute-start(bf16[272,128]{1,0:T(8,128)(2,1)S(1)} %get-tuple-element.43.refs_2_.after_ref), channel_id=1, source_target_pairs={{0,2},{2,0},{4,6},{6,4},{8,10},{10,8},{12,14},{14,12},{16,18},{18,... | collective-permute-start | bytes 208904 | tf_op jit(solution)/shard_map/ppermute | solution.py:292
  15.8 5.6 %collective-permute-start.4 = (bf16[272,128]{1,0:T(8,128)(2,1)S(1)}, bf16[272,128]{1,0:T(8,128)(2,1)S(1)}, u32[]{:S(2)}, u32[]{:S(2)}) collective-permute-start(bf16[272,128]{1,0:T(8,128)(2,1)S(1)} %get-tuple-element.45.refs_2_), channel_id=1, source_target_pairs={{0,12},{2,14},{4,8},{6,10},{8,4},{10,6},{12,0},{14,2},{16,28},{18,... | collective-permute-start | bytes 208904 | tf_op jit(solution)/shard_map/ppermute | solution.py:292
  21.4 15.8 %copy-start = (bf16[1024,2048]{1,0:T(8,128)(2,1)S(1)}, bf16[1024,2048]{1,0:T(8,128)(2,1)}, u32[]{:S(2)}) copy-start(bf16[1024,2048]{1,0:T(8,128)(2,1)} %weight_ref.1) | copy-start | bytes 12582916
  21.4 15.8 %copy-start.1 = (f32[1024]{0:T(1024)S(1)}, f32[1024]{0:T(1024)}, u32[]{:S(2)}) copy-start(f32[1024]{0:T(1024)} %param.11) | copy-start | bytes 12292
  21.5 6.5 %collective-permute-start.7 = (bf16[272,128]{1,0:T(8,128)(2,1)S(1)}, bf16[272,128]{1,0:T(8,128)(2,1)S(1)}, u32[]{:S(2)}, u32[]{:S(2)}) collective-permute-start(bf16[272,128]{1,0:T(8,128)(2,1)S(1)} %get-tuple-element.56.refs_2_), channel_id=1, source_target_pairs={{0,32},{2,34},{4,36},{6,38},{8,40},{10,42},{12,44},{14,46},{16,48}... | collective-permute-start | bytes 208904 | tf_op jit(solution)/shard_map/ppermute | solution.py:292
  24.3 4.6 %collective-permute-start.6 = (bf16[272,128]{1,0:T(8,128)(2,1)S(1)}, bf16[272,128]{1,0:T(8,128)(2,1)S(1)}, u32[]{:S(2)}, u32[]{:S(2)}) collective-permute-start(bf16[272,128]{1,0:T(8,128)(2,1)S(1)} %get-tuple-element.56.refs_2_), channel_id=1, source_target_pairs={{0,48},{2,50},{4,52},{6,54},{8,56},{10,58},{12,60},{14,62},{16,32}... | collective-permute-start | bytes 208904 | tf_op jit(solution)/shard_map/ppermute | solution.py:292
  25.2 3.8 %collective-permute-start.5 = (bf16[272,128]{1,0:T(8,128)(2,1)S(1)}, bf16[272,128]{1,0:T(8,128)(2,1)S(1)}, u32[]{:S(2)}, u32[]{:S(2)}) collective-permute-start(bf16[272,128]{1,0:T(8,128)(2,1)S(1)} %get-tuple-element.56.refs_2_), channel_id=1, source_target_pairs={{0,16},{2,18},{4,20},{6,22},{8,24},{10,26},{12,28},{14,30},{16,0},... | collective-permute-start | bytes 208904 | tf_op jit(solution)/shard_map/ppermute | solution.py:292
  29.1 4.8 %collective-permute-start.10 = (bf16[272,128]{1,0:T(8,128)(2,1)S(1)}, bf16[272,128]{1,0:T(8,128)(2,1)S(1)}, u32[]{:S(2)}, u32[]{:S(2)}) collective-permute-start(bf16[272,128]{1,0:T(8,128)(2,1)S(1)} %get-tuple-element.63), channel_id=1, source_target_pairs={{0,128},{2,130},{4,132},{6,134},{8,136},{10,138},{12,140},{14,142}... | collective-permute-start | bytes 208904 | tf_op jit(solution)/shard_map/ppermute | solution.py:292
  32.1 5.1 %collective-permute-start.9 = (bf16[272,128]{1,0:T(8,128)(2,1)S(1)}, bf16[272,128]{1,0:T(8,128)(2,1)S(1)}, u32[]{:S(2)}, u32[]{:S(2)}) collective-permute-start(bf16[272,128]{1,0:T(8,128)(2,1)S(1)} %get-tuple-element.63), channel_id=1, source_target_pairs={{0,192},{2,194},{4,196},{6,198},{8,200},{10,202},{12,204},{14,206}... | collective-permute-start | bytes 208904 | tf_op jit(solution)/shard_map/ppermute | solution.py:292
  32.9 4.3 %collective-permute-start.8 = (bf16[272,128]{1,0:T(8,128)(2,1)S(1)}, bf16[272,128]{1,0:T(8,128)(2,1)S(1)}, u32[]{:S(2)}, u32[]{:S(2)}) collective-permute-start(bf16[272,128]{1,0:T(8,128)(2,1)S(1)} %get-tuple-element.63), channel_id=1, source_target_pairs={{0,64},{2,66},{4,68},{6,70},{8,72},{10,74},{12,76},{14,78},{16,80}... | collective-permute-start | bytes 208904 | tf_op jit(solution)/shard_map/ppermute | solution.py:292
  39.3 4.9 %collective-permute-start.12 = (bf16[256,1024]{1,0:T(8,128)(2,1)S(1)}, bf16[256,1024]{1,0:T(8,128)(2,1)S(1)}, u32[]{:S(2)}, u32[]{:S(2)}) collective-permute-start(bf16[256,1024]{1,0:T(8,128)(2,1)S(1)} %get-tuple-element.70), channel_id=1, source_target_pairs={{0,1},{1,0},{2,3},{3,2},{4,5},{5,4},{6,7},{7,6},{8,9},{9,8},{10,11... | collective-permute-start | bytes 1572872 | tf_op jit(solution)/shard_map/ppermute | solution.py:222
  42.7 2.4 %collective-permute-start.11 = (bf16[256,1024]{1,0:T(8,128)(2,1)S(1)}, bf16[256,1024]{1,0:T(8,128)(2,1)S(1)}, u32[]{:S(2)}, u32[]{:S(2)}) collective-permute-start(bf16[256,1024]{1,0:T(8,128)(2,1)S(1)} %get-tuple-element.69), channel_id=1, source_target_pairs={{0,1},{1,0},{2,3},{3,2},{4,5},{5,4},{6,7},{7,6},{8,9},{9,8},{10,11... | collective-permute-start | bytes 1572872 | tf_op jit(solution)/shard_map/ppermute | solution.py:222

commit v7 on v6

--- a/solution.py
+++ b/solution.py
@@ -105,12 +105,18 @@
     message_ref[heads * HEAD :, :] = jnp.broadcast_to(last, (ID_ROWS, HEAD)).astype(BF16)
 
 
-def stage_kernel(after_ref, weight_hbm, weight_ref, sems):
-    size = weight_ref.shape[0] // STAGE_COPIES
+def stage_kernel(core_ref, after_ref, wq_hbm, out_hbm, wq_ref, far_ref, sems):
+    half = far_ref.shape[1]
+    far = pl.ds(pl.multiple_of((1 - core_ref[0]) * half, half), half)
     copies = []
     for i in range(STAGE_COPIES):
+        size = wq_ref.shape[0] // STAGE_COPIES
         cut = slice(i * size, (i + 1) * size)
-        copies.append(pltpu.make_async_copy(weight_hbm.at[cut, :], weight_ref.at[cut, :], sems.at[i]))
+        copies.append((wq_hbm.at[cut, :], wq_ref.at[cut, :]))
+        size = far_ref.shape[0] // STAGE_COPIES
+        cut = slice(i * size, (i + 1) * size)
+        copies.append((out_hbm.at[cut, far], far_ref.at[cut, :]))
+    copies = [pltpu.make_async_copy(a, b, sems.at[i]) for i, (a, b) in enumerate(copies)]
     for copy in copies:
         copy.start()
     for copy in copies:
@@ -172,10 +178,10 @@
     return held.astype(BF16)
 
 
-def norm_kernel(bits, groups, core_ref, place_ref, held_ref, *refs):
+def norm_kernel(bits, groups, place_ref, held_ref, *refs):
     got, refs = refs[: len(bits)], refs[len(bits) :]
     queries, intras, refs = refs[:groups], refs[groups : 2 * groups], refs[2 * groups :]
-    col_ref, gain_ref, weight_ref, normed_ref, *theirs = refs
+    col_ref, gain_ref, *normed = refs
     incoming = incoming_of(bits, place_ref, col_ref, held_ref, got)
     for start in range(0, col_ref.shape[0], BLOCK):
         here = slice(start, start + BLOCK)
@@ -188,8 +194,7 @@
                 carried = dot(queries[k][here, cut], incoming[k * HEAD : (k + 1) * HEAD, :])
                 combined = intras[k][here, cut] + jnp.where(joins, carried, 0.0)
                 scale = lax.rsqrt(jnp.mean(combined * combined, axis=-1, keepdims=True) + EPSILON)
-                normed_ref[here, out] = (combined * scale * gain_ref[:1, out]).astype(BF16)
-        theirs[start // BLOCK][...] = dot(normed_ref[here, :], columns(weight_ref, 1 - core_ref[0])).astype(BF16)
+                normed[start // BLOCK][:, out] = (combined * scale * gain_ref[:1, out]).astype(BF16)
 
 
 def columns(weight_ref, part):
@@ -197,17 +202,20 @@
     return weight_ref[:, pl.ds(pl.multiple_of(part * half, half), half)]
 
 
-def own_kernel(core_ref, normed_ref, weight_ref, out_ref):
-    out_ref[...] = dot(normed_ref[...], columns(weight_ref, core_ref[0]))
-
-
-def add_kernel(mine_ref, theirs_ref, *refs):
+def own_kernel(core_ref, *refs):
+    *normed, weight_ref, out_ref = refs
+    weight = columns(weight_ref, core_ref[0])
+    out_ref[...] = dot(jnp.concatenate([part[...] for part in normed]), weight)
+
+
+def add_kernel(mine_ref, other_ref, near_ref, *refs):
     out_ref = refs[-1]
-    size = out_ref.shape[0]
-    step = pl.program_id(0)
-    first = pl.multiple_of((step + (pl.num_programs(0) if len(refs) > 1 else 0)) * size, size)
-    here = pl.ds(pl.multiple_of(step * size, size), size)
-    out_ref[...] = (mine_ref[pl.ds(first, size), :] + theirs_ref[here, :].astype(F32)).astype(BF16)
+    width = out_ref.shape[1]
+    cut = pl.ds(pl.multiple_of(pl.program_id(0) * width, width), width)
+    rows = other_ref.shape[0]
+    first = mine_ref.shape[0] - rows if len(refs) > 1 else 0
+    product = dot(other_ref[...], near_ref[:, cut])
+    out_ref[...] = (mine_ref[first : first + rows, cut] + product).astype(BF16)
 
 
 def shape(dims, dtype):
@@ -291,15 +299,15 @@
         final = step == len(ROUNDS) - 1
         got = [lax.ppermute(message, "seq", [(i, i ^ b) for i in range(count)]) for b in bits]
         if step == 0:
-            wq = pl.pallas_call(
+            wq, far = pl.pallas_call(
                 stage_kernel,
-                out_shape=shape(q_weight.shape, BF16),
-                in_specs=[VMEM, HBM],
-                out_specs=VMEM,
-                scratch_shapes=[pltpu.SemaphoreType.DMA((STAGE_COPIES,))],
+                out_shape=(shape(q_weight.shape, BF16), shape((q_width, half), BF16)),
+                in_specs=[SMEM, VMEM, HBM, HBM],
+                out_specs=(VMEM, VMEM),
+                scratch_shapes=[pltpu.SemaphoreType.DMA((2 * STAGE_COPIES,))],
                 compiler_params=params(2),
                 name="stage",
-            )(message, in_hbm(q_weight))
+            )(core, message, in_hbm(q_weight), in_hbm(out_weight))
         if step in INTRA_STEPS:
             (key, value), _ = lax.optimization_barrier(((key, value), message))
             query, part = intra(INTRA_STEPS.index(step), key, value)
@@ -317,42 +325,42 @@
             name="combine",
         )(place, col, message, *got, *extra)
         if step == 0:
-            message, wq = lax.optimization_barrier((message, wq))
+            message, wq, far = lax.optimization_barrier((message, wq, far))
+            near = swap_head(far)
         if step in INTRA_STEPS:
             message, queries[-1] = lax.optimization_barrier((message, queries[-1]))
 
-    normed, *theirs = pl.pallas_call(
+    parts = rows // BLOCK
+    normed = pl.pallas_call(
         lambda *refs: norm_kernel(ROUNDS[-1], kv_heads, *refs),
-        out_shape=(shape((rows, q_width), BF16),) + (shape((BLOCK, half), BF16),) * (rows // BLOCK),
-        in_specs=[SMEM, SMEM] + [VMEM] * (1 + len(got) + 2 * kv_heads + 3),
-        out_specs=(VMEM,) * (1 + rows // BLOCK),
+        out_shape=(shape((BLOCK, q_width), BF16),) * parts,
+        in_specs=[SMEM] + [VMEM] * (1 + len(got) + 2 * kv_heads + 2),
+        out_specs=(VMEM,) * parts,
         compiler_params=params(16),
         name="norm",
-    )(core, place, held, *got, *queries, *intras, col, gain, out_weight)
-    received = [swap_head(part) for part in theirs]
+    )(place, held, *got, *queries, *intras, col, gain)
+    received = [swap_head(part) for part in normed]
     mine = pl.pallas_call(
         own_kernel,
         out_shape=shape((rows, half), F32),
-        in_specs=[SMEM, VMEM, VMEM],
+        in_specs=[SMEM] + [VMEM] * (parts + 1),
         out_specs=VMEM,
         compiler_params=params(16),
         name="own",
-    )(core, normed, out_weight)
+    )(core, *normed, out_weight)
     out = ()
-    for part in range(rows // BLOCK):
+    for part in range(parts):
         out = (
             pl.pallas_call(
                 add_kernel,
                 grid=(ADD_STEPS,),
                 out_shape=shape((rows, half), BF16),
-                in_specs=[VMEM, VMEM] + [HBM] * len(out),
-                out_specs=pl.BlockSpec(
-                    (BLOCK // ADD_STEPS, half), lambda i, part=part: (i + part * ADD_STEPS, 0)
-                ),
-                input_output_aliases={2: 0} if out else {},
+                in_specs=[VMEM, VMEM, VMEM] + [HBM] * len(out),
+                out_specs=pl.BlockSpec((BLOCK, half // ADD_STEPS), lambda i, part=part: (part, i)),
+                input_output_aliases={3: 0} if out else {},
                 compiler_params=params(8),
                 name=f"add_{part}",
-            )(mine, received[part], *out),
+            )(mine, received[part], near, *out),
         )
     return out[0]
 

time: 46 us -> 46.7 us (1.015)
  waiting for transfers between devices: 9.1 us -> 7.73 us
  Pallas kernels: 16.1 us -> 17.2 us
  starting transfers between devices: 20.6 us -> 21.4 us
    pallas_call x2, Pallas kernels: 1.69 us -> 3.19 us  [on_device(): pl.pallas_call(add_kernel, grid=(ADD_STEPS,), out_shape=shape((rows, half...]
    ppermute x10, waiting for transfers between devices: 8.49 us -> 7.11 us  [on_device(): lax.ppermute(message, 'seq', [(i, i ^ b) for i in range(count)])]
    pallas_call x1, Pallas kernels: 2.08 us -> 0.95 us  [on_device(): pl.pallas_call(lambda *refs: norm_kernel(ROUNDS[-1], kv_heads, *refs), ou...]
    pallas_call x1, Pallas kernels: 2.2 us -> 2.95 us  [on_device(): pl.pallas_call(stage_kernel, out_shape=(shape(q_weight.shape, BF16), shap...]
    ppermute x10, starting transfers between devices: 13.9 us -> 14.5 us  [on_device(): lax.ppermute(message, 'seq', [(i, i ^ b) for i in range(count)])]
    ppermute x3 -> x4, starting transfers between devices: 6.7 us -> 6.91 us  [swap_head(): return lax.ppermute(x, 'head', [(0, 1), (1, 0)])]
  transfers between devices with their start and end apart: 13 -> 14, of which waited for: 7 -> 6; matrix products, arithmetic and copies ran while one was open for 0% -> 0% of each run, Pallas kernels for 26% -> 31%
where the time goes in v7:
time: 46.7 us; the launch traced here: 46.5 us
  starting transfers between devices  21.4 us (46%)
  Pallas kernels  17.2 us (37%)
  waiting for transfers between devices  7.73 us (17%)
    ppermute x10, starting transfers between devices, on_device(): lax.ppermute(message, 'seq', [(i, i ^ b) for i in range(count)])  14.5 us
    ppermute x10, waiting for transfers between devices, on_device(): lax.ppermute(message, 'seq', [(i, i ^ b) for i in range(count)])  7.11 us
    ppermute x4, starting transfers between devices, swap_head(): return lax.ppermute(x, 'head', [(0, 1), (1, 0)])  6.91 us
    pallas_call x2, Pallas kernels, intra(): pl.pallas_call(intra_kernel, out_shape=(shape((rows, group_width), BF16),...  5.54 us
    pallas_call x2, Pallas kernels, on_device(): pl.pallas_call(add_kernel, grid=(ADD_STEPS,), out_shape=shape((rows, half...  3.19 us
    pallas_call x1, Pallas kernels, on_device(): pl.pallas_call(stage_kernel, out_shape=(shape(q_weight.shape, BF16), shap...  2.95 us
    pallas_call x1, Pallas kernels, on_device(): pl.pallas_call(own_half_kernel, out_shape=(shape(tokens.shape, BF16), sha...  2.06 us
    pallas_call x1, Pallas kernels, on_device(): pl.pallas_call(own_kernel, out_shape=shape((rows, half), F32), in_specs=[...  1.25 us
  transfers between devices with their start and end apart: 14, of which 6 were waited for; matrix products, arithmetic and copies ran while one was open for 0% of the time, Pallas kernels for 31%

profile of v7, /device:TPU:1, one launch (start us, length us, event | category | flops | bytes accessed | tf_op | source)
XLA Modules:
  0.0 46.5 jit_solution(3812429061685261119)
XLA Ops:
  0.0 3.2 %collective-permute-start = (bf16[512,1024]{1,0:T(8,128)(2,1)}, bf16[512,1024]{1,0:T(8,128)(2,1)S(1)}, u32[]{:S(2)}, u32[]{:S(2)}) collective-permute-start(bf16[512,1024]{1,0:T(8,128)(2,1)} %own_hbm.1), channel_id=1, source_target_pairs={{0,1},{1,0},{2,3},{3,2},{4,5},{5,4},{6,7},{7,6},{8,9},{9,8},{10,11... | collective-permute-start | bytes 3145736 | tf_op jit(solution)/shard_map/ppermute | solution.py:230
  3.2 2.1 %own_half.1 = (bf16[512,1024]{1,0:T(8,128)(2,1)S(1)}, bf16[2048,256]{1,0:T(8,128)(2,1)S(1)}, bf16[2048,256]{1,0:T(8,128)(2,1)S(1)}, f32[512,256]{1,0:T(8,128)S(1...) custom-call(s32[1]{0:T(128)} %bitcast.core_ref, s32[1,512]{1,0:T(1,128)} %bitcast.5, ...), custom_call_target="tpu_custom_call" | custom-call | tf_op jit(solution)/shard_map/own_half/pallas_call | solution.py:245
  5.3 0.4 collective-permute-done.other_ref
  5.7 1.0 %key_value.1 = (bf16[512,256]{1,0:T(8,128)(2,1)S(1)}, bf16[512,256]{1,0:T(8,128)(2,1)S(1)}, bf16[272,128]{1,0:T(8,128)(2,1)S(1)}) custom-call(s32[1]{0:T(128)} %bitcast.core_ref, bf16[512,1024]{1,0:T(8,128)(2,1)S(1)} %collective-permute-done.other_ref, f32[512,256]{1,0:T(8,128)S(1)} %get-tuple-element.41.k_part_ref, ...), custom_call_target="tpu_custom_call" | custom-call | tf_op jit(solution)/shard_map/key_value/pallas_call | solution.py:263
  6.8 2.7 %collective-permute-start.3 = (bf16[272,128]{1,0:T(8,128)(2,1)S(1)}, bf16[272,128]{1,0:T(8,128)(2,1)S(1)}, u32[]{:S(2)}, u32[]{:S(2)}) collective-permute-start(bf16[272,128]{1,0:T(8,128)(2,1)S(1)} %get-tuple-element.45.refs_2_.after_ref), channel_id=1, source_target_pairs={{0,6},{2,4},{4,2},{6,0},{8,14},{10,12},{12,10},{14,8},{16,22},{18,... | collective-permute-start | bytes 208904 | tf_op jit(solution)/shard_map/ppermute | solution.py:300
  9.5 0.9 %collective-permute-start.1 = (bf16[272,128]{1,0:T(8,128)(2,1)S(1)}, bf16[272,128]{1,0:T(8,128)(2,1)S(1)}, u32[]{:S(2)}, u32[]{:S(2)}) collective-permute-start(bf16[272,128]{1,0:T(8,128)(2,1)S(1)} %get-tuple-element.45.refs_2_.after_ref), channel_id=1, source_target_pairs={{0,2},{2,0},{4,6},{6,4},{8,10},{10,8},{12,14},{14,12},{16,18},{18,... | collective-permute-start | bytes 208904 | tf_op jit(solution)/shard_map/ppermute | solution.py:300
  10.4 3.0 %stage.1 = (bf16[2048,1024]{1,0:T(8,128)(2,1)S(1)}, bf16[1024,1024]{1,0:T(8,128)(2,1)S(1)}) custom-call(s32[1]{0:T(128)} %bitcast.core_ref, bf16[272,128]{1,0:T(8,128)(2,1)S(1)} %get-tuple-element.45.refs_2_.after_ref, bf16[2048,1024]{1,0:T(8,128)(2,1)} %wq_hbm.1, bf16[1024,2048]{1,0:T(8,128)(2,1)} %refs_2_.1), custom_call_target="tpu_custom_call" | custom-call | tf_op jit(solution)/shard_map/stage/pallas_call | solution.py:302
  13.4 2.4 %collective-permute-done.2.refs_4_ = bf16[272,128]{1,0:T(8,128)(2,1)S(1)} collective-permute-done((bf16[272,128]{1,0:T(8,128)(2,1)S(1)}, bf16[272,128]{1,0:T(8,128)(2,1)S(1)}, u32[]{:S(2)}, u32[]{:S(2)}) %collective-permute-start.2) | collective-permute-done | bytes 69664 | tf_op jit(solution)/shard_map/ppermute | solution.py:300
  15.8 0.1 combine.3
  15.8 0.6 %collective-permute-start.12 = (bf16[1024,1024]{1,0:T(8,128)(2,1)S(1)}, bf16[1024,1024]{1,0:T(8,128)(2,1)S(1)}, u32[]{:S(2)}, u32[]{:S(2)}) collective-permute-start(bf16[1024,1024]{1,0:T(8,128)(2,1)S(1)} %get-tuple-element.74), channel_id=1, source_target_pairs={{0,1},{1,0},{2,3},{3,2},{4,5},{5,4},{6,7},{7,6},{8,9},{9,8},{10,11... | collective-permute-start | bytes 6291464 | tf_op jit(solution)/shard_map/ppermute | solution.py:230
  16.5 3.4 %collective-permute-start.4 = (bf16[272,128]{1,0:T(8,128)(2,1)S(1)}, bf16[272,128]{1,0:T(8,128)(2,1)S(1)}, u32[]{:S(2)}, u32[]{:S(2)}) collective-permute-start(bf16[272,128]{1,0:T(8,128)(2,1)S(1)} %get-tuple-element.49.refs_2_), channel_id=1, source_target_pairs={{0,12},{2,14},{4,8},{6,10},{8,4},{10,6},{12,0},{14,2},{16,28},{18,... | collective-permute-start | bytes 208904 | tf_op jit(solution)/shard_map/ppermute | solution.py:300
  19.9 2.8 %intra_0.1 = (bf16[512,512]{1,0:T(8,128)(2,1)S(1)}, f32[512,512]{1,0:T(8,128)S(1)}) custom-call(s32[1]{0:T(128)} %bitcast.core_ref, bf16[512,1024]{1,0:T(8,128)(2,1)S(1)} %get-tuple-element.52.own_ref, bf16[512,1024]{1,0:T(8,128)(2,1)S(1)} %collective-permute-done.other_ref, bf16[2048,1024]{1,0:T(8,128)(2,1)S(1)} %get-tuple-element.53.wq_ref, ...), custom_call_target="tpu_custom_call" | custom-call | tf_op jit(solution)/shard_map/intra_0/pallas_call | solution.py:277
  22.6 0.0 copy-start.1
  22.7 0.0 collective-permute-done.4.refs_3_
  22.7 0.0 copy-start
  22.7 2.8 %collective-permute-start.7 = (bf16[272,128]{1,0:T(8,128)(2,1)S(1)}, bf16[272,128]{1,0:T(8,128)(2,1)S(1)}, u32[]{:S(2)}, u32[]{:S(2)}) collective-permute-start(bf16[272,128]{1,0:T(8,128)(2,1)S(1)} %get-tuple-element.60.refs_2_), channel_id=1, source_target_pairs={{0,32},{2,34},{4,36},{6,38},{8,40},{10,42},{12,44},{14,46},{16,48}... | collective-permute-start | bytes 208904 | tf_op jit(solution)/shard_map/ppermute | solution.py:300
  25.6 0.9 %collective-permute-start.6 = (bf16[272,128]{1,0:T(8,128)(2,1)S(1)}, bf16[272,128]{1,0:T(8,128)(2,1)S(1)}, u32[]{:S(2)}, u32[]{:S(2)}) collective-permute-start(bf16[272,128]{1,0:T(8,128)(2,1)S(1)} %get-tuple-element.60.refs_2_), channel_id=1, source_target_pairs={{0,48},{2,50},{4,52},{6,54},{8,56},{10,58},{12,60},{14,62},{16,32}... | collective-permute-start | bytes 208904 | tf_op jit(solution)/shard_map/ppermute | solution.py:300
  26.4 2.8 %intra_1.1 = (bf16[512,512]{1,0:T(8,128)(2,1)S(1)}, f32[512,512]{1,0:T(8,128)S(1)}) custom-call(s32[1]{0:T(128)} %bitcast.core_ref, bf16[512,1024]{1,0:T(8,128)(2,1)S(1)} %get-tuple-element.52.own_ref, bf16[512,1024]{1,0:T(8,128)(2,1)S(1)} %collective-permute-done.other_ref, bf16[2048,1024]{1,0:T(8,128)(2,1)S(1)} %get-tuple-element.53.wq_ref, ...), custom_call_target="tpu_custom_call" | custom-call | tf_op jit(solution)/shard_map/intra_1/pallas_call | solution.py:277
  29.2 0.7 %collective-permute-done.6.refs_4_ = bf16[272,128]{1,0:T(8,128)(2,1)S(1)} collective-permute-done((bf16[272,128]{1,0:T(8,128)(2,1)S(1)}, bf16[272,128]{1,0:T(8,128)(2,1)S(1)}, u32[]{:S(2)}, u32[]{:S(2)}) %collective-permute-start.6) | collective-permute-done | bytes 69664 | tf_op jit(solution)/shard_map/ppermute | solution.py:300
  29.9 0.1 combine.5
  30.0 3.0 %collective-permute-start.10 = (bf16[272,128]{1,0:T(8,128)(2,1)S(1)}, bf16[272,128]{1,0:T(8,128)(2,1)S(1)}, u32[]{:S(2)}, u32[]{:S(2)}) collective-permute-start(bf16[272,128]{1,0:T(8,128)(2,1)S(1)} %get-tuple-element.67), channel_id=1, source_target_pairs={{0,128},{2,130},{4,132},{6,134},{8,136},{10,138},{12,140},{14,142}... | collective-permute-start | bytes 208904 | tf_op jit(solution)/shard_map/ppermute | solution.py:300
  33.0 0.8 %collective-permute-start.9 = (bf16[272,128]{1,0:T(8,128)(2,1)S(1)}, bf16[272,128]{1,0:T(8,128)(2,1)S(1)}, u32[]{:S(2)}, u32[]{:S(2)}) collective-permute-start(bf16[272,128]{1,0:T(8,128)(2,1)S(1)} %get-tuple-element.67), channel_id=1, source_target_pairs={{0,192},{2,194},{4,196},{6,198},{8,200},{10,202},{12,204},{14,206}... | collective-permute-start | bytes 208904 | tf_op jit(solution)/shard_map/ppermute | solution.py:300
  33.8 0.0 collective-permute-start.8
  33.8 1.0 %collective-permute-done.10.refs_4_ = bf16[272,128]{1,0:T(8,128)(2,1)S(1)} collective-permute-done((bf16[272,128]{1,0:T(8,128)(2,1)S(1)}, bf16[272,128]{1,0:T(8,128)(2,1)S(1)}, u32[]{:S(2)}, u32[]{:S(2)}) %collective-permute-start.10) | collective-permute-done | bytes 69664 | tf_op jit(solution)/shard_map/ppermute | solution.py:300
  34.8 3.0 %collective-permute-done.9.refs_3_ = bf16[272,128]{1,0:T(8,128)(2,1)S(1)} collective-permute-done((bf16[272,128]{1,0:T(8,128)(2,1)S(1)}, bf16[272,128]{1,0:T(8,128)(2,1)S(1)}, u32[]{:S(2)}, u32[]{:S(2)}) %collective-permute-start.9) | collective-permute-done | bytes 69664 | tf_op jit(solution)/shard_map/ppermute | solution.py:300
  37.8 1.0 %norm.1 = (bf16[256,1024]{1,0:T(8,128)(2,1)S(1)}, bf16[256,1024]{1,0:T(8,128)(2,1)S(1)}) custom-call(s32[1]{0:T(128)} %bitcast.1.refs_0_, f32[256,128]{1,0:T(8,128)S(1)} %get-tuple-element.62.refs_1_, bf16[272,128]{1,0:T(8,128)(2,1)S(1)} %collective-permute-done.8.refs_2_, bf16[272,128]{1,0:T(8,128)(2,1)S(1)} %collective-permute-done.9.refs_3_, ...), custom_call_target="tpu_custom_call" | custom-call | tf_op jit(solution)/shard_map/norm/pallas_call | solution.py:334
  38.8 2.9 %collective-permute-start.13 = (bf16[256,1024]{1,0:T(8,128)(2,1)S(1)}, bf16[256,1024]{1,0:T(8,128)(2,1)S(1)}, u32[]{:S(2)}, u32[]{:S(2)}) collective-permute-start(bf16[256,1024]{1,0:T(8,128)(2,1)S(1)} %get-tuple-element.72.refs_0_), channel_id=1, source_target_pairs={{0,1},{1,0},{2,3},{3,2},{4,5},{5,4},{6,7},{7,6},{8,9},{9,8},{10,11... | collective-permute-start | bytes 1572872 | tf_op jit(solution)/shard_map/ppermute | solution.py:230
  41.7 0.1 collective-permute-start.11
  41.8 1.3 %own.1.mine_ref = f32[512,1024]{1,0:T(8,128)S(1)} custom-call(s32[1]{0:T(128)} %bitcast.core_ref, bf16[256,1024]{1,0:T(8,128)(2,1)S(1)} %get-tuple-element.72.refs_0_, bf16[256,1024]{1,0:T(8,128)(2,1)S(1)} %get-tuple-element.73.refs_1_, bf16[1024,2048]{1,0:T(8,128)(2,1)S(1)} %copy-done), custom_call_target="tpu_custom_call" | custom-call | tf_op jit(solution)/shard_map/own/pallas_call | solution.py:343
  43.1 0.2 collective-permute-done.13.other_ref
  43.3 1.6 %add_0.1.refs_0_ = bf16[512,1024]{1,0:T(8,128)(2,1)} custom-call(f32[512,1024]{1,0:T(8,128)S(1)} %own.1.mine_ref, bf16[256,1024]{1,0:T(8,128)(2,1)S(1)} %collective-permute-done.13.other_ref, bf16[1024,1024]{1,0:T(8,128)(2,1)S(1)} %collective-permute-done.12.near_ref), custom_call_target="tpu_custom_call" | custom-call | tf_op jit(solution)/shard_map/add_0/pallas_call | solution.py:354
  44.9 1.6 %add_1.1 = bf16[512,1024]{1,0:T(8,128)(2,1)} custom-call(f32[512,1024]{1,0:T(8,128)S(1)} %own.1.mine_ref, bf16[256,1024]{1,0:T(8,128)(2,1)S(1)} %collective-permute-done.11.other_ref, bf16[1024,1024]{1,0:T(8,128)(2,1)S(1)} %collective-permute-done.12.near_ref, bf16[512,1024]{1,0:T(8,128)(2,1)} %add_0.1.refs_0_), custom_call_target="tpu_custom_call", output_to_operand_aliasing={{}: (3, {})} | custom-call | tf_op jit(solution)/shard_map/add_1/pallas_call | solution.py:354
  (12 shorter events, 0.1 us)
Async XLA Ops:
  0.0 5.7 %collective-permute-start = (bf16[512,1024]{1,0:T(8,128)(2,1)}, bf16[512,1024]{1,0:T(8,128)(2,1)S(1)}, u32[]{:S(2)}, u32[]{:S(2)}) collective-permute-start(bf16[512,1024]{1,0:T(8,128)(2,1)} %own_hbm.1), channel_id=1, source_target_pairs={{0,1},{1,0},{2,3},{3,2},{4,5},{5,4},{6,7},{7,6},{8,9},{9,8},{10,11... | collective-permute-start | bytes 3145736 | tf_op jit(solution)/shard_map/ppermute | solution.py:230
  6.8 6.6 %collective-permute-start.3 = (bf16[272,128]{1,0:T(8,128)(2,1)S(1)}, bf16[272,128]{1,0:T(8,128)(2,1)S(1)}, u32[]{:S(2)}, u32[]{:S(2)}) collective-permute-start(bf16[272,128]{1,0:T(8,128)(2,1)S(1)} %get-tuple-element.45.refs_2_.after_ref), channel_id=1, source_target_pairs={{0,6},{2,4},{4,2},{6,0},{8,14},{10,12},{12,10},{14,8},{16,22},{18,... | collective-permute-start | bytes 208904 | tf_op jit(solution)/shard_map/ppermute | solution.py:300
  9.5 6.3 %collective-permute-start.2 = (bf16[272,128]{1,0:T(8,128)(2,1)S(1)}, bf16[272,128]{1,0:T(8,128)(2,1)S(1)}, u32[]{:S(2)}, u32[]{:S(2)}) collective-permute-start(bf16[272,128]{1,0:T(8,128)(2,1)S(1)} %get-tuple-element.45.refs_2_.after_ref), channel_id=1, source_target_pairs={{0,4},{2,6},{4,0},{6,2},{8,12},{10,14},{12,8},{14,10},{16,20},{18,... | collective-permute-start | bytes 208904 | tf_op jit(solution)/shard_map/ppermute | solution.py:300
  9.5 6.3 %collective-permute-start.1 = (bf16[272,128]{1,0:T(8,128)(2,1)S(1)}, bf16[272,128]{1,0:T(8,128)(2,1)S(1)}, u32[]{:S(2)}, u32[]{:S(2)}) collective-permute-start(bf16[272,128]{1,0:T(8,128)(2,1)S(1)} %get-tuple-element.45.refs_2_.after_ref), channel_id=1, source_target_pairs={{0,2},{2,0},{4,6},{6,4},{8,10},{10,8},{12,14},{14,12},{16,18},{18,... | collective-permute-start | bytes 208904 | tf_op jit(solution)/shard_map/ppermute | solution.py:300
  15.8 27.4 %collective-permute-start.12 = (bf16[1024,1024]{1,0:T(8,128)(2,1)S(1)}, bf16[1024,1024]{1,0:T(8,128)(2,1)S(1)}, u32[]{:S(2)}, u32[]{:S(2)}) collective-permute-start(bf16[1024,1024]{1,0:T(8,128)(2,1)S(1)} %get-tuple-element.74), channel_id=1, source_target_pairs={{0,1},{1,0},{2,3},{3,2},{4,5},{5,4},{6,7},{7,6},{8,9},{9,8},{10,11... | collective-permute-start | bytes 6291464 | tf_op jit(solution)/shard_map/ppermute | solution.py:230
  16.5 6.2 %collective-permute-start.4 = (bf16[272,128]{1,0:T(8,128)(2,1)S(1)}, bf16[272,128]{1,0:T(8,128)(2,1)S(1)}, u32[]{:S(2)}, u32[]{:S(2)}) collective-permute-start(bf16[272,128]{1,0:T(8,128)(2,1)S(1)} %get-tuple-element.49.refs_2_), channel_id=1, source_target_pairs={{0,12},{2,14},{4,8},{6,10},{8,4},{10,6},{12,0},{14,2},{16,28},{18,... | collective-permute-start | bytes 208904 | tf_op jit(solution)/shard_map/ppermute | solution.py:300
  22.6 15.2 %copy-start.1 = (f32[1024]{0:T(1024)S(1)}, f32[1024]{0:T(1024)}, u32[]{:S(2)}) copy-start(f32[1024]{0:T(1024)} %param.11) | copy-start | bytes 12292
  22.7 19.1 %copy-start = (bf16[1024,2048]{1,0:T(8,128)(2,1)S(1)}, bf16[1024,2048]{1,0:T(8,128)(2,1)}, u32[]{:S(2)}) copy-start(bf16[1024,2048]{1,0:T(8,128)(2,1)} %refs_2_.1) | copy-start | bytes 12582916
  22.7 6.5 %collective-permute-start.7 = (bf16[272,128]{1,0:T(8,128)(2,1)S(1)}, bf16[272,128]{1,0:T(8,128)(2,1)S(1)}, u32[]{:S(2)}, u32[]{:S(2)}) collective-permute-start(bf16[272,128]{1,0:T(8,128)(2,1)S(1)} %get-tuple-element.60.refs_2_), channel_id=1, source_target_pairs={{0,32},{2,34},{4,36},{6,38},{8,40},{10,42},{12,44},{14,46},{16,48}... | collective-permute-start | bytes 208904 | tf_op jit(solution)/shard_map/ppermute | solution.py:300
  25.6 4.4 %collective-permute-start.6 = (bf16[272,128]{1,0:T(8,128)(2,1)S(1)}, bf16[272,128]{1,0:T(8,128)(2,1)S(1)}, u32[]{:S(2)}, u32[]{:S(2)}) collective-permute-start(bf16[272,128]{1,0:T(8,128)(2,1)S(1)} %get-tuple-element.60.refs_2_), channel_id=1, source_target_pairs={{0,48},{2,50},{4,52},{6,54},{8,56},{10,58},{12,60},{14,62},{16,32}... | collective-permute-start | bytes 208904 | tf_op jit(solution)/shard_map/ppermute | solution.py:300
  26.4 3.5 %collective-permute-start.5 = (bf16[272,128]{1,0:T(8,128)(2,1)S(1)}, bf16[272,128]{1,0:T(8,128)(2,1)S(1)}, u32[]{:S(2)}, u32[]{:S(2)}) collective-permute-start(bf16[272,128]{1,0:T(8,128)(2,1)S(1)} %get-tuple-element.60.refs_2_), channel_id=1, source_target_pairs={{0,16},{2,18},{4,20},{6,22},{8,24},{10,26},{12,28},{14,30},{16,0},... | collective-permute-start | bytes 208904 | tf_op jit(solution)/shard_map/ppermute | solution.py:300
  30.0 4.8 %collective-permute-start.10 = (bf16[272,128]{1,0:T(8,128)(2,1)S(1)}, bf16[272,128]{1,0:T(8,128)(2,1)S(1)}, u32[]{:S(2)}, u32[]{:S(2)}) collective-permute-start(bf16[272,128]{1,0:T(8,128)(2,1)S(1)} %get-tuple-element.67), channel_id=1, source_target_pairs={{0,128},{2,130},{4,132},{6,134},{8,136},{10,138},{12,140},{14,142}... | collective-permute-start | bytes 208904 | tf_op jit(solution)/shard_map/ppermute | solution.py:300
  33.0 4.8 %collective-permute-start.9 = (bf16[272,128]{1,0:T(8,128)(2,1)S(1)}, bf16[272,128]{1,0:T(8,128)(2,1)S(1)}, u32[]{:S(2)}, u32[]{:S(2)}) collective-permute-start(bf16[272,128]{1,0:T(8,128)(2,1)S(1)} %get-tuple-element.67), channel_id=1, source_target_pairs={{0,192},{2,194},{4,196},{6,198},{8,200},{10,202},{12,204},{14,206}... | collective-permute-start | bytes 208904 | tf_op jit(solution)/shard_map/ppermute | solution.py:300
  33.8 4.0 %collective-permute-start.8 = (bf16[272,128]{1,0:T(8,128)(2,1)S(1)}, bf16[272,128]{1,0:T(8,128)(2,1)S(1)}, u32[]{:S(2)}, u32[]{:S(2)}) collective-permute-start(bf16[272,128]{1,0:T(8,128)(2,1)S(1)} %get-tuple-element.67), channel_id=1, source_target_pairs={{0,64},{2,66},{4,68},{6,70},{8,72},{10,74},{12,76},{14,78},{16,80}... | collective-permute-start | bytes 208904 | tf_op jit(solution)/shard_map/ppermute | solution.py:300
  38.8 4.5 %collective-permute-start.13 = (bf16[256,1024]{1,0:T(8,128)(2,1)S(1)}, bf16[256,1024]{1,0:T(8,128)(2,1)S(1)}, u32[]{:S(2)}, u32[]{:S(2)}) collective-permute-start(bf16[256,1024]{1,0:T(8,128)(2,1)S(1)} %get-tuple-element.72.refs_0_), channel_id=1, source_target_pairs={{0,1},{1,0},{2,3},{3,2},{4,5},{5,4},{6,7},{7,6},{8,9},{9,8},{10,11... | collective-permute-start | bytes 1572872 | tf_op jit(solution)/shard_map/ppermute | solution.py:230
  41.7 3.1 %collective-permute-start.11 = (bf16[256,1024]{1,0:T(8,128)(2,1)S(1)}, bf16[256,1024]{1,0:T(8,128)(2,1)S(1)}, u32[]{:S(2)}, u32[]{:S(2)}) collective-permute-start(bf16[256,1024]{1,0:T(8,128)(2,1)S(1)} %get-tuple-element.73.refs_1_), channel_id=1, source_target_pairs={{0,1},{1,0},{2,3},{3,2},{4,5},{5,4},{6,7},{7,6},{8,9},{9,8},{10,11... | collective-permute-start | bytes 1572872 | tf_op jit(solution)/shard_map/ppermute | solution.py:230

commit v8 on v6

--- a/solution.py
+++ b/solution.py
@@ -8,6 +8,7 @@
 HEAD = 128
 ID_ROWS = 16
 BLOCK = 256
+NORM_BLOCK = 512
 ROUNDS = ((1, 2, 3), (6,), (8, 24, 16), (32, 96, 64))
 INTRA_STEPS = (1, 2)
 CHUNKS = 2
@@ -177,8 +178,8 @@
     queries, intras, refs = refs[:groups], refs[groups : 2 * groups], refs[2 * groups :]
     col_ref, gain_ref, weight_ref, normed_ref, *theirs = refs
     incoming = incoming_of(bits, place_ref, col_ref, held_ref, got)
-    for start in range(0, col_ref.shape[0], BLOCK):
-        here = slice(start, start + BLOCK)
+    for start in range(0, col_ref.shape[0], NORM_BLOCK):
+        here = slice(start, start + NORM_BLOCK)
         joins = col_ref[here, :] == col_ref[:1, :]
         for k in range(groups):
             width = queries[k].shape[1]
@@ -189,7 +190,10 @@
                 combined = intras[k][here, cut] + jnp.where(joins, carried, 0.0)
                 scale = lax.rsqrt(jnp.mean(combined * combined, axis=-1, keepdims=True) + EPSILON)
                 normed_ref[here, out] = (combined * scale * gain_ref[:1, out]).astype(BF16)
-        theirs[start // BLOCK][...] = dot(normed_ref[here, :], columns(weight_ref, 1 - core_ref[0])).astype(BF16)
+    product = dot(normed_ref[...], columns(weight_ref, 1 - core_ref[0])).astype(BF16)
+    size = theirs[0].shape[0]
+    for i, part in enumerate(theirs):
+        part[...] = product[i * size : (i + 1) * size, :]
 
 
 def columns(weight_ref, part):

time: 46 us -> 45.8 us (level)
  no operation moved by 1% of the time
where the time goes in v8:
time: 45.8 us; the launch traced here: 45.7 us
  starting transfers between devices  20.6 us (45%)
  Pallas kernels  15.8 us (34%)
  waiting for transfers between devices  9.1 us (20%)
    ppermute x10, starting transfers between devices, on_device(): lax.ppermute(message, 'seq', [(i, i ^ b) for i in range(count)])  13.9 us
    ppermute x10, waiting for transfers between devices, on_device(): lax.ppermute(message, 'seq', [(i, i ^ b) for i in range(count)])  8.49 us
    ppermute x3, starting transfers between devices, swap_head(): return lax.ppermute(x, 'head', [(0, 1), (1, 0)])  6.71 us
    pallas_call x2, Pallas kernels, intra(): pl.pallas_call(intra_kernel, out_shape=(shape((rows, group_width), BF16),...  5.53 us
    pallas_call x1, Pallas kernels, on_device(): pl.pallas_call(stage_kernel, out_shape=shape(q_weight.shape, BF16), in_sp...  2.2 us
    pallas_call x1, Pallas kernels, on_device(): pl.pallas_call(own_half_kernel, out_shape=(shape(tokens.shape, BF16), sha...  2.06 us
    pallas_call x1, Pallas kernels, on_device(): pl.pallas_call(lambda *refs: norm_kernel(ROUNDS[-1], kv_heads, *refs), ou...  1.81 us
    pallas_call x2, Pallas kernels, on_device(): pl.pallas_call(add_kernel, grid=(ADD_STEPS,), out_shape=shape((rows, half...  1.69 us
  transfers between devices with their start and end apart: 13, of which 7 were waited for; matrix products, arithmetic and copies ran while one was open for 0% of the time, Pallas kernels for 26%

profile of v8, /device:TPU:1, one launch (start us, length us, event | category | flops | bytes accessed | tf_op | source)
XLA Modules:
  0.0 45.7 jit_solution(2538669058339892789)
XLA Ops:
  0.0 3.2 %collective-permute-start = (bf16[512,1024]{1,0:T(8,128)(2,1)}, bf16[512,1024]{1,0:T(8,128)(2,1)S(1)}, u32[]{:S(2)}, u32[]{:S(2)}) collective-permute-start(bf16[512,1024]{1,0:T(8,128)(2,1)} %own_hbm.1), channel_id=1, source_target_pairs={{0,1},{1,0},{2,3},{3,2},{4,5},{5,4},{6,7},{7,6},{8,9},{9,8},{10,11... | collective-permute-start | bytes 3145736 | tf_op jit(solution)/shard_map/ppermute | solution.py:226
  3.2 2.1 %own_half.1 = (bf16[512,1024]{1,0:T(8,128)(2,1)S(1)}, bf16[2048,256]{1,0:T(8,128)(2,1)S(1)}, bf16[2048,256]{1,0:T(8,128)(2,1)S(1)}, f32[512,256]{1,0:T(8,128)S(1...) custom-call(s32[1]{0:T(128)} %bitcast.core_ref.refs_0_, s32[1,512]{1,0:T(1,128)} %bitcast.5, ...), custom_call_target="tpu_custom_call" | custom-call | tf_op jit(solution)/shard_map/own_half/pallas_call | solution.py:241
  5.3 0.4 collective-permute-done.other_ref
  5.7 1.0 %key_value.1 = (bf16[512,256]{1,0:T(8,128)(2,1)S(1)}, bf16[512,256]{1,0:T(8,128)(2,1)S(1)}, bf16[272,128]{1,0:T(8,128)(2,1)S(1)}) custom-call(s32[1]{0:T(128)} %bitcast.core_ref.refs_0_, bf16[512,1024]{1,0:T(8,128)(2,1)S(1)} %collective-permute-done.other_ref, f32[512,256]{1,0:T(8,128)S(1)} %get-tuple-element.39.k_part_ref, ...), custom_call_target="tpu_custom_call" | custom-call | tf_op jit(solution)/shard_map/key_value/pallas_call | solution.py:259
  6.8 2.7 %collective-permute-start.3 = (bf16[272,128]{1,0:T(8,128)(2,1)S(1)}, bf16[272,128]{1,0:T(8,128)(2,1)S(1)}, u32[]{:S(2)}, u32[]{:S(2)}) collective-permute-start(bf16[272,128]{1,0:T(8,128)(2,1)S(1)} %get-tuple-element.43.refs_2_.after_ref), channel_id=1, source_target_pairs={{0,6},{2,4},{4,2},{6,0},{8,14},{10,12},{12,10},{14,8},{16,22},{18,... | collective-permute-start | bytes 208904 | tf_op jit(solution)/shard_map/ppermute | solution.py:296
  9.5 0.9 %collective-permute-start.1 = (bf16[272,128]{1,0:T(8,128)(2,1)S(1)}, bf16[272,128]{1,0:T(8,128)(2,1)S(1)}, u32[]{:S(2)}, u32[]{:S(2)}) collective-permute-start(bf16[272,128]{1,0:T(8,128)(2,1)S(1)} %get-tuple-element.43.refs_2_.after_ref), channel_id=1, source_target_pairs={{0,2},{2,0},{4,6},{6,4},{8,10},{10,8},{12,14},{14,12},{16,18},{18,... | collective-permute-start | bytes 208904 | tf_op jit(solution)/shard_map/ppermute | solution.py:296
  10.4 2.2 %stage.1.wq_ref = bf16[2048,1024]{1,0:T(8,128)(2,1)S(1)} custom-call(bf16[272,128]{1,0:T(8,128)(2,1)S(1)} %get-tuple-element.43.refs_2_.after_ref, bf16[2048,1024]{1,0:T(8,128)(2,1)} %weight_hbm.1), custom_call_target="tpu_custom_call" | custom-call | tf_op jit(solution)/shard_map/stage/pallas_call | solution.py:298
  12.6 3.1 %collective-permute-done.2.refs_4_ = bf16[272,128]{1,0:T(8,128)(2,1)S(1)} collective-permute-done((bf16[272,128]{1,0:T(8,128)(2,1)S(1)}, bf16[272,128]{1,0:T(8,128)(2,1)S(1)}, u32[]{:S(2)}, u32[]{:S(2)}) %collective-permute-start.2) | collective-permute-done | bytes 69664 | tf_op jit(solution)/shard_map/ppermute | solution.py:296
  15.7 0.0 collective-permute-done.1.refs_3_
  15.8 0.1 combine.3
  15.8 2.8 %collective-permute-start.4 = (bf16[272,128]{1,0:T(8,128)(2,1)S(1)}, bf16[272,128]{1,0:T(8,128)(2,1)S(1)}, u32[]{:S(2)}, u32[]{:S(2)}) collective-permute-start(bf16[272,128]{1,0:T(8,128)(2,1)S(1)} %get-tuple-element.45.refs_2_), channel_id=1, source_target_pairs={{0,12},{2,14},{4,8},{6,10},{8,4},{10,6},{12,0},{14,2},{16,28},{18,... | collective-permute-start | bytes 208904 | tf_op jit(solution)/shard_map/ppermute | solution.py:296
  18.6 2.8 %intra_0.1 = (bf16[512,512]{1,0:T(8,128)(2,1)S(1)}, f32[512,512]{1,0:T(8,128)S(1)}) custom-call(s32[1]{0:T(128)} %bitcast.core_ref.refs_0_, bf16[512,1024]{1,0:T(8,128)(2,1)S(1)} %get-tuple-element.48.own_ref, bf16[512,1024]{1,0:T(8,128)(2,1)S(1)} %collective-permute-done.other_ref, bf16[2048,1024]{1,0:T(8,128)(2,1)S(1)} %stage.1.wq_ref, ...), custom_call_target="tpu_custom_call" | custom-call | tf_op jit(solution)/shard_map/intra_0/pallas_call | solution.py:273
  21.4 0.0 copy-start
  21.4 0.0 copy-start.1
  21.5 2.8 %collective-permute-start.7 = (bf16[272,128]{1,0:T(8,128)(2,1)S(1)}, bf16[272,128]{1,0:T(8,128)(2,1)S(1)}, u32[]{:S(2)}, u32[]{:S(2)}) collective-permute-start(bf16[272,128]{1,0:T(8,128)(2,1)S(1)} %get-tuple-element.56.refs_2_), channel_id=1, source_target_pairs={{0,32},{2,34},{4,36},{6,38},{8,40},{10,42},{12,44},{14,46},{16,48}... | collective-permute-start | bytes 208904 | tf_op jit(solution)/shard_map/ppermute | solution.py:296
  24.3 0.9 %collective-permute-start.6 = (bf16[272,128]{1,0:T(8,128)(2,1)S(1)}, bf16[272,128]{1,0:T(8,128)(2,1)S(1)}, u32[]{:S(2)}, u32[]{:S(2)}) collective-permute-start(bf16[272,128]{1,0:T(8,128)(2,1)S(1)} %get-tuple-element.56.refs_2_), channel_id=1, source_target_pairs={{0,48},{2,50},{4,52},{6,54},{8,56},{10,58},{12,60},{14,62},{16,32}... | collective-permute-start | bytes 208904 | tf_op jit(solution)/shard_map/ppermute | solution.py:296
  25.2 2.8 %intra_1.1 = (bf16[512,512]{1,0:T(8,128)(2,1)S(1)}, f32[512,512]{1,0:T(8,128)S(1)}) custom-call(s32[1]{0:T(128)} %bitcast.core_ref.refs_0_, bf16[512,1024]{1,0:T(8,128)(2,1)S(1)} %get-tuple-element.48.own_ref, bf16[512,1024]{1,0:T(8,128)(2,1)S(1)} %collective-permute-done.other_ref, bf16[2048,1024]{1,0:T(8,128)(2,1)S(1)} %stage.1.wq_ref, ...), custom_call_target="tpu_custom_call" | custom-call | tf_op jit(solution)/shard_map/intra_1/pallas_call | solution.py:273
  28.0 1.0 %collective-permute-done.6.refs_4_ = bf16[272,128]{1,0:T(8,128)(2,1)S(1)} collective-permute-done((bf16[272,128]{1,0:T(8,128)(2,1)S(1)}, bf16[272,128]{1,0:T(8,128)(2,1)S(1)}, u32[]{:S(2)}, u32[]{:S(2)}) %collective-permute-start.6) | collective-permute-done | bytes 69664 | tf_op jit(solution)/shard_map/ppermute | solution.py:296
  28.9 0.1 collective-permute-done.5.refs_3_
  29.0 0.1 combine.5
  29.1 3.0 %collective-permute-start.10 = (bf16[272,128]{1,0:T(8,128)(2,1)S(1)}, bf16[272,128]{1,0:T(8,128)(2,1)S(1)}, u32[]{:S(2)}, u32[]{:S(2)}) collective-permute-start(bf16[272,128]{1,0:T(8,128)(2,1)S(1)} %get-tuple-element.63), channel_id=1, source_target_pairs={{0,128},{2,130},{4,132},{6,134},{8,136},{10,138},{12,140},{14,142}... | collective-permute-start | bytes 208904 | tf_op jit(solution)/shard_map/ppermute | solution.py:296
  32.1 0.8 %collective-permute-start.9 = (bf16[272,128]{1,0:T(8,128)(2,1)S(1)}, bf16[272,128]{1,0:T(8,128)(2,1)S(1)}, u32[]{:S(2)}, u32[]{:S(2)}) collective-permute-start(bf16[272,128]{1,0:T(8,128)(2,1)S(1)} %get-tuple-element.63), channel_id=1, source_target_pairs={{0,192},{2,194},{4,196},{6,198},{8,200},{10,202},{12,204},{14,206}... | collective-permute-start | bytes 208904 | tf_op jit(solution)/shard_map/ppermute | solution.py:296
  32.9 0.0 collective-permute-start.8
  32.9 1.0 %collective-permute-done.10.refs_5_ = bf16[272,128]{1,0:T(8,128)(2,1)S(1)} collective-permute-done((bf16[272,128]{1,0:T(8,128)(2,1)S(1)}, bf16[272,128]{1,0:T(8,128)(2,1)S(1)}, u32[]{:S(2)}, u32[]{:S(2)}) %collective-permute-start.10) | collective-permute-done | bytes 69664 | tf_op jit(solution)/shard_map/ppermute | solution.py:296
  33.9 3.4 %collective-permute-done.9.refs_4_ = bf16[272,128]{1,0:T(8,128)(2,1)S(1)} collective-permute-done((bf16[272,128]{1,0:T(8,128)(2,1)S(1)}, bf16[272,128]{1,0:T(8,128)(2,1)S(1)}, u32[]{:S(2)}, u32[]{:S(2)}) %collective-permute-start.9) | collective-permute-done | bytes 69664 | tf_op jit(solution)/shard_map/ppermute | solution.py:296
  37.3 1.8 %norm.1 = (bf16[512,1024]{1,0:T(8,128)(2,1)S(1)}, bf16[256,1024]{1,0:T(8,128)(2,1)S(1)}, bf16[256,1024]{1,0:T(8,128)(2,1)S(1)}) custom-call(s32[1]{0:T(128)} %bitcast.core_ref.refs_0_, s32[1]{0:T(128)} %bitcast.1.refs_0_.refs_1_, f32[256,128]{1,0:T(8,128)S(1)} %get-tuple-element.58.refs_2_, bf16[272,128]{1,0:T(8,128)(2,1)S(1)} %collective-permute-done.8.refs_3_, ...), custom_call_target="tpu_custom_call" | custom-call | tf_op jit(solution)/shard_map/norm/pallas_call | solution.py:328
  39.1 3.4 %collective-permute-start.12 = (bf16[256,1024]{1,0:T(8,128)(2,1)S(1)}, bf16[256,1024]{1,0:T(8,128)(2,1)S(1)}, u32[]{:S(2)}, u32[]{:S(2)}) collective-permute-start(bf16[256,1024]{1,0:T(8,128)(2,1)S(1)} %get-tuple-element.70), channel_id=1, source_target_pairs={{0,1},{1,0},{2,3},{3,2},{4,5},{5,4},{6,7},{7,6},{8,9},{9,8},{10,11... | collective-permute-start | bytes 1572872 | tf_op jit(solution)/shard_map/ppermute | solution.py:226
  42.4 0.1 collective-permute-start.11
  42.5 1.3 %own.1.mine_ref = f32[512,1024]{1,0:T(8,128)S(1)} custom-call(s32[1]{0:T(128)} %bitcast.core_ref.refs_0_, bf16[512,1024]{1,0:T(8,128)(2,1)S(1)} %get-tuple-element.68.normed_ref, bf16[1024,2048]{1,0:T(8,128)(2,1)S(1)} %copy-done), custom_call_target="tpu_custom_call" | custom-call | tf_op jit(solution)/shard_map/own/pallas_call | solution.py:337
  43.8 0.2 collective-permute-done.12.theirs_ref
  44.0 0.9 %add_0.1.refs_0_ = bf16[512,1024]{1,0:T(8,128)(2,1)} custom-call(f32[512,1024]{1,0:T(8,128)S(1)} %own.1.mine_ref, bf16[256,1024]{1,0:T(8,128)(2,1)S(1)} %collective-permute-done.12.theirs_ref), custom_call_target="tpu_custom_call" | custom-call | tf_op jit(solution)/shard_map/add_0/pallas_call | solution.py:348
  44.8 0.8 %add_1.1 = bf16[512,1024]{1,0:T(8,128)(2,1)} custom-call(f32[512,1024]{1,0:T(8,128)S(1)} %own.1.mine_ref, bf16[256,1024]{1,0:T(8,128)(2,1)S(1)} %collective-permute-done.11.theirs_ref, bf16[512,1024]{1,0:T(8,128)(2,1)} %add_0.1.refs_0_), custom_call_target="tpu_custom_call", output_to_operand_aliasing={{}: (2, {})} | custom-call | tf_op jit(solution)/shard_map/add_1/pallas_call | solution.py:348
  (10 shorter events, 0.1 us)
Async XLA Ops:
  0.0 5.7 %collective-permute-start = (bf16[512,1024]{1,0:T(8,128)(2,1)}, bf16[512,1024]{1,0:T(8,128)(2,1)S(1)}, u32[]{:S(2)}, u32[]{:S(2)}) collective-permute-start(bf16[512,1024]{1,0:T(8,128)(2,1)} %own_hbm.1), channel_id=1, source_target_pairs={{0,1},{1,0},{2,3},{3,2},{4,5},{5,4},{6,7},{7,6},{8,9},{9,8},{10,11... | collective-permute-start | bytes 3145736 | tf_op jit(solution)/shard_map/ppermute | solution.py:226
  6.8 5.9 %collective-permute-start.3 = (bf16[272,128]{1,0:T(8,128)(2,1)S(1)}, bf16[272,128]{1,0:T(8,128)(2,1)S(1)}, u32[]{:S(2)}, u32[]{:S(2)}) collective-permute-start(bf16[272,128]{1,0:T(8,128)(2,1)S(1)} %get-tuple-element.43.refs_2_.after_ref), channel_id=1, source_target_pairs={{0,6},{2,4},{4,2},{6,0},{8,14},{10,12},{12,10},{14,8},{16,22},{18,... | collective-permute-start | bytes 208904 | tf_op jit(solution)/shard_map/ppermute | solution.py:296
  9.5 6.3 %collective-permute-start.2 = (bf16[272,128]{1,0:T(8,128)(2,1)S(1)}, bf16[272,128]{1,0:T(8,128)(2,1)S(1)}, u32[]{:S(2)}, u32[]{:S(2)}) collective-permute-start(bf16[272,128]{1,0:T(8,128)(2,1)S(1)} %get-tuple-element.43.refs_2_.after_ref), channel_id=1, source_target_pairs={{0,4},{2,6},{4,0},{6,2},{8,12},{10,14},{12,8},{14,10},{16,20},{18,... | collective-permute-start | bytes 208904 | tf_op jit(solution)/shard_map/ppermute | solution.py:296
  9.5 6.3 %collective-permute-start.1 = (bf16[272,128]{1,0:T(8,128)(2,1)S(1)}, bf16[272,128]{1,0:T(8,128)(2,1)S(1)}, u32[]{:S(2)}, u32[]{:S(2)}) collective-permute-start(bf16[272,128]{1,0:T(8,128)(2,1)S(1)} %get-tuple-element.43.refs_2_.after_ref), channel_id=1, source_target_pairs={{0,2},{2,0},{4,6},{6,4},{8,10},{10,8},{12,14},{14,12},{16,18},{18,... | collective-permute-start | bytes 208904 | tf_op jit(solution)/shard_map/ppermute | solution.py:296
  15.8 5.6 %collective-permute-start.4 = (bf16[272,128]{1,0:T(8,128)(2,1)S(1)}, bf16[272,128]{1,0:T(8,128)(2,1)S(1)}, u32[]{:S(2)}, u32[]{:S(2)}) collective-permute-start(bf16[272,128]{1,0:T(8,128)(2,1)S(1)} %get-tuple-element.45.refs_2_), channel_id=1, source_target_pairs={{0,12},{2,14},{4,8},{6,10},{8,4},{10,6},{12,0},{14,2},{16,28},{18,... | collective-permute-start | bytes 208904 | tf_op jit(solution)/shard_map/ppermute | solution.py:296
  21.4 15.8 %copy-start = (bf16[1024,2048]{1,0:T(8,128)(2,1)S(1)}, bf16[1024,2048]{1,0:T(8,128)(2,1)}, u32[]{:S(2)}) copy-start(bf16[1024,2048]{1,0:T(8,128)(2,1)} %weight_ref.1) | copy-start | bytes 12582916
  21.4 15.8 %copy-start.1 = (f32[1024]{0:T(1024)S(1)}, f32[1024]{0:T(1024)}, u32[]{:S(2)}) copy-start(f32[1024]{0:T(1024)} %param.11) | copy-start | bytes 12292
  21.5 6.5 %collective-permute-start.7 = (bf16[272,128]{1,0:T(8,128)(2,1)S(1)}, bf16[272,128]{1,0:T(8,128)(2,1)S(1)}, u32[]{:S(2)}, u32[]{:S(2)}) collective-permute-start(bf16[272,128]{1,0:T(8,128)(2,1)S(1)} %get-tuple-element.56.refs_2_), channel_id=1, source_target_pairs={{0,32},{2,34},{4,36},{6,38},{8,40},{10,42},{12,44},{14,46},{16,48}... | collective-permute-start | bytes 208904 | tf_op jit(solution)/shard_map/ppermute | solution.py:296
  24.3 4.6 %collective-permute-start.6 = (bf16[272,128]{1,0:T(8,128)(2,1)S(1)}, bf16[272,128]{1,0:T(8,128)(2,1)S(1)}, u32[]{:S(2)}, u32[]{:S(2)}) collective-permute-start(bf16[272,128]{1,0:T(8,128)(2,1)S(1)} %get-tuple-element.56.refs_2_), channel_id=1, source_target_pairs={{0,48},{2,50},{4,52},{6,54},{8,56},{10,58},{12,60},{14,62},{16,32}... | collective-permute-start | bytes 208904 | tf_op jit(solution)/shard_map/ppermute | solution.py:296
  25.2 3.8 %collective-permute-start.5 = (bf16[272,128]{1,0:T(8,128)(2,1)S(1)}, bf16[272,128]{1,0:T(8,128)(2,1)S(1)}, u32[]{:S(2)}, u32[]{:S(2)}) collective-permute-start(bf16[272,128]{1,0:T(8,128)(2,1)S(1)} %get-tuple-element.56.refs_2_), channel_id=1, source_target_pairs={{0,16},{2,18},{4,20},{6,22},{8,24},{10,26},{12,28},{14,30},{16,0},... | collective-permute-start | bytes 208904 | tf_op jit(solution)/shard_map/ppermute | solution.py:296
  29.1 4.8 %collective-permute-start.10 = (bf16[272,128]{1,0:T(8,128)(2,1)S(1)}, bf16[272,128]{1,0:T(8,128)(2,1)S(1)}, u32[]{:S(2)}, u32[]{:S(2)}) collective-permute-start(bf16[272,128]{1,0:T(8,128)(2,1)S(1)} %get-tuple-element.63), channel_id=1, source_target_pairs={{0,128},{2,130},{4,132},{6,134},{8,136},{10,138},{12,140},{14,142}... | collective-permute-start | bytes 208904 | tf_op jit(solution)/shard_map/ppermute | solution.py:296
  32.1 5.1 %collective-permute-start.9 = (bf16[272,128]{1,0:T(8,128)(2,1)S(1)}, bf16[272,128]{1,0:T(8,128)(2,1)S(1)}, u32[]{:S(2)}, u32[]{:S(2)}) collective-permute-start(bf16[272,128]{1,0:T(8,128)(2,1)S(1)} %get-tuple-element.63), channel_id=1, source_target_pairs={{0,192},{2,194},{4,196},{6,198},{8,200},{10,202},{12,204},{14,206}... | collective-permute-start | bytes 208904 | tf_op jit(solution)/shard_map/ppermute | solution.py:296
  32.9 4.3 %collective-permute-start.8 = (bf16[272,128]{1,0:T(8,128)(2,1)S(1)}, bf16[272,128]{1,0:T(8,128)(2,1)S(1)}, u32[]{:S(2)}, u32[]{:S(2)}) collective-permute-start(bf16[272,128]{1,0:T(8,128)(2,1)S(1)} %get-tuple-element.63), channel_id=1, source_target_pairs={{0,64},{2,66},{4,68},{6,70},{8,72},{10,74},{12,76},{14,78},{16,80}... | collective-permute-start | bytes 208904 | tf_op jit(solution)/shard_map/ppermute | solution.py:296
  39.1 4.9 %collective-permute-start.12 = (bf16[256,1024]{1,0:T(8,128)(2,1)S(1)}, bf16[256,1024]{1,0:T(8,128)(2,1)S(1)}, u32[]{:S(2)}, u32[]{:S(2)}) collective-permute-start(bf16[256,1024]{1,0:T(8,128)(2,1)S(1)} %get-tuple-element.70), channel_id=1, source_target_pairs={{0,1},{1,0},{2,3},{3,2},{4,5},{5,4},{6,7},{7,6},{8,9},{9,8},{10,11... | collective-permute-start | bytes 1572872 | tf_op jit(solution)/shard_map/ppermute | solution.py:226
  42.4 2.4 %collective-permute-start.11 = (bf16[256,1024]{1,0:T(8,128)(2,1)S(1)}, bf16[256,1024]{1,0:T(8,128)(2,1)S(1)}, u32[]{:S(2)}, u32[]{:S(2)}) collective-permute-start(bf16[256,1024]{1,0:T(8,128)(2,1)S(1)} %get-tuple-element.69), channel_id=1, source_target_pairs={{0,1},{1,0},{2,3},{3,2},{4,5},{5,4},{6,7},{7,6},{8,9},{9,8},{10,11... | collective-permute-start | bytes 1572872 | tf_op jit(solution)/shard_map/ppermute | solution.py:226

commit v9 on v8

--- a/solution.py
+++ b/solution.py
@@ -9,7 +9,7 @@
 ID_ROWS = 16
 BLOCK = 256
 NORM_BLOCK = 512
-ROUNDS = ((1, 2, 3), (6,), (8, 24, 16), (32, 96, 64))
+ROUNDS = ((1, 2, 3), (6,), (8, 24, 16), (32, 64, 96))
 INTRA_STEPS = (1, 2)
 CHUNKS = 2
 STAGE_COPIES = 4
@@ -293,7 +293,14 @@
     queries, intras = [], []
     for step, bits in enumerate(ROUNDS):
         final = step == len(ROUNDS) - 1
-        got = [lax.ppermute(message, "seq", [(i, i ^ b) for i in range(count)]) for b in bits]
+        got = [
+            lax.ppermute(
+                message,
+                "seq",
+                [(i, i ^ b) for i in range(count) if not (final and 4 * i >= 3 * count > 12 * (i ^ b))],
+            )
+            for b in bits
+        ]
         if step == 0:
             wq = pl.pallas_call(
                 stage_kernel,

time: 45.8 us -> 47.8 us (1.044)
  starting transfers between devices: 20.6 us -> 22.7 us
    ppermute x10, starting transfers between devices: 13.9 us -> 15.2 us  [on_device(): lax.ppermute(message, 'seq', [(i, i ^ b) for i in range(count) if not (fi...]
    ppermute x3, starting transfers between devices: 6.71 us -> 7.46 us  [swap_head(): return lax.ppermute(x, 'head', [(0, 1), (1, 0)])]
  transfers between devices with their start and end apart: 13 -> 13, of which waited for: 7 -> 7; matrix products, arithmetic and copies ran while one was open for 0% -> 0% of each run, Pallas kernels for 26% -> 25%
where the time goes in v9:
time: 47.8 us; the launch traced here: 47.7 us
  starting transfers between devices  22.7 us (47%)
  Pallas kernels  15.8 us (33%)
  waiting for transfers between devices  9.08 us (19%)
    ppermute x10, starting transfers between devices, on_device(): lax.ppermute(message, 'seq', [(i, i ^ b) for i in range(count) if not (fi...  15.2 us
    ppermute x10, waiting for transfers between devices, on_device(): lax.ppermute(message, 'seq', [(i, i ^ b) for i in range(count) if not (fi...  8.47 us
    ppermute x3, starting transfers between devices, swap_head(): return lax.ppermute(x, 'head', [(0, 1), (1, 0)])  7.46 us
    pallas_call x2, Pallas kernels, intra(): pl.pallas_call(intra_kernel, out_shape=(shape((rows, group_width), BF16),...  5.53 us
    pallas_call x1, Pallas kernels, on_device(): pl.pallas_call(stage_kernel, out_shape=shape(q_weight.shape, BF16), in_sp...  2.2 us
    pallas_call x1, Pallas kernels, on_device(): pl.pallas_call(own_half_kernel, out_shape=(shape(tokens.shape, BF16), sha...  2.06 us
    pallas_call x1, Pallas kernels, on_device(): pl.pallas_call(lambda *refs: norm_kernel(ROUNDS[-1], kv_heads, *refs), ou...  1.82 us
    pallas_call x2, Pallas kernels, on_device(): pl.pallas_call(add_kernel, grid=(ADD_STEPS,), out_shape=shape((rows, half...  1.69 us
  transfers between devices with their start and end apart: 13, of which 7 were waited for; matrix products, arithmetic and copies ran while one was open for 0% of the time, Pallas kernels for 25%

profile of v9, /device:TPU:1, one launch (start us, length us, event | category | flops | bytes accessed | tf_op | source)
XLA Modules:
  0.0 47.7 jit_solution(12805773527731148024)
XLA Ops:
  0.0 3.2 %collective-permute-start = (bf16[512,1024]{1,0:T(8,128)(2,1)}, bf16[512,1024]{1,0:T(8,128)(2,1)S(1)}, u32[]{:S(2)}, u32[]{:S(2)}) collective-permute-start(bf16[512,1024]{1,0:T(8,128)(2,1)} %own_hbm.1), channel_id=1, source_target_pairs={{0,1},{1,0},{2,3},{3,2},{4,5},{5,4},{6,7},{7,6},{8,9},{9,8},{10,11... | collective-permute-start | bytes 3145736 | tf_op jit(solution)/shard_map/ppermute | solution.py:226
  3.2 2.1 %own_half.1 = (bf16[512,1024]{1,0:T(8,128)(2,1)S(1)}, bf16[2048,256]{1,0:T(8,128)(2,1)S(1)}, bf16[2048,256]{1,0:T(8,128)(2,1)S(1)}, f32[512,256]{1,0:T(8,128)S(1...) custom-call(s32[1]{0:T(128)} %bitcast.core_ref.refs_0_, s32[1,512]{1,0:T(1,128)} %bitcast.5, ...), custom_call_target="tpu_custom_call" | custom-call | tf_op jit(solution)/shard_map/own_half/pallas_call | solution.py:241
  5.3 0.4 collective-permute-done.other_ref
  5.7 1.0 %key_value.1 = (bf16[512,256]{1,0:T(8,128)(2,1)S(1)}, bf16[512,256]{1,0:T(8,128)(2,1)S(1)}, bf16[272,128]{1,0:T(8,128)(2,1)S(1)}) custom-call(s32[1]{0:T(128)} %bitcast.core_ref.refs_0_, bf16[512,1024]{1,0:T(8,128)(2,1)S(1)} %collective-permute-done.other_ref, f32[512,256]{1,0:T(8,128)S(1)} %get-tuple-element.39.k_part_ref, ...), custom_call_target="tpu_custom_call" | custom-call | tf_op jit(solution)/shard_map/key_value/pallas_call | solution.py:259
  6.8 2.7 %collective-permute-start.3 = (bf16[272,128]{1,0:T(8,128)(2,1)S(1)}, bf16[272,128]{1,0:T(8,128)(2,1)S(1)}, u32[]{:S(2)}, u32[]{:S(2)}) collective-permute-start(bf16[272,128]{1,0:T(8,128)(2,1)S(1)} %get-tuple-element.43.refs_2_.after_ref), channel_id=1, source_target_pairs={{0,6},{2,4},{4,2},{6,0},{8,14},{10,12},{12,10},{14,8},{16,22},{18,... | collective-permute-start | bytes 208904 | tf_op jit(solution)/shard_map/ppermute | solution.py:297
  9.5 0.0 collective-permute-start.2
  9.5 0.9 %collective-permute-start.1 = (bf16[272,128]{1,0:T(8,128)(2,1)S(1)}, bf16[272,128]{1,0:T(8,128)(2,1)S(1)}, u32[]{:S(2)}, u32[]{:S(2)}) collective-permute-start(bf16[272,128]{1,0:T(8,128)(2,1)S(1)} %get-tuple-element.43.refs_2_.after_ref), channel_id=1, source_target_pairs={{0,2},{2,0},{4,6},{6,4},{8,10},{10,8},{12,14},{14,12},{16,18},{18,... | collective-permute-start | bytes 208904 | tf_op jit(solution)/shard_map/ppermute | solution.py:297
  10.4 2.2 %stage.1.wq_ref = bf16[2048,1024]{1,0:T(8,128)(2,1)S(1)} custom-call(bf16[272,128]{1,0:T(8,128)(2,1)S(1)} %get-tuple-element.43.refs_2_.after_ref, bf16[2048,1024]{1,0:T(8,128)(2,1)} %weight_hbm.1), custom_call_target="tpu_custom_call" | custom-call | tf_op jit(solution)/shard_map/stage/pallas_call | solution.py:305
  12.6 3.1 %collective-permute-done.2.refs_4_ = bf16[272,128]{1,0:T(8,128)(2,1)S(1)} collective-permute-done((bf16[272,128]{1,0:T(8,128)(2,1)S(1)}, bf16[272,128]{1,0:T(8,128)(2,1)S(1)}, u32[]{:S(2)}, u32[]{:S(2)}) %collective-permute-start.2) | collective-permute-done | bytes 69664 | tf_op jit(solution)/shard_map/ppermute | solution.py:297
  15.8 0.1 combine.3
  15.8 2.8 %collective-permute-start.4 = (bf16[272,128]{1,0:T(8,128)(2,1)S(1)}, bf16[272,128]{1,0:T(8,128)(2,1)S(1)}, u32[]{:S(2)}, u32[]{:S(2)}) collective-permute-start(bf16[272,128]{1,0:T(8,128)(2,1)S(1)} %get-tuple-element.45.refs_2_), channel_id=1, source_target_pairs={{0,12},{2,14},{4,8},{6,10},{8,4},{10,6},{12,0},{14,2},{16,28},{18,... | collective-permute-start | bytes 208904 | tf_op jit(solution)/shard_map/ppermute | solution.py:297
  18.6 2.8 %intra_0.1 = (bf16[512,512]{1,0:T(8,128)(2,1)S(1)}, f32[512,512]{1,0:T(8,128)S(1)}) custom-call(s32[1]{0:T(128)} %bitcast.core_ref.refs_0_, bf16[512,1024]{1,0:T(8,128)(2,1)S(1)} %get-tuple-element.48.own_ref, bf16[512,1024]{1,0:T(8,128)(2,1)S(1)} %collective-permute-done.other_ref, bf16[2048,1024]{1,0:T(8,128)(2,1)S(1)} %stage.1.wq_ref, ...), custom_call_target="tpu_custom_call" | custom-call | tf_op jit(solution)/shard_map/intra_0/pallas_call | solution.py:273
  21.4 0.0 copy-start
  21.4 0.0 copy-start.1
  21.5 2.8 %collective-permute-start.7 = (bf16[272,128]{1,0:T(8,128)(2,1)S(1)}, bf16[272,128]{1,0:T(8,128)(2,1)S(1)}, u32[]{:S(2)}, u32[]{:S(2)}) collective-permute-start(bf16[272,128]{1,0:T(8,128)(2,1)S(1)} %get-tuple-element.56.refs_2_), channel_id=1, source_target_pairs={{0,32},{2,34},{4,36},{6,38},{8,40},{10,42},{12,44},{14,46},{16,48}... | collective-permute-start | bytes 208904 | tf_op jit(solution)/shard_map/ppermute | solution.py:297
  24.3 0.9 %collective-permute-start.6 = (bf16[272,128]{1,0:T(8,128)(2,1)S(1)}, bf16[272,128]{1,0:T(8,128)(2,1)S(1)}, u32[]{:S(2)}, u32[]{:S(2)}) collective-permute-start(bf16[272,128]{1,0:T(8,128)(2,1)S(1)} %get-tuple-element.56.refs_2_), channel_id=1, source_target_pairs={{0,48},{2,50},{4,52},{6,54},{8,56},{10,58},{12,60},{14,62},{16,32}... | collective-permute-start | bytes 208904 | tf_op jit(solution)/shard_map/ppermute | solution.py:297
  25.2 2.8 %intra_1.1 = (bf16[512,512]{1,0:T(8,128)(2,1)S(1)}, f32[512,512]{1,0:T(8,128)S(1)}) custom-call(s32[1]{0:T(128)} %bitcast.core_ref.refs_0_, bf16[512,1024]{1,0:T(8,128)(2,1)S(1)} %get-tuple-element.48.own_ref, bf16[512,1024]{1,0:T(8,128)(2,1)S(1)} %collective-permute-done.other_ref, bf16[2048,1024]{1,0:T(8,128)(2,1)S(1)} %stage.1.wq_ref, ...), custom_call_target="tpu_custom_call" | custom-call | tf_op jit(solution)/shard_map/intra_1/pallas_call | solution.py:273
  28.0 1.0 %collective-permute-done.6.refs_4_ = bf16[272,128]{1,0:T(8,128)(2,1)S(1)} collective-permute-done((bf16[272,128]{1,0:T(8,128)(2,1)S(1)}, bf16[272,128]{1,0:T(8,128)(2,1)S(1)}, u32[]{:S(2)}, u32[]{:S(2)}) %collective-permute-start.6) | collective-permute-done | bytes 69664 | tf_op jit(solution)/shard_map/ppermute | solution.py:297
  28.9 0.1 collective-permute-done.5.refs_3_
  29.0 0.1 combine.5
  29.1 4.7 %collective-permute-start.10 = (bf16[272,128]{1,0:T(8,128)(2,1)S(1)}, bf16[272,128]{1,0:T(8,128)(2,1)S(1)}, u32[]{:S(2)}, u32[]{:S(2)}) collective-permute-start(bf16[272,128]{1,0:T(8,128)(2,1)S(1)} %get-tuple-element.63), channel_id=1, source_target_pairs={{0,192},{2,194},{4,196},{6,198},{8,200},{10,202},{12,204},{14,206}... | collective-permute-start | bytes 208904 | tf_op jit(solution)/shard_map/ppermute | solution.py:297
  33.8 0.4 collective-permute-start.9
  34.2 0.0 collective-permute-start.8
  34.2 1.3 %collective-permute-done.10.refs_5_ = bf16[272,128]{1,0:T(8,128)(2,1)S(1)} collective-permute-done((bf16[272,128]{1,0:T(8,128)(2,1)S(1)}, bf16[272,128]{1,0:T(8,128)(2,1)S(1)}, u32[]{:S(2)}, u32[]{:S(2)}) %collective-permute-start.10) | collective-permute-done | bytes 69664 | tf_op jit(solution)/shard_map/ppermute | solution.py:297
  35.5 3.0 %collective-permute-done.9.refs_4_ = bf16[272,128]{1,0:T(8,128)(2,1)S(1)} collective-permute-done((bf16[272,128]{1,0:T(8,128)(2,1)S(1)}, bf16[272,128]{1,0:T(8,128)(2,1)S(1)}, u32[]{:S(2)}, u32[]{:S(2)}) %collective-permute-start.9) | collective-permute-done | bytes 69664 | tf_op jit(solution)/shard_map/ppermute | solution.py:297
  38.5 1.8 %norm.1 = (bf16[512,1024]{1,0:T(8,128)(2,1)S(1)}, bf16[256,1024]{1,0:T(8,128)(2,1)S(1)}, bf16[256,1024]{1,0:T(8,128)(2,1)S(1)}) custom-call(s32[1]{0:T(128)} %bitcast.core_ref.refs_0_, s32[1]{0:T(128)} %bitcast.1.refs_0_.refs_1_, f32[256,128]{1,0:T(8,128)S(1)} %get-tuple-element.58.refs_2_, bf16[272,128]{1,0:T(8,128)(2,1)S(1)} %collective-permute-done.8.refs_3_, ...), custom_call_target="tpu_custom_call" | custom-call | tf_op jit(solution)/shard_map/norm/pallas_call | solution.py:335
  40.4 4.1 %collective-permute-start.12 = (bf16[256,1024]{1,0:T(8,128)(2,1)S(1)}, bf16[256,1024]{1,0:T(8,128)(2,1)S(1)}, u32[]{:S(2)}, u32[]{:S(2)}) collective-permute-start(bf16[256,1024]{1,0:T(8,128)(2,1)S(1)} %get-tuple-element.70), channel_id=1, source_target_pairs={{0,1},{1,0},{2,3},{3,2},{4,5},{5,4},{6,7},{7,6},{8,9},{9,8},{10,11... | collective-permute-start | bytes 1572872 | tf_op jit(solution)/shard_map/ppermute | solution.py:226
  44.5 0.1 collective-permute-start.11
  44.6 1.3 %own.1.mine_ref = f32[512,1024]{1,0:T(8,128)S(1)} custom-call(s32[1]{0:T(128)} %bitcast.core_ref.refs_0_, bf16[512,1024]{1,0:T(8,128)(2,1)S(1)} %get-tuple-element.68.normed_ref, bf16[1024,2048]{1,0:T(8,128)(2,1)S(1)} %copy-done), custom_call_target="tpu_custom_call" | custom-call | tf_op jit(solution)/shard_map/own/pallas_call | solution.py:344
  45.8 0.2 collective-permute-done.12.theirs_ref
  46.0 0.9 %add_0.1.refs_0_ = bf16[512,1024]{1,0:T(8,128)(2,1)} custom-call(f32[512,1024]{1,0:T(8,128)S(1)} %own.1.mine_ref, bf16[256,1024]{1,0:T(8,128)(2,1)S(1)} %collective-permute-done.12.theirs_ref), custom_call_target="tpu_custom_call" | custom-call | tf_op jit(solution)/shard_map/add_0/pallas_call | solution.py:355
  46.9 0.8 %add_1.1 = bf16[512,1024]{1,0:T(8,128)(2,1)} custom-call(f32[512,1024]{1,0:T(8,128)S(1)} %own.1.mine_ref, bf16[256,1024]{1,0:T(8,128)(2,1)S(1)} %collective-permute-done.11.theirs_ref, bf16[512,1024]{1,0:T(8,128)(2,1)} %add_0.1.refs_0_), custom_call_target="tpu_custom_call", output_to_operand_aliasing={{}: (2, {})} | custom-call | tf_op jit(solution)/shard_map/add_1/pallas_call | solution.py:355
  (10 shorter events, 0.1 us)
Async XLA Ops:
  0.0 5.7 %collective-permute-start = (bf16[512,1024]{1,0:T(8,128)(2,1)}, bf16[512,1024]{1,0:T(8,128)(2,1)S(1)}, u32[]{:S(2)}, u32[]{:S(2)}) collective-permute-start(bf16[512,1024]{1,0:T(8,128)(2,1)} %own_hbm.1), channel_id=1, source_target_pairs={{0,1},{1,0},{2,3},{3,2},{4,5},{5,4},{6,7},{7,6},{8,9},{9,8},{10,11... | collective-permute-start | bytes 3145736 | tf_op jit(solution)/shard_map/ppermute | solution.py:226
  6.8 5.9 %collective-permute-start.3 = (bf16[272,128]{1,0:T(8,128)(2,1)S(1)}, bf16[272,128]{1,0:T(8,128)(2,1)S(1)}, u32[]{:S(2)}, u32[]{:S(2)}) collective-permute-start(bf16[272,128]{1,0:T(8,128)(2,1)S(1)} %get-tuple-element.43.refs_2_.after_ref), channel_id=1, source_target_pairs={{0,6},{2,4},{4,2},{6,0},{8,14},{10,12},{12,10},{14,8},{16,22},{18,... | collective-permute-start | bytes 208904 | tf_op jit(solution)/shard_map/ppermute | solution.py:297
  9.5 6.3 %collective-permute-start.2 = (bf16[272,128]{1,0:T(8,128)(2,1)S(1)}, bf16[272,128]{1,0:T(8,128)(2,1)S(1)}, u32[]{:S(2)}, u32[]{:S(2)}) collective-permute-start(bf16[272,128]{1,0:T(8,128)(2,1)S(1)} %get-tuple-element.43.refs_2_.after_ref), channel_id=1, source_target_pairs={{0,4},{2,6},{4,0},{6,2},{8,12},{10,14},{12,8},{14,10},{16,20},{18,... | collective-permute-start | bytes 208904 | tf_op jit(solution)/shard_map/ppermute | solution.py:297
  9.5 6.3 %collective-permute-start.1 = (bf16[272,128]{1,0:T(8,128)(2,1)S(1)}, bf16[272,128]{1,0:T(8,128)(2,1)S(1)}, u32[]{:S(2)}, u32[]{:S(2)}) collective-permute-start(bf16[272,128]{1,0:T(8,128)(2,1)S(1)} %get-tuple-element.43.refs_2_.after_ref), channel_id=1, source_target_pairs={{0,2},{2,0},{4,6},{6,4},{8,10},{10,8},{12,14},{14,12},{16,18},{18,... | collective-permute-start | bytes 208904 | tf_op jit(solution)/shard_map/ppermute | solution.py:297
  15.8 5.6 %collective-permute-start.4 = (bf16[272,128]{1,0:T(8,128)(2,1)S(1)}, bf16[272,128]{1,0:T(8,128)(2,1)S(1)}, u32[]{:S(2)}, u32[]{:S(2)}) collective-permute-start(bf16[272,128]{1,0:T(8,128)(2,1)S(1)} %get-tuple-element.45.refs_2_), channel_id=1, source_target_pairs={{0,12},{2,14},{4,8},{6,10},{8,4},{10,6},{12,0},{14,2},{16,28},{18,... | collective-permute-start | bytes 208904 | tf_op jit(solution)/shard_map/ppermute | solution.py:297
  21.4 17.1 %copy-start = (bf16[1024,2048]{1,0:T(8,128)(2,1)S(1)}, bf16[1024,2048]{1,0:T(8,128)(2,1)}, u32[]{:S(2)}) copy-start(bf16[1024,2048]{1,0:T(8,128)(2,1)} %weight_ref.1) | copy-start | bytes 12582916
  21.4 17.1 %copy-start.1 = (f32[1024]{0:T(1024)S(1)}, f32[1024]{0:T(1024)}, u32[]{:S(2)}) copy-start(f32[1024]{0:T(1024)} %param.11) | copy-start | bytes 12292
  21.5 6.5 %collective-permute-start.7 = (bf16[272,128]{1,0:T(8,128)(2,1)S(1)}, bf16[272,128]{1,0:T(8,128)(2,1)S(1)}, u32[]{:S(2)}, u32[]{:S(2)}) collective-permute-start(bf16[272,128]{1,0:T(8,128)(2,1)S(1)} %get-tuple-element.56.refs_2_), channel_id=1, source_target_pairs={{0,32},{2,34},{4,36},{6,38},{8,40},{10,42},{12,44},{14,46},{16,48}... | collective-permute-start | bytes 208904 | tf_op jit(solution)/shard_map/ppermute | solution.py:297
  24.3 4.6 %collective-permute-start.6 = (bf16[272,128]{1,0:T(8,128)(2,1)S(1)}, bf16[272,128]{1,0:T(8,128)(2,1)S(1)}, u32[]{:S(2)}, u32[]{:S(2)}) collective-permute-start(bf16[272,128]{1,0:T(8,128)(2,1)S(1)} %get-tuple-element.56.refs_2_), channel_id=1, source_target_pairs={{0,48},{2,50},{4,52},{6,54},{8,56},{10,58},{12,60},{14,62},{16,32}... | collective-permute-start | bytes 208904 | tf_op jit(solution)/shard_map/ppermute | solution.py:297
  25.2 3.8 %collective-permute-start.5 = (bf16[272,128]{1,0:T(8,128)(2,1)S(1)}, bf16[272,128]{1,0:T(8,128)(2,1)S(1)}, u32[]{:S(2)}, u32[]{:S(2)}) collective-permute-start(bf16[272,128]{1,0:T(8,128)(2,1)S(1)} %get-tuple-element.56.refs_2_), channel_id=1, source_target_pairs={{0,16},{2,18},{4,20},{6,22},{8,24},{10,26},{12,28},{14,30},{16,0},... | collective-permute-start | bytes 208904 | tf_op jit(solution)/shard_map/ppermute | solution.py:297
  29.1 6.4 %collective-permute-start.10 = (bf16[272,128]{1,0:T(8,128)(2,1)S(1)}, bf16[272,128]{1,0:T(8,128)(2,1)S(1)}, u32[]{:S(2)}, u32[]{:S(2)}) collective-permute-start(bf16[272,128]{1,0:T(8,128)(2,1)S(1)} %get-tuple-element.63), channel_id=1, source_target_pairs={{0,192},{2,194},{4,196},{6,198},{8,200},{10,202},{12,204},{14,206}... | collective-permute-start | bytes 208904 | tf_op jit(solution)/shard_map/ppermute | solution.py:297
  33.8 4.8 %collective-permute-start.9 = (bf16[272,128]{1,0:T(8,128)(2,1)S(1)}, bf16[272,128]{1,0:T(8,128)(2,1)S(1)}, u32[]{:S(2)}, u32[]{:S(2)}) collective-permute-start(bf16[272,128]{1,0:T(8,128)(2,1)S(1)} %get-tuple-element.63), channel_id=1, source_target_pairs={{0,128},{2,130},{4,132},{6,134},{8,136},{10,138},{12,140},{14,142}... | collective-permute-start | bytes 208904 | tf_op jit(solution)/shard_map/ppermute | solution.py:297
  34.2 4.3 %collective-permute-start.8 = (bf16[272,128]{1,0:T(8,128)(2,1)S(1)}, bf16[272,128]{1,0:T(8,128)(2,1)S(1)}, u32[]{:S(2)}, u32[]{:S(2)}) collective-permute-start(bf16[272,128]{1,0:T(8,128)(2,1)S(1)} %get-tuple-element.63), channel_id=1, source_target_pairs={{0,64},{2,66},{4,68},{6,70},{8,72},{10,74},{12,76},{14,78},{16,80}... | collective-permute-start | bytes 208904 | tf_op jit(solution)/shard_map/ppermute | solution.py:297
  40.4 5.7 %collective-permute-start.12 = (bf16[256,1024]{1,0:T(8,128)(2,1)S(1)}, bf16[256,1024]{1,0:T(8,128)(2,1)S(1)}, u32[]{:S(2)}, u32[]{:S(2)}) collective-permute-start(bf16[256,1024]{1,0:T(8,128)(2,1)S(1)} %get-tuple-element.70), channel_id=1, source_target_pairs={{0,1},{1,0},{2,3},{3,2},{4,5},{5,4},{6,7},{7,6},{8,9},{9,8},{10,11... | collective-permute-start | bytes 1572872 | tf_op jit(solution)/shard_map/ppermute | solution.py:226
  44.5 2.4 %collective-permute-start.11 = (bf16[256,1024]{1,0:T(8,128)(2,1)S(1)}, bf16[256,1024]{1,0:T(8,128)(2,1)S(1)}, u32[]{:S(2)}, u32[]{:S(2)}) collective-permute-start(bf16[256,1024]{1,0:T(8,128)(2,1)S(1)} %get-tuple-element.69), channel_id=1, source_target_pairs={{0,1},{1,0},{2,3},{3,2},{4,5},{5,4},{6,7},{7,6},{8,9},{9,8},{10,11... | collective-permute-start | bytes 1572872 | tf_op jit(solution)/shard_map/ppermute | solution.py:226

commit v10 on v8

--- a/solution.py
+++ b/solution.py
@@ -6,11 +6,11 @@
 from jax.sharding import PartitionSpec as P
 
 HEAD = 128
-ID_ROWS = 16
+ID_ROWS = 8
 BLOCK = 256
 NORM_BLOCK = 512
 ROUNDS = ((1, 2, 3), (6,), (8, 24, 16), (32, 96, 64))
-INTRA_STEPS = (1, 2)
+INTRA_STEPS = (1, 3)
 CHUNKS = 2
 STAGE_COPIES = 4
 ADD_STEPS = 2
@@ -322,7 +322,7 @@
         )(place, col, message, *got, *extra)
         if step == 0:
             message, wq = lax.optimization_barrier((message, wq))
-        if step in INTRA_STEPS:
+        if step in INTRA_STEPS and not final:
             message, queries[-1] = lax.optimization_barrier((message, queries[-1]))
 
     normed, *theirs = pl.pallas_call(

time: 45.8 us -> 45.6 us (level)
  no operation moved by 1% of the time
where the time goes in v10:
time: 45.6 us; the launch traced here: 45.5 us
  starting transfers between devices  20.6 us (45%)
  Pallas kernels  15.8 us (35%)
  waiting for transfers between devices  8.93 us (20%)
    ppermute x10, starting transfers between devices, on_device(): lax.ppermute(message, 'seq', [(i, i ^ b) for i in range(count)])  13.9 us
    ppermute x10, waiting for transfers between devices, on_device(): lax.ppermute(message, 'seq', [(i, i ^ b) for i in range(count)])  8.32 us
    ppermute x3, starting transfers between devices, swap_head(): return lax.ppermute(x, 'head', [(0, 1), (1, 0)])  6.72 us
    pallas_call x2, Pallas kernels, intra(): pl.pallas_call(intra_kernel, out_shape=(shape((rows, group_width), BF16),...  5.51 us
    pallas_call x1, Pallas kernels, on_device(): pl.pallas_call(stage_kernel, out_shape=shape(q_weight.shape, BF16), in_sp...  2.2 us
    pallas_call x1, Pallas kernels, on_device(): pl.pallas_call(own_half_kernel, out_shape=(shape(tokens.shape, BF16), sha...  2.06 us
    pallas_call x1, Pallas kernels, on_device(): pl.pallas_call(lambda *refs: norm_kernel(ROUNDS[-1], kv_heads, *refs), ou...  1.81 us
    pallas_call x2, Pallas kernels, on_device(): pl.pallas_call(add_kernel, grid=(ADD_STEPS,), out_shape=shape((rows, half...  1.69 us
  transfers between devices with their start and end apart: 13, of which 7 were waited for; matrix products, arithmetic and copies ran while one was open for 0% of the time, Pallas kernels for 26%

profile of v10, /device:TPU:1, one launch (start us, length us, event | category | flops | bytes accessed | tf_op | source)
XLA Modules:
  0.0 45.5 jit_solution(17975222829347941956)
XLA Ops:
  0.0 3.2 %collective-permute-start = (bf16[512,1024]{1,0:T(8,128)(2,1)}, bf16[512,1024]{1,0:T(8,128)(2,1)S(1)}, u32[]{:S(2)}, u32[]{:S(2)}) collective-permute-start(bf16[512,1024]{1,0:T(8,128)(2,1)} %own_hbm.1), channel_id=1, source_target_pairs={{0,1},{1,0},{2,3},{3,2},{4,5},{5,4},{6,7},{7,6},{8,9},{9,8},{10,11... | collective-permute-start | bytes 3145736 | tf_op jit(solution)/shard_map/ppermute | solution.py:226
  3.2 2.1 %own_half.1 = (bf16[512,1024]{1,0:T(8,128)(2,1)S(1)}, bf16[2048,256]{1,0:T(8,128)(2,1)S(1)}, bf16[2048,256]{1,0:T(8,128)(2,1)S(1)}, f32[512,256]{1,0:T(8,128)S(1...) custom-call(s32[1]{0:T(128)} %bitcast.core_ref.refs_0_, s32[1,512]{1,0:T(1,128)} %bitcast.5, ...), custom_call_target="tpu_custom_call" | custom-call | tf_op jit(solution)/shard_map/own_half/pallas_call | solution.py:241
  5.3 0.4 collective-permute-done.other_ref
  5.7 1.0 %key_value.1 = (bf16[512,256]{1,0:T(8,128)(2,1)S(1)}, bf16[512,256]{1,0:T(8,128)(2,1)S(1)}, bf16[264,128]{1,0:T(8,128)(2,1)S(1)}) custom-call(s32[1]{0:T(128)} %bitcast.core_ref.refs_0_, bf16[512,1024]{1,0:T(8,128)(2,1)S(1)} %collective-permute-done.other_ref, f32[512,256]{1,0:T(8,128)S(1)} %get-tuple-element.37.k_part_ref, ...), custom_call_target="tpu_custom_call" | custom-call | tf_op jit(solution)/shard_map/key_value/pallas_call | solution.py:259
  6.8 2.7 %collective-permute-start.3 = (bf16[264,128]{1,0:T(8,128)(2,1)S(1)}, bf16[264,128]{1,0:T(8,128)(2,1)S(1)}, u32[]{:S(2)}, u32[]{:S(2)}) collective-permute-start(bf16[264,128]{1,0:T(8,128)(2,1)S(1)} %get-tuple-element.41.refs_2_.after_ref), channel_id=1, source_target_pairs={{0,6},{2,4},{4,2},{6,0},{8,14},{10,12},{12,10},{14,8},{16,22},{18,... | collective-permute-start | bytes 202760 | tf_op jit(solution)/shard_map/ppermute | solution.py:296
  9.5 0.0 collective-permute-start.2
  9.5 0.9 %collective-permute-start.1 = (bf16[264,128]{1,0:T(8,128)(2,1)S(1)}, bf16[264,128]{1,0:T(8,128)(2,1)S(1)}, u32[]{:S(2)}, u32[]{:S(2)}) collective-permute-start(bf16[264,128]{1,0:T(8,128)(2,1)S(1)} %get-tuple-element.41.refs_2_.after_ref), channel_id=1, source_target_pairs={{0,2},{2,0},{4,6},{6,4},{8,10},{10,8},{12,14},{14,12},{16,18},{18,... | collective-permute-start | bytes 202760 | tf_op jit(solution)/shard_map/ppermute | solution.py:296
  10.4 2.2 %stage.1.wq_ref = bf16[2048,1024]{1,0:T(8,128)(2,1)S(1)} custom-call(bf16[264,128]{1,0:T(8,128)(2,1)S(1)} %get-tuple-element.41.refs_2_.after_ref, bf16[2048,1024]{1,0:T(8,128)(2,1)} %weight_hbm.1), custom_call_target="tpu_custom_call" | custom-call | tf_op jit(solution)/shard_map/stage/pallas_call | solution.py:298
  12.6 3.0 %collective-permute-done.2.refs_4_ = bf16[264,128]{1,0:T(8,128)(2,1)S(1)} collective-permute-done((bf16[264,128]{1,0:T(8,128)(2,1)S(1)}, bf16[264,128]{1,0:T(8,128)(2,1)S(1)}, u32[]{:S(2)}, u32[]{:S(2)}) %collective-permute-start.2) | collective-permute-done | bytes 67616 | tf_op jit(solution)/shard_map/ppermute | solution.py:296
  15.6 0.1 combine.3
  15.7 2.8 %collective-permute-start.4 = (bf16[264,128]{1,0:T(8,128)(2,1)S(1)}, bf16[264,128]{1,0:T(8,128)(2,1)S(1)}, u32[]{:S(2)}, u32[]{:S(2)}) collective-permute-start(bf16[264,128]{1,0:T(8,128)(2,1)S(1)} %get-tuple-element.43.refs_2_), channel_id=1, source_target_pairs={{0,12},{2,14},{4,8},{6,10},{8,4},{10,6},{12,0},{14,2},{16,28},{18,... | collective-permute-start | bytes 202760 | tf_op jit(solution)/shard_map/ppermute | solution.py:296
  18.5 2.8 %intra_0.1 = (bf16[512,512]{1,0:T(8,128)(2,1)S(1)}, f32[512,512]{1,0:T(8,128)S(1)}) custom-call(s32[1]{0:T(128)} %bitcast.core_ref.refs_0_, bf16[512,1024]{1,0:T(8,128)(2,1)S(1)} %get-tuple-element.46.own_ref, bf16[512,1024]{1,0:T(8,128)(2,1)S(1)} %collective-permute-done.other_ref, bf16[2048,1024]{1,0:T(8,128)(2,1)S(1)} %stage.1.wq_ref, ...), custom_call_target="tpu_custom_call" | custom-call | tf_op jit(solution)/shard_map/intra_0/pallas_call | solution.py:273
  21.3 0.0 copy-start
  21.3 0.0 copy-start.1
  21.4 2.8 %collective-permute-start.7 = (bf16[264,128]{1,0:T(8,128)(2,1)S(1)}, bf16[264,128]{1,0:T(8,128)(2,1)S(1)}, u32[]{:S(2)}, u32[]{:S(2)}) collective-permute-start(bf16[264,128]{1,0:T(8,128)(2,1)S(1)} %get-tuple-element.54.refs_2_), channel_id=1, source_target_pairs={{0,32},{2,34},{4,36},{6,38},{8,40},{10,42},{12,44},{14,46},{16,48}... | collective-permute-start | bytes 202760 | tf_op jit(solution)/shard_map/ppermute | solution.py:296
  24.2 0.9 %collective-permute-start.6 = (bf16[264,128]{1,0:T(8,128)(2,1)S(1)}, bf16[264,128]{1,0:T(8,128)(2,1)S(1)}, u32[]{:S(2)}, u32[]{:S(2)}) collective-permute-start(bf16[264,128]{1,0:T(8,128)(2,1)S(1)} %get-tuple-element.54.refs_2_), channel_id=1, source_target_pairs={{0,48},{2,50},{4,52},{6,54},{8,56},{10,58},{12,60},{14,62},{16,32}... | collective-permute-start | bytes 202760 | tf_op jit(solution)/shard_map/ppermute | solution.py:296
  25.1 1.0 %collective-permute-done.7.refs_5_ = bf16[264,128]{1,0:T(8,128)(2,1)S(1)} collective-permute-done((bf16[264,128]{1,0:T(8,128)(2,1)S(1)}, bf16[264,128]{1,0:T(8,128)(2,1)S(1)}, u32[]{:S(2)}, u32[]{:S(2)}) %collective-permute-start.7) | collective-permute-done | bytes 67616 | tf_op jit(solution)/shard_map/ppermute | solution.py:296
  26.1 2.7 %collective-permute-done.6.refs_4_ = bf16[264,128]{1,0:T(8,128)(2,1)S(1)} collective-permute-done((bf16[264,128]{1,0:T(8,128)(2,1)S(1)}, bf16[264,128]{1,0:T(8,128)(2,1)S(1)}, u32[]{:S(2)}, u32[]{:S(2)}) %collective-permute-start.6) | collective-permute-done | bytes 67616 | tf_op jit(solution)/shard_map/ppermute | solution.py:296
  28.8 0.1 collective-permute-done.5.refs_3_
  28.8 0.1 combine.5
  28.9 3.0 %collective-permute-start.10 = (bf16[264,128]{1,0:T(8,128)(2,1)S(1)}, bf16[264,128]{1,0:T(8,128)(2,1)S(1)}, u32[]{:S(2)}, u32[]{:S(2)}) collective-permute-start(bf16[264,128]{1,0:T(8,128)(2,1)S(1)} %get-tuple-element.57), channel_id=1, source_target_pairs={{0,128},{2,130},{4,132},{6,134},{8,136},{10,138},{12,140},{14,142}... | collective-permute-start | bytes 202760 | tf_op jit(solution)/shard_map/ppermute | solution.py:296
  31.9 0.8 %collective-permute-start.9 = (bf16[264,128]{1,0:T(8,128)(2,1)S(1)}, bf16[264,128]{1,0:T(8,128)(2,1)S(1)}, u32[]{:S(2)}, u32[]{:S(2)}) collective-permute-start(bf16[264,128]{1,0:T(8,128)(2,1)S(1)} %get-tuple-element.57), channel_id=1, source_target_pairs={{0,192},{2,194},{4,196},{6,198},{8,200},{10,202},{12,204},{14,206}... | collective-permute-start | bytes 202760 | tf_op jit(solution)/shard_map/ppermute | solution.py:296
  32.7 0.0 collective-permute-start.8
  32.7 2.8 %intra_1.1 = (bf16[512,512]{1,0:T(8,128)(2,1)S(1)}, f32[512,512]{1,0:T(8,128)S(1)}) custom-call(s32[1]{0:T(128)} %bitcast.core_ref.refs_0_, bf16[512,1024]{1,0:T(8,128)(2,1)S(1)} %get-tuple-element.46.own_ref, bf16[512,1024]{1,0:T(8,128)(2,1)S(1)} %collective-permute-done.other_ref, bf16[2048,1024]{1,0:T(8,128)(2,1)S(1)} %stage.1.wq_ref, ...), custom_call_target="tpu_custom_call" | custom-call | tf_op jit(solution)/shard_map/intra_1/pallas_call | solution.py:273
  35.5 1.5 %collective-permute-done.9.refs_4_ = bf16[264,128]{1,0:T(8,128)(2,1)S(1)} collective-permute-done((bf16[264,128]{1,0:T(8,128)(2,1)S(1)}, bf16[264,128]{1,0:T(8,128)(2,1)S(1)}, u32[]{:S(2)}, u32[]{:S(2)}) %collective-permute-start.9) | collective-permute-done | bytes 67616 | tf_op jit(solution)/shard_map/ppermute | solution.py:296
  37.1 1.8 %norm.1 = (bf16[512,1024]{1,0:T(8,128)(2,1)S(1)}, bf16[256,1024]{1,0:T(8,128)(2,1)S(1)}, bf16[256,1024]{1,0:T(8,128)(2,1)S(1)}) custom-call(s32[1]{0:T(128)} %bitcast.core_ref.refs_0_, s32[1]{0:T(128)} %bitcast.1.refs_0_.refs_1_, f32[256,128]{1,0:T(8,128)S(1)} %get-tuple-element.56.refs_2_, bf16[264,128]{1,0:T(8,128)(2,1)S(1)} %collective-permute-done.8.refs_3_, ...), custom_call_target="tpu_custom_call" | custom-call | tf_op jit(solution)/shard_map/norm/pallas_call | solution.py:328
  38.9 3.4 %collective-permute-start.12 = (bf16[256,1024]{1,0:T(8,128)(2,1)S(1)}, bf16[256,1024]{1,0:T(8,128)(2,1)S(1)}, u32[]{:S(2)}, u32[]{:S(2)}) collective-permute-start(bf16[256,1024]{1,0:T(8,128)(2,1)S(1)} %get-tuple-element.66), channel_id=1, source_target_pairs={{0,1},{1,0},{2,3},{3,2},{4,5},{5,4},{6,7},{7,6},{8,9},{9,8},{10,11... | collective-permute-start | bytes 1572872 | tf_op jit(solution)/shard_map/ppermute | solution.py:226
  42.3 0.1 collective-permute-start.11
  42.4 1.3 %own.1.mine_ref = f32[512,1024]{1,0:T(8,128)S(1)} custom-call(s32[1]{0:T(128)} %bitcast.core_ref.refs_0_, bf16[512,1024]{1,0:T(8,128)(2,1)S(1)} %get-tuple-element.64.normed_ref, bf16[1024,2048]{1,0:T(8,128)(2,1)S(1)} %copy-done), custom_call_target="tpu_custom_call" | custom-call | tf_op jit(solution)/shard_map/own/pallas_call | solution.py:337
  43.6 0.2 collective-permute-done.12.theirs_ref
  43.8 0.9 %add_0.1.refs_0_ = bf16[512,1024]{1,0:T(8,128)(2,1)} custom-call(f32[512,1024]{1,0:T(8,128)S(1)} %own.1.mine_ref, bf16[256,1024]{1,0:T(8,128)(2,1)S(1)} %collective-permute-done.12.theirs_ref), custom_call_target="tpu_custom_call" | custom-call | tf_op jit(solution)/shard_map/add_0/pallas_call | solution.py:348
  44.7 0.8 %add_1.1 = bf16[512,1024]{1,0:T(8,128)(2,1)} custom-call(f32[512,1024]{1,0:T(8,128)S(1)} %own.1.mine_ref, bf16[256,1024]{1,0:T(8,128)(2,1)S(1)} %collective-permute-done.11.theirs_ref, bf16[512,1024]{1,0:T(8,128)(2,1)} %add_0.1.refs_0_), custom_call_target="tpu_custom_call", output_to_operand_aliasing={{}: (2, {})} | custom-call | tf_op jit(solution)/shard_map/add_1/pallas_call | solution.py:348
  (10 shorter events, 0.1 us)
Async XLA Ops:
  0.0 5.7 %collective-permute-start = (bf16[512,1024]{1,0:T(8,128)(2,1)}, bf16[512,1024]{1,0:T(8,128)(2,1)S(1)}, u32[]{:S(2)}, u32[]{:S(2)}) collective-permute-start(bf16[512,1024]{1,0:T(8,128)(2,1)} %own_hbm.1), channel_id=1, source_target_pairs={{0,1},{1,0},{2,3},{3,2},{4,5},{5,4},{6,7},{7,6},{8,9},{9,8},{10,11... | collective-permute-start | bytes 3145736 | tf_op jit(solution)/shard_map/ppermute | solution.py:226
  6.8 5.9 %collective-permute-start.3 = (bf16[264,128]{1,0:T(8,128)(2,1)S(1)}, bf16[264,128]{1,0:T(8,128)(2,1)S(1)}, u32[]{:S(2)}, u32[]{:S(2)}) collective-permute-start(bf16[264,128]{1,0:T(8,128)(2,1)S(1)} %get-tuple-element.41.refs_2_.after_ref), channel_id=1, source_target_pairs={{0,6},{2,4},{4,2},{6,0},{8,14},{10,12},{12,10},{14,8},{16,22},{18,... | collective-permute-start | bytes 202760 | tf_op jit(solution)/shard_map/ppermute | solution.py:296
  9.5 6.1 %collective-permute-start.2 = (bf16[264,128]{1,0:T(8,128)(2,1)S(1)}, bf16[264,128]{1,0:T(8,128)(2,1)S(1)}, u32[]{:S(2)}, u32[]{:S(2)}) collective-permute-start(bf16[264,128]{1,0:T(8,128)(2,1)S(1)} %get-tuple-element.41.refs_2_.after_ref), channel_id=1, source_target_pairs={{0,4},{2,6},{4,0},{6,2},{8,12},{10,14},{12,8},{14,10},{16,20},{18,... | collective-permute-start | bytes 202760 | tf_op jit(solution)/shard_map/ppermute | solution.py:296
  9.5 6.1 %collective-permute-start.1 = (bf16[264,128]{1,0:T(8,128)(2,1)S(1)}, bf16[264,128]{1,0:T(8,128)(2,1)S(1)}, u32[]{:S(2)}, u32[]{:S(2)}) collective-permute-start(bf16[264,128]{1,0:T(8,128)(2,1)S(1)} %get-tuple-element.41.refs_2_.after_ref), channel_id=1, source_target_pairs={{0,2},{2,0},{4,6},{6,4},{8,10},{10,8},{12,14},{14,12},{16,18},{18,... | collective-permute-start | bytes 202760 | tf_op jit(solution)/shard_map/ppermute | solution.py:296
  15.7 5.6 %collective-permute-start.4 = (bf16[264,128]{1,0:T(8,128)(2,1)S(1)}, bf16[264,128]{1,0:T(8,128)(2,1)S(1)}, u32[]{:S(2)}, u32[]{:S(2)}) collective-permute-start(bf16[264,128]{1,0:T(8,128)(2,1)S(1)} %get-tuple-element.43.refs_2_), channel_id=1, source_target_pairs={{0,12},{2,14},{4,8},{6,10},{8,4},{10,6},{12,0},{14,2},{16,28},{18,... | collective-permute-start | bytes 202760 | tf_op jit(solution)/shard_map/ppermute | solution.py:296
  21.3 15.8 %copy-start = (bf16[1024,2048]{1,0:T(8,128)(2,1)S(1)}, bf16[1024,2048]{1,0:T(8,128)(2,1)}, u32[]{:S(2)}) copy-start(bf16[1024,2048]{1,0:T(8,128)(2,1)} %weight_ref.1) | copy-start | bytes 12582916
  21.3 15.8 %copy-start.1 = (f32[1024]{0:T(1024)S(1)}, f32[1024]{0:T(1024)}, u32[]{:S(2)}) copy-start(f32[1024]{0:T(1024)} %param.11) | copy-start | bytes 12292
  21.4 4.7 %collective-permute-start.7 = (bf16[264,128]{1,0:T(8,128)(2,1)S(1)}, bf16[264,128]{1,0:T(8,128)(2,1)S(1)}, u32[]{:S(2)}, u32[]{:S(2)}) collective-permute-start(bf16[264,128]{1,0:T(8,128)(2,1)S(1)} %get-tuple-element.54.refs_2_), channel_id=1, source_target_pairs={{0,32},{2,34},{4,36},{6,38},{8,40},{10,42},{12,44},{14,46},{16,48}... | collective-permute-start | bytes 202760 | tf_op jit(solution)/shard_map/ppermute | solution.py:296
  24.2 4.6 %collective-permute-start.6 = (bf16[264,128]{1,0:T(8,128)(2,1)S(1)}, bf16[264,128]{1,0:T(8,128)(2,1)S(1)}, u32[]{:S(2)}, u32[]{:S(2)}) collective-permute-start(bf16[264,128]{1,0:T(8,128)(2,1)S(1)} %get-tuple-element.54.refs_2_), channel_id=1, source_target_pairs={{0,48},{2,50},{4,52},{6,54},{8,56},{10,58},{12,60},{14,62},{16,32}... | collective-permute-start | bytes 202760 | tf_op jit(solution)/shard_map/ppermute | solution.py:296
  25.1 3.8 %collective-permute-start.5 = (bf16[264,128]{1,0:T(8,128)(2,1)S(1)}, bf16[264,128]{1,0:T(8,128)(2,1)S(1)}, u32[]{:S(2)}, u32[]{:S(2)}) collective-permute-start(bf16[264,128]{1,0:T(8,128)(2,1)S(1)} %get-tuple-element.54.refs_2_), channel_id=1, source_target_pairs={{0,16},{2,18},{4,20},{6,22},{8,24},{10,26},{12,28},{14,30},{16,0},... | collective-permute-start | bytes 202760 | tf_op jit(solution)/shard_map/ppermute | solution.py:296
  28.9 6.5 %collective-permute-start.10 = (bf16[264,128]{1,0:T(8,128)(2,1)S(1)}, bf16[264,128]{1,0:T(8,128)(2,1)S(1)}, u32[]{:S(2)}, u32[]{:S(2)}) collective-permute-start(bf16[264,128]{1,0:T(8,128)(2,1)S(1)} %get-tuple-element.57), channel_id=1, source_target_pairs={{0,128},{2,130},{4,132},{6,134},{8,136},{10,138},{12,140},{14,142}... | collective-permute-start | bytes 202760 | tf_op jit(solution)/shard_map/ppermute | solution.py:296
  31.9 5.1 %collective-permute-start.9 = (bf16[264,128]{1,0:T(8,128)(2,1)S(1)}, bf16[264,128]{1,0:T(8,128)(2,1)S(1)}, u32[]{:S(2)}, u32[]{:S(2)}) collective-permute-start(bf16[264,128]{1,0:T(8,128)(2,1)S(1)} %get-tuple-element.57), channel_id=1, source_target_pairs={{0,192},{2,194},{4,196},{6,198},{8,200},{10,202},{12,204},{14,206}... | collective-permute-start | bytes 202760 | tf_op jit(solution)/shard_map/ppermute | solution.py:296
  32.7 4.3 %collective-permute-start.8 = (bf16[264,128]{1,0:T(8,128)(2,1)S(1)}, bf16[264,128]{1,0:T(8,128)(2,1)S(1)}, u32[]{:S(2)}, u32[]{:S(2)}) collective-permute-start(bf16[264,128]{1,0:T(8,128)(2,1)S(1)} %get-tuple-element.57), channel_id=1, source_target_pairs={{0,64},{2,66},{4,68},{6,70},{8,72},{10,74},{12,76},{14,78},{16,80}... | collective-permute-start | bytes 202760 | tf_op jit(solution)/shard_map/ppermute | solution.py:296
  38.9 4.9 %collective-permute-start.12 = (bf16[256,1024]{1,0:T(8,128)(2,1)S(1)}, bf16[256,1024]{1,0:T(8,128)(2,1)S(1)}, u32[]{:S(2)}, u32[]{:S(2)}) collective-permute-start(bf16[256,1024]{1,0:T(8,128)(2,1)S(1)} %get-tuple-element.66), channel_id=1, source_target_pairs={{0,1},{1,0},{2,3},{3,2},{4,5},{5,4},{6,7},{7,6},{8,9},{9,8},{10,11... | collective-permute-start | bytes 1572872 | tf_op jit(solution)/shard_map/ppermute | solution.py:226
  42.3 2.4 %collective-permute-start.11 = (bf16[256,1024]{1,0:T(8,128)(2,1)S(1)}, bf16[256,1024]{1,0:T(8,128)(2,1)S(1)}, u32[]{:S(2)}, u32[]{:S(2)}) collective-permute-start(bf16[256,1024]{1,0:T(8,128)(2,1)S(1)} %get-tuple-element.65), channel_id=1, source_target_pairs={{0,1},{1,0},{2,3},{3,2},{4,5},{5,4},{6,7},{7,6},{8,9},{9,8},{10,11... | collective-permute-start | bytes 1572872 | tf_op jit(solution)/shard_map/ppermute | solution.py:226

commit v11 on v10

--- a/solution.py
+++ b/solution.py
@@ -10,7 +10,7 @@
 BLOCK = 256
 NORM_BLOCK = 512
 ROUNDS = ((1, 2, 3), (6,), (8, 24, 16), (32, 96, 64))
-INTRA_STEPS = (1, 3)
+INTRA_STEPS = (2, 3)
 CHUNKS = 2
 STAGE_COPIES = 4
 ADD_STEPS = 2

time: 45.6 us -> 45.3 us (level)
    ppermute x3, starting transfers between devices: 6.72 us -> 7.91 us  [swap_head(): return lax.ppermute(x, 'head', [(0, 1), (1, 0)])]
    ppermute x10, starting transfers between devices: 13.9 us -> 12.8 us  [on_device(): lax.ppermute(message, 'seq', [(i, i ^ b) for i in range(count)])]
  transfers between devices with their start and end apart: 13 -> 13, of which waited for: 7 -> 6; matrix products, arithmetic and copies ran while one was open for 0% -> 0% of each run, Pallas kernels for 26% -> 26%
where the time goes in v11:
time: 45.3 us; the launch traced here: 45.2 us
  starting transfers between devices  20.7 us (46%)
  Pallas kernels  15.8 us (35%)
  waiting for transfers between devices  8.57 us (19%)
    ppermute x10, starting transfers between devices, on_device(): lax.ppermute(message, 'seq', [(i, i ^ b) for i in range(count)])  12.8 us
    ppermute x10, waiting for transfers between devices, on_device(): lax.ppermute(message, 'seq', [(i, i ^ b) for i in range(count)])  7.96 us
    ppermute x3, starting transfers between devices, swap_head(): return lax.ppermute(x, 'head', [(0, 1), (1, 0)])  7.91 us
    pallas_call x2, Pallas kernels, intra(): pl.pallas_call(intra_kernel, out_shape=(shape((rows, group_width), BF16),...  5.53 us
    pallas_call x1, Pallas kernels, on_device(): pl.pallas_call(stage_kernel, out_shape=shape(q_weight.shape, BF16), in_sp...  2.2 us
    pallas_call x1, Pallas kernels, on_device(): pl.pallas_call(own_half_kernel, out_shape=(shape(tokens.shape, BF16), sha...  2.06 us
    pallas_call x1, Pallas kernels, on_device(): pl.pallas_call(lambda *refs: norm_kernel(ROUNDS[-1], kv_heads, *refs), ou...  1.81 us
    pallas_call x2, Pallas kernels, on_device(): pl.pallas_call(add_kernel, grid=(ADD_STEPS,), out_shape=shape((rows, half...  1.69 us
  transfers between devices with their start and end apart: 13, of which 6 were waited for; matrix products, arithmetic and copies ran while one was open for 0% of the time, Pallas kernels for 26%

profile of v11, /device:TPU:1, one launch (start us, length us, event | category | flops | bytes accessed | tf_op | source)
XLA Modules:
  0.0 45.2 jit_solution(9160487904105329593)
XLA Ops:
  0.0 3.2 %collective-permute-start = (bf16[512,1024]{1,0:T(8,128)(2,1)}, bf16[512,1024]{1,0:T(8,128)(2,1)S(1)}, u32[]{:S(2)}, u32[]{:S(2)}) collective-permute-start(bf16[512,1024]{1,0:T(8,128)(2,1)} %own_hbm.1), channel_id=1, source_target_pairs={{0,1},{1,0},{2,3},{3,2},{4,5},{5,4},{6,7},{7,6},{8,9},{9,8},{10,11... | collective-permute-start | bytes 3145736 | tf_op jit(solution)/shard_map/ppermute | solution.py:226
  3.2 2.1 %own_half.1 = (bf16[512,1024]{1,0:T(8,128)(2,1)S(1)}, bf16[2048,256]{1,0:T(8,128)(2,1)S(1)}, bf16[2048,256]{1,0:T(8,128)(2,1)S(1)}, f32[512,256]{1,0:T(8,128)S(1...) custom-call(s32[1]{0:T(128)} %bitcast.core_ref.refs_0_, s32[1,512]{1,0:T(1,128)} %bitcast.5, ...), custom_call_target="tpu_custom_call" | custom-call | tf_op jit(solution)/shard_map/own_half/pallas_call | solution.py:241
  5.3 0.4 collective-permute-done.other_ref
  5.7 1.0 %key_value.1 = (bf16[512,256]{1,0:T(8,128)(2,1)S(1)}, bf16[512,256]{1,0:T(8,128)(2,1)S(1)}, bf16[264,128]{1,0:T(8,128)(2,1)S(1)}) custom-call(s32[1]{0:T(128)} %bitcast.core_ref.refs_0_, bf16[512,1024]{1,0:T(8,128)(2,1)S(1)} %collective-permute-done.other_ref, f32[512,256]{1,0:T(8,128)S(1)} %get-tuple-element.37.k_part_ref, ...), custom_call_target="tpu_custom_call" | custom-call | tf_op jit(solution)/shard_map/key_value/pallas_call | solution.py:259
  6.8 2.7 %collective-permute-start.3 = (bf16[264,128]{1,0:T(8,128)(2,1)S(1)}, bf16[264,128]{1,0:T(8,128)(2,1)S(1)}, u32[]{:S(2)}, u32[]{:S(2)}) collective-permute-start(bf16[264,128]{1,0:T(8,128)(2,1)S(1)} %get-tuple-element.41.refs_2_.after_ref), channel_id=1, source_target_pairs={{0,6},{2,4},{4,2},{6,0},{8,14},{10,12},{12,10},{14,8},{16,22},{18,... | collective-permute-start | bytes 202760 | tf_op jit(solution)/shard_map/ppermute | solution.py:296
  9.5 0.9 %collective-permute-start.1 = (bf16[264,128]{1,0:T(8,128)(2,1)S(1)}, bf16[264,128]{1,0:T(8,128)(2,1)S(1)}, u32[]{:S(2)}, u32[]{:S(2)}) collective-permute-start(bf16[264,128]{1,0:T(8,128)(2,1)S(1)} %get-tuple-element.41.refs_2_.after_ref), channel_id=1, source_target_pairs={{0,2},{2,0},{4,6},{6,4},{8,10},{10,8},{12,14},{14,12},{16,18},{18,... | collective-permute-start | bytes 202760 | tf_op jit(solution)/shard_map/ppermute | solution.py:296
  10.4 2.2 %stage.1.wq_ref = bf16[2048,1024]{1,0:T(8,128)(2,1)S(1)} custom-call(bf16[264,128]{1,0:T(8,128)(2,1)S(1)} %get-tuple-element.41.refs_2_.after_ref, bf16[2048,1024]{1,0:T(8,128)(2,1)} %weight_hbm.1), custom_call_target="tpu_custom_call" | custom-call | tf_op jit(solution)/shard_map/stage/pallas_call | solution.py:298
  12.6 0.0 collective-permute-done.3.refs_5_
  12.6 3.0 %collective-permute-done.2.refs_4_ = bf16[264,128]{1,0:T(8,128)(2,1)S(1)} collective-permute-done((bf16[264,128]{1,0:T(8,128)(2,1)S(1)}, bf16[264,128]{1,0:T(8,128)(2,1)S(1)}, u32[]{:S(2)}, u32[]{:S(2)}) %collective-permute-start.2) | collective-permute-done | bytes 67616 | tf_op jit(solution)/shard_map/ppermute | solution.py:296
  15.6 0.0 collective-permute-done.1.refs_3_
  15.6 0.1 combine.3
  15.7 2.8 %collective-permute-start.4 = (bf16[264,128]{1,0:T(8,128)(2,1)S(1)}, bf16[264,128]{1,0:T(8,128)(2,1)S(1)}, u32[]{:S(2)}, u32[]{:S(2)}) collective-permute-start(bf16[264,128]{1,0:T(8,128)(2,1)S(1)} %get-tuple-element.43.refs_2_), channel_id=1, source_target_pairs={{0,12},{2,14},{4,8},{6,10},{8,4},{10,6},{12,0},{14,2},{16,28},{18,... | collective-permute-start | bytes 202760 | tf_op jit(solution)/shard_map/ppermute | solution.py:296
  18.5 2.6 %collective-permute-done.4.refs_3_ = bf16[264,128]{1,0:T(8,128)(2,1)S(1)} collective-permute-done((bf16[264,128]{1,0:T(8,128)(2,1)S(1)}, bf16[264,128]{1,0:T(8,128)(2,1)S(1)}, u32[]{:S(2)}, u32[]{:S(2)}) %collective-permute-start.4) | collective-permute-done | bytes 67616 | tf_op jit(solution)/shard_map/ppermute | solution.py:296
  21.1 1.9 %collective-permute-start.7 = (bf16[264,128]{1,0:T(8,128)(2,1)S(1)}, bf16[264,128]{1,0:T(8,128)(2,1)S(1)}, u32[]{:S(2)}, u32[]{:S(2)}) collective-permute-start(bf16[264,128]{1,0:T(8,128)(2,1)S(1)} %get-tuple-element.45.refs_2_), channel_id=1, source_target_pairs={{0,32},{2,34},{4,36},{6,38},{8,40},{10,42},{12,44},{14,46},{16,48}... | collective-permute-start | bytes 202760 | tf_op jit(solution)/shard_map/ppermute | solution.py:296
  23.1 0.9 %collective-permute-start.6 = (bf16[264,128]{1,0:T(8,128)(2,1)S(1)}, bf16[264,128]{1,0:T(8,128)(2,1)S(1)}, u32[]{:S(2)}, u32[]{:S(2)}) collective-permute-start(bf16[264,128]{1,0:T(8,128)(2,1)S(1)} %get-tuple-element.45.refs_2_), channel_id=1, source_target_pairs={{0,48},{2,50},{4,52},{6,54},{8,56},{10,58},{12,60},{14,62},{16,32}... | collective-permute-start | bytes 202760 | tf_op jit(solution)/shard_map/ppermute | solution.py:296
  23.9 2.8 %intra_0.1 = (bf16[512,512]{1,0:T(8,128)(2,1)S(1)}, f32[512,512]{1,0:T(8,128)S(1)}) custom-call(s32[1]{0:T(128)} %bitcast.core_ref.refs_0_, bf16[512,1024]{1,0:T(8,128)(2,1)S(1)} %get-tuple-element.49.own_ref, bf16[512,1024]{1,0:T(8,128)(2,1)S(1)} %collective-permute-done.other_ref, bf16[2048,1024]{1,0:T(8,128)(2,1)S(1)} %stage.1.wq_ref, ...), custom_call_target="tpu_custom_call" | custom-call | tf_op jit(solution)/shard_map/intra_0/pallas_call | solution.py:273
  26.7 0.0 copy-start
  26.7 0.0 copy-start.1
  26.7 1.6 %collective-permute-done.6.refs_4_ = bf16[264,128]{1,0:T(8,128)(2,1)S(1)} collective-permute-done((bf16[264,128]{1,0:T(8,128)(2,1)S(1)}, bf16[264,128]{1,0:T(8,128)(2,1)S(1)}, u32[]{:S(2)}, u32[]{:S(2)}) %collective-permute-start.6) | collective-permute-done | bytes 67616 | tf_op jit(solution)/shard_map/ppermute | solution.py:296
  28.4 0.1 combine.5
  28.5 2.8 %collective-permute-start.10 = (bf16[264,128]{1,0:T(8,128)(2,1)S(1)}, bf16[264,128]{1,0:T(8,128)(2,1)S(1)}, u32[]{:S(2)}, u32[]{:S(2)}) collective-permute-start(bf16[264,128]{1,0:T(8,128)(2,1)S(1)} %get-tuple-element.57), channel_id=1, source_target_pairs={{0,128},{2,130},{4,132},{6,134},{8,136},{10,138},{12,140},{14,142}... | collective-permute-start | bytes 202760 | tf_op jit(solution)/shard_map/ppermute | solution.py:296
  31.2 0.8 %collective-permute-start.9 = (bf16[264,128]{1,0:T(8,128)(2,1)S(1)}, bf16[264,128]{1,0:T(8,128)(2,1)S(1)}, u32[]{:S(2)}, u32[]{:S(2)}) collective-permute-start(bf16[264,128]{1,0:T(8,128)(2,1)S(1)} %get-tuple-element.57), channel_id=1, source_target_pairs={{0,192},{2,194},{4,196},{6,198},{8,200},{10,202},{12,204},{14,206}... | collective-permute-start | bytes 202760 | tf_op jit(solution)/shard_map/ppermute | solution.py:296
  32.0 0.0 collective-permute-start.8
  32.0 2.8 %intra_1.1 = (bf16[512,512]{1,0:T(8,128)(2,1)S(1)}, f32[512,512]{1,0:T(8,128)S(1)}) custom-call(s32[1]{0:T(128)} %bitcast.core_ref.refs_0_, bf16[512,1024]{1,0:T(8,128)(2,1)S(1)} %get-tuple-element.49.own_ref, bf16[512,1024]{1,0:T(8,128)(2,1)S(1)} %collective-permute-done.other_ref, bf16[2048,1024]{1,0:T(8,128)(2,1)S(1)} %stage.1.wq_ref, ...), custom_call_target="tpu_custom_call" | custom-call | tf_op jit(solution)/shard_map/intra_1/pallas_call | solution.py:273
  34.8 0.8 %collective-permute-done.9.refs_4_ = bf16[264,128]{1,0:T(8,128)(2,1)S(1)} collective-permute-done((bf16[264,128]{1,0:T(8,128)(2,1)S(1)}, bf16[264,128]{1,0:T(8,128)(2,1)S(1)}, u32[]{:S(2)}, u32[]{:S(2)}) %collective-permute-start.9) | collective-permute-done | bytes 67616 | tf_op jit(solution)/shard_map/ppermute | solution.py:296
  35.6 1.8 %norm.1 = (bf16[512,1024]{1,0:T(8,128)(2,1)S(1)}, bf16[256,1024]{1,0:T(8,128)(2,1)S(1)}, bf16[256,1024]{1,0:T(8,128)(2,1)S(1)}) custom-call(s32[1]{0:T(128)} %bitcast.core_ref.refs_0_, s32[1]{0:T(128)} %bitcast.1.refs_0_.refs_1_, f32[256,128]{1,0:T(8,128)S(1)} %get-tuple-element.47.refs_2_, bf16[264,128]{1,0:T(8,128)(2,1)S(1)} %collective-permute-done.8.refs_3_, ...), custom_call_target="tpu_custom_call" | custom-call | tf_op jit(solution)/shard_map/norm/pallas_call | solution.py:328
  37.4 4.6 %collective-permute-start.12 = (bf16[256,1024]{1,0:T(8,128)(2,1)S(1)}, bf16[256,1024]{1,0:T(8,128)(2,1)S(1)}, u32[]{:S(2)}, u32[]{:S(2)}) collective-permute-start(bf16[256,1024]{1,0:T(8,128)(2,1)S(1)} %get-tuple-element.66), channel_id=1, source_target_pairs={{0,1},{1,0},{2,3},{3,2},{4,5},{5,4},{6,7},{7,6},{8,9},{9,8},{10,11... | collective-permute-start | bytes 1572872 | tf_op jit(solution)/shard_map/ppermute | solution.py:226
  42.0 0.1 collective-permute-start.11
  42.1 1.3 %own.1.mine_ref = f32[512,1024]{1,0:T(8,128)S(1)} custom-call(s32[1]{0:T(128)} %bitcast.core_ref.refs_0_, bf16[512,1024]{1,0:T(8,128)(2,1)S(1)} %get-tuple-element.64.normed_ref, bf16[1024,2048]{1,0:T(8,128)(2,1)S(1)} %copy-done), custom_call_target="tpu_custom_call" | custom-call | tf_op jit(solution)/shard_map/own/pallas_call | solution.py:337
  43.4 0.2 collective-permute-done.12.theirs_ref
  43.5 0.9 %add_0.1.refs_0_ = bf16[512,1024]{1,0:T(8,128)(2,1)} custom-call(f32[512,1024]{1,0:T(8,128)S(1)} %own.1.mine_ref, bf16[256,1024]{1,0:T(8,128)(2,1)S(1)} %collective-permute-done.12.theirs_ref), custom_call_target="tpu_custom_call" | custom-call | tf_op jit(solution)/shard_map/add_0/pallas_call | solution.py:348
  44.4 0.8 %add_1.1 = bf16[512,1024]{1,0:T(8,128)(2,1)} custom-call(f32[512,1024]{1,0:T(8,128)S(1)} %own.1.mine_ref, bf16[256,1024]{1,0:T(8,128)(2,1)S(1)} %collective-permute-done.11.theirs_ref, bf16[512,1024]{1,0:T(8,128)(2,1)} %add_0.1.refs_0_), custom_call_target="tpu_custom_call", output_to_operand_aliasing={{}: (2, {})} | custom-call | tf_op jit(solution)/shard_map/add_1/pallas_call | solution.py:348
  (10 shorter events, 0.1 us)
Async XLA Ops:
  0.0 5.7 %collective-permute-start = (bf16[512,1024]{1,0:T(8,128)(2,1)}, bf16[512,1024]{1,0:T(8,128)(2,1)S(1)}, u32[]{:S(2)}, u32[]{:S(2)}) collective-permute-start(bf16[512,1024]{1,0:T(8,128)(2,1)} %own_hbm.1), channel_id=1, source_target_pairs={{0,1},{1,0},{2,3},{3,2},{4,5},{5,4},{6,7},{7,6},{8,9},{9,8},{10,11... | collective-permute-start | bytes 3145736 | tf_op jit(solution)/shard_map/ppermute | solution.py:226
  6.8 5.9 %collective-permute-start.3 = (bf16[264,128]{1,0:T(8,128)(2,1)S(1)}, bf16[264,128]{1,0:T(8,128)(2,1)S(1)}, u32[]{:S(2)}, u32[]{:S(2)}) collective-permute-start(bf16[264,128]{1,0:T(8,128)(2,1)S(1)} %get-tuple-element.41.refs_2_.after_ref), channel_id=1, source_target_pairs={{0,6},{2,4},{4,2},{6,0},{8,14},{10,12},{12,10},{14,8},{16,22},{18,... | collective-permute-start | bytes 202760 | tf_op jit(solution)/shard_map/ppermute | solution.py:296
  9.5 6.1 %collective-permute-start.2 = (bf16[264,128]{1,0:T(8,128)(2,1)S(1)}, bf16[264,128]{1,0:T(8,128)(2,1)S(1)}, u32[]{:S(2)}, u32[]{:S(2)}) collective-permute-start(bf16[264,128]{1,0:T(8,128)(2,1)S(1)} %get-tuple-element.41.refs_2_.after_ref), channel_id=1, source_target_pairs={{0,4},{2,6},{4,0},{6,2},{8,12},{10,14},{12,8},{14,10},{16,20},{18,... | collective-permute-start | bytes 202760 | tf_op jit(solution)/shard_map/ppermute | solution.py:296
  9.5 6.1 %collective-permute-start.1 = (bf16[264,128]{1,0:T(8,128)(2,1)S(1)}, bf16[264,128]{1,0:T(8,128)(2,1)S(1)}, u32[]{:S(2)}, u32[]{:S(2)}) collective-permute-start(bf16[264,128]{1,0:T(8,128)(2,1)S(1)} %get-tuple-element.41.refs_2_.after_ref), channel_id=1, source_target_pairs={{0,2},{2,0},{4,6},{6,4},{8,10},{10,8},{12,14},{14,12},{16,18},{18,... | collective-permute-start | bytes 202760 | tf_op jit(solution)/shard_map/ppermute | solution.py:296
  15.7 5.4 %collective-permute-start.4 = (bf16[264,128]{1,0:T(8,128)(2,1)S(1)}, bf16[264,128]{1,0:T(8,128)(2,1)S(1)}, u32[]{:S(2)}, u32[]{:S(2)}) collective-permute-start(bf16[264,128]{1,0:T(8,128)(2,1)S(1)} %get-tuple-element.43.refs_2_), channel_id=1, source_target_pairs={{0,12},{2,14},{4,8},{6,10},{8,4},{10,6},{12,0},{14,2},{16,28},{18,... | collective-permute-start | bytes 202760 | tf_op jit(solution)/shard_map/ppermute | solution.py:296
  21.1 5.6 %collective-permute-start.7 = (bf16[264,128]{1,0:T(8,128)(2,1)S(1)}, bf16[264,128]{1,0:T(8,128)(2,1)S(1)}, u32[]{:S(2)}, u32[]{:S(2)}) collective-permute-start(bf16[264,128]{1,0:T(8,128)(2,1)S(1)} %get-tuple-element.45.refs_2_), channel_id=1, source_target_pairs={{0,32},{2,34},{4,36},{6,38},{8,40},{10,42},{12,44},{14,46},{16,48}... | collective-permute-start | bytes 202760 | tf_op jit(solution)/shard_map/ppermute | solution.py:296
  23.1 5.3 %collective-permute-start.6 = (bf16[264,128]{1,0:T(8,128)(2,1)S(1)}, bf16[264,128]{1,0:T(8,128)(2,1)S(1)}, u32[]{:S(2)}, u32[]{:S(2)}) collective-permute-start(bf16[264,128]{1,0:T(8,128)(2,1)S(1)} %get-tuple-element.45.refs_2_), channel_id=1, source_target_pairs={{0,48},{2,50},{4,52},{6,54},{8,56},{10,58},{12,60},{14,62},{16,32}... | collective-permute-start | bytes 202760 | tf_op jit(solution)/shard_map/ppermute | solution.py:296
  23.9 4.4 %collective-permute-start.5 = (bf16[264,128]{1,0:T(8,128)(2,1)S(1)}, bf16[264,128]{1,0:T(8,128)(2,1)S(1)}, u32[]{:S(2)}, u32[]{:S(2)}) collective-permute-start(bf16[264,128]{1,0:T(8,128)(2,1)S(1)} %get-tuple-element.45.refs_2_), channel_id=1, source_target_pairs={{0,16},{2,18},{4,20},{6,22},{8,24},{10,26},{12,28},{14,30},{16,0},... | collective-permute-start | bytes 202760 | tf_op jit(solution)/shard_map/ppermute | solution.py:296
  26.7 8.9 %copy-start = (bf16[1024,2048]{1,0:T(8,128)(2,1)S(1)}, bf16[1024,2048]{1,0:T(8,128)(2,1)}, u32[]{:S(2)}) copy-start(bf16[1024,2048]{1,0:T(8,128)(2,1)} %weight_ref.1) | copy-start | bytes 12582916
  26.7 8.9 %copy-start.1 = (f32[1024]{0:T(1024)S(1)}, f32[1024]{0:T(1024)}, u32[]{:S(2)}) copy-start(f32[1024]{0:T(1024)} %param.11) | copy-start | bytes 12292
  28.5 6.3 %collective-permute-start.10 = (bf16[264,128]{1,0:T(8,128)(2,1)S(1)}, bf16[264,128]{1,0:T(8,128)(2,1)S(1)}, u32[]{:S(2)}, u32[]{:S(2)}) collective-permute-start(bf16[264,128]{1,0:T(8,128)(2,1)S(1)} %get-tuple-element.57), channel_id=1, source_target_pairs={{0,128},{2,130},{4,132},{6,134},{8,136},{10,138},{12,140},{14,142}... | collective-permute-start | bytes 202760 | tf_op jit(solution)/shard_map/ppermute | solution.py:296
  31.2 4.3 %collective-permute-start.9 = (bf16[264,128]{1,0:T(8,128)(2,1)S(1)}, bf16[264,128]{1,0:T(8,128)(2,1)S(1)}, u32[]{:S(2)}, u32[]{:S(2)}) collective-permute-start(bf16[264,128]{1,0:T(8,128)(2,1)S(1)} %get-tuple-element.57), channel_id=1, source_target_pairs={{0,192},{2,194},{4,196},{6,198},{8,200},{10,202},{12,204},{14,206}... | collective-permute-start | bytes 202760 | tf_op jit(solution)/shard_map/ppermute | solution.py:296
  32.0 3.6 %collective-permute-start.8 = (bf16[264,128]{1,0:T(8,128)(2,1)S(1)}, bf16[264,128]{1,0:T(8,128)(2,1)S(1)}, u32[]{:S(2)}, u32[]{:S(2)}) collective-permute-start(bf16[264,128]{1,0:T(8,128)(2,1)S(1)} %get-tuple-element.57), channel_id=1, source_target_pairs={{0,64},{2,66},{4,68},{6,70},{8,72},{10,74},{12,76},{14,78},{16,80}... | collective-permute-start | bytes 202760 | tf_op jit(solution)/shard_map/ppermute | solution.py:296
  37.4 6.1 %collective-permute-start.12 = (bf16[256,1024]{1,0:T(8,128)(2,1)S(1)}, bf16[256,1024]{1,0:T(8,128)(2,1)S(1)}, u32[]{:S(2)}, u32[]{:S(2)}) collective-permute-start(bf16[256,1024]{1,0:T(8,128)(2,1)S(1)} %get-tuple-element.66), channel_id=1, source_target_pairs={{0,1},{1,0},{2,3},{3,2},{4,5},{5,4},{6,7},{7,6},{8,9},{9,8},{10,11... | collective-permute-start | bytes 1572872 | tf_op jit(solution)/shard_map/ppermute | solution.py:226
  42.0 2.4 %collective-permute-start.11 = (bf16[256,1024]{1,0:T(8,128)(2,1)S(1)}, bf16[256,1024]{1,0:T(8,128)(2,1)S(1)}, u32[]{:S(2)}, u32[]{:S(2)}) collective-permute-start(bf16[256,1024]{1,0:T(8,128)(2,1)S(1)} %get-tuple-element.65), channel_id=1, source_target_pairs={{0,1},{1,0},{2,3},{3,2},{4,5},{5,4},{6,7},{7,6},{8,9},{9,8},{10,11... | collective-permute-start | bytes 1572872 | tf_op jit(solution)/shard_map/ppermute | solution.py:226

commit v12 on v11

--- a/solution.py
+++ b/solution.py
@@ -13,7 +13,7 @@
 INTRA_STEPS = (2, 3)
 CHUNKS = 2
 STAGE_COPIES = 4
-ADD_STEPS = 2
+ADD_STEPS = 1
 EPSILON = 1e-05
 F32 = jnp.float32
 BF16 = jnp.bfloat16
@@ -96,13 +96,11 @@
     last = col_ref[rows - 1 : rows, :]
     tail = col_ref[...] == last
     heads = key.shape[1] // HEAD
+    tail_key = jnp.where(jnp.concatenate([tail] * heads, axis=1), key.astype(F32), 0.0).astype(BF16)
+    state = lax.dot_general(tail_key, value, (((0,), (0,)), ((), ())), preferred_element_type=F32)
     for h in range(heads):
         cut = slice(h * HEAD, (h + 1) * HEAD)
-        tail_key = jnp.where(tail, key[:, cut].astype(F32), 0.0).astype(BF16)
-        state = lax.dot_general(
-            tail_key, value[:, cut], (((0,), (0,)), ((), ())), preferred_element_type=F32
-        )
-        message_ref[cut, :] = state.astype(BF16)
+        message_ref[cut, :] = state[cut, cut].astype(BF16)
     message_ref[heads * HEAD :, :] = jnp.broadcast_to(last, (ID_ROWS, HEAD)).astype(BF16)
 
 

time: 45.3 us -> 45.4 us (level)
  no operation moved by 1% of the time
where the time goes in v12:
time: 45.4 us; the launch traced here: 45.3 us
  starting transfers between devices  20.7 us (46%)
  Pallas kernels  15.9 us (35%)
  waiting for transfers between devices  8.54 us (19%)
    ppermute x10, starting transfers between devices, on_device(): lax.ppermute(message, 'seq', [(i, i ^ b) for i in range(count)])  12.8 us
    ppermute x10, waiting for transfers between devices, on_device(): lax.ppermute(message, 'seq', [(i, i ^ b) for i in range(count)])  7.93 us
    ppermute x3, starting transfers between devices, swap_head(): return lax.ppermute(x, 'head', [(0, 1), (1, 0)])  7.91 us
    pallas_call x2, Pallas kernels, intra(): pl.pallas_call(intra_kernel, out_shape=(shape((rows, group_width), BF16),...  5.53 us
    pallas_call x1, Pallas kernels, on_device(): pl.pallas_call(stage_kernel, out_shape=shape(q_weight.shape, BF16), in_sp...  2.2 us
    pallas_call x1, Pallas kernels, on_device(): pl.pallas_call(own_half_kernel, out_shape=(shape(tokens.shape, BF16), sha...  2.06 us
    pallas_call x1, Pallas kernels, on_device(): pl.pallas_call(lambda *refs: norm_kernel(ROUNDS[-1], kv_heads, *refs), ou...  1.81 us
    pallas_call x2, Pallas kernels, on_device(): pl.pallas_call(add_kernel, grid=(ADD_STEPS,), out_shape=shape((rows, half...  1.81 us
  transfers between devices with their start and end apart: 13, of which 6 were waited for; matrix products, arithmetic and copies ran while one was open for 0% of the time, Pallas kernels for 26%

profile of v12, /device:TPU:1, one launch (start us, length us, event | category | flops | bytes accessed | tf_op | source)
XLA Modules:
  0.0 45.3 jit_solution(3779607377342718199)
XLA Ops:
  0.0 3.2 %collective-permute-start = (bf16[512,1024]{1,0:T(8,128)(2,1)}, bf16[512,1024]{1,0:T(8,128)(2,1)S(1)}, u32[]{:S(2)}, u32[]{:S(2)}) collective-permute-start(bf16[512,1024]{1,0:T(8,128)(2,1)} %own_hbm.1), channel_id=1, source_target_pairs={{0,1},{1,0},{2,3},{3,2},{4,5},{5,4},{6,7},{7,6},{8,9},{9,8},{10,11... | collective-permute-start | bytes 3145736 | tf_op jit(solution)/shard_map/ppermute | solution.py:224
  3.2 2.1 %own_half.1 = (bf16[512,1024]{1,0:T(8,128)(2,1)S(1)}, bf16[2048,256]{1,0:T(8,128)(2,1)S(1)}, bf16[2048,256]{1,0:T(8,128)(2,1)S(1)}, f32[512,256]{1,0:T(8,128)S(1...) custom-call(s32[1]{0:T(128)} %bitcast.core_ref.refs_0_, s32[1,512]{1,0:T(1,128)} %bitcast.5, ...), custom_call_target="tpu_custom_call" | custom-call | tf_op jit(solution)/shard_map/own_half/pallas_call | solution.py:239
  5.3 0.4 collective-permute-done.other_ref
  5.7 1.0 %key_value.1 = (bf16[512,256]{1,0:T(8,128)(2,1)S(1)}, bf16[512,256]{1,0:T(8,128)(2,1)S(1)}, bf16[264,128]{1,0:T(8,128)(2,1)S(1)}) custom-call(s32[1]{0:T(128)} %bitcast.core_ref.refs_0_, bf16[512,1024]{1,0:T(8,128)(2,1)S(1)} %collective-permute-done.other_ref, f32[512,256]{1,0:T(8,128)S(1)} %get-tuple-element.37.k_part_ref, ...), custom_call_target="tpu_custom_call" | custom-call | tf_op jit(solution)/shard_map/key_value/pallas_call | solution.py:257
  6.7 2.7 %collective-permute-start.3 = (bf16[264,128]{1,0:T(8,128)(2,1)S(1)}, bf16[264,128]{1,0:T(8,128)(2,1)S(1)}, u32[]{:S(2)}, u32[]{:S(2)}) collective-permute-start(bf16[264,128]{1,0:T(8,128)(2,1)S(1)} %get-tuple-element.41.refs_2_.after_ref), channel_id=1, source_target_pairs={{0,6},{2,4},{4,2},{6,0},{8,14},{10,12},{12,10},{14,8},{16,22},{18,... | collective-permute-start | bytes 202760 | tf_op jit(solution)/shard_map/ppermute | solution.py:294
  9.4 0.0 collective-permute-start.2
  9.4 0.9 %collective-permute-start.1 = (bf16[264,128]{1,0:T(8,128)(2,1)S(1)}, bf16[264,128]{1,0:T(8,128)(2,1)S(1)}, u32[]{:S(2)}, u32[]{:S(2)}) collective-permute-start(bf16[264,128]{1,0:T(8,128)(2,1)S(1)} %get-tuple-element.41.refs_2_.after_ref), channel_id=1, source_target_pairs={{0,2},{2,0},{4,6},{6,4},{8,10},{10,8},{12,14},{14,12},{16,18},{18,... | collective-permute-start | bytes 202760 | tf_op jit(solution)/shard_map/ppermute | solution.py:294
  10.4 2.2 %stage.1.wq_ref = bf16[2048,1024]{1,0:T(8,128)(2,1)S(1)} custom-call(bf16[264,128]{1,0:T(8,128)(2,1)S(1)} %get-tuple-element.41.refs_2_.after_ref, bf16[2048,1024]{1,0:T(8,128)(2,1)} %weight_hbm.1), custom_call_target="tpu_custom_call" | custom-call | tf_op jit(solution)/shard_map/stage/pallas_call | solution.py:296
  12.6 0.0 collective-permute-done.3.refs_5_
  12.6 3.0 %collective-permute-done.2.refs_4_ = bf16[264,128]{1,0:T(8,128)(2,1)S(1)} collective-permute-done((bf16[264,128]{1,0:T(8,128)(2,1)S(1)}, bf16[264,128]{1,0:T(8,128)(2,1)S(1)}, u32[]{:S(2)}, u32[]{:S(2)}) %collective-permute-start.2) | collective-permute-done | bytes 67616 | tf_op jit(solution)/shard_map/ppermute | solution.py:294
  15.6 0.1 combine.3
  15.7 2.8 %collective-permute-start.4 = (bf16[264,128]{1,0:T(8,128)(2,1)S(1)}, bf16[264,128]{1,0:T(8,128)(2,1)S(1)}, u32[]{:S(2)}, u32[]{:S(2)}) collective-permute-start(bf16[264,128]{1,0:T(8,128)(2,1)S(1)} %get-tuple-element.43.refs_2_), channel_id=1, source_target_pairs={{0,12},{2,14},{4,8},{6,10},{8,4},{10,6},{12,0},{14,2},{16,28},{18,... | collective-permute-start | bytes 202760 | tf_op jit(solution)/shard_map/ppermute | solution.py:294
  18.5 2.6 %collective-permute-done.4.refs_3_ = bf16[264,128]{1,0:T(8,128)(2,1)S(1)} collective-permute-done((bf16[264,128]{1,0:T(8,128)(2,1)S(1)}, bf16[264,128]{1,0:T(8,128)(2,1)S(1)}, u32[]{:S(2)}, u32[]{:S(2)}) %collective-permute-start.4) | collective-permute-done | bytes 67616 | tf_op jit(solution)/shard_map/ppermute | solution.py:294
  21.1 1.9 %collective-permute-start.7 = (bf16[264,128]{1,0:T(8,128)(2,1)S(1)}, bf16[264,128]{1,0:T(8,128)(2,1)S(1)}, u32[]{:S(2)}, u32[]{:S(2)}) collective-permute-start(bf16[264,128]{1,0:T(8,128)(2,1)S(1)} %get-tuple-element.45.refs_2_), channel_id=1, source_target_pairs={{0,32},{2,34},{4,36},{6,38},{8,40},{10,42},{12,44},{14,46},{16,48}... | collective-permute-start | bytes 202760 | tf_op jit(solution)/shard_map/ppermute | solution.py:294
  23.0 0.9 %collective-permute-start.6 = (bf16[264,128]{1,0:T(8,128)(2,1)S(1)}, bf16[264,128]{1,0:T(8,128)(2,1)S(1)}, u32[]{:S(2)}, u32[]{:S(2)}) collective-permute-start(bf16[264,128]{1,0:T(8,128)(2,1)S(1)} %get-tuple-element.45.refs_2_), channel_id=1, source_target_pairs={{0,48},{2,50},{4,52},{6,54},{8,56},{10,58},{12,60},{14,62},{16,32}... | collective-permute-start | bytes 202760 | tf_op jit(solution)/shard_map/ppermute | solution.py:294
  23.9 2.8 %intra_0.1 = (bf16[512,512]{1,0:T(8,128)(2,1)S(1)}, f32[512,512]{1,0:T(8,128)S(1)}) custom-call(s32[1]{0:T(128)} %bitcast.core_ref.refs_0_, bf16[512,1024]{1,0:T(8,128)(2,1)S(1)} %get-tuple-element.49.own_ref, bf16[512,1024]{1,0:T(8,128)(2,1)S(1)} %collective-permute-done.other_ref, bf16[2048,1024]{1,0:T(8,128)(2,1)S(1)} %stage.1.wq_ref, ...), custom_call_target="tpu_custom_call" | custom-call | tf_op jit(solution)/shard_map/intra_0/pallas_call | solution.py:271
  26.7 0.0 copy-start
  26.7 0.0 copy-start.1
  26.7 1.6 %collective-permute-done.6.refs_4_ = bf16[264,128]{1,0:T(8,128)(2,1)S(1)} collective-permute-done((bf16[264,128]{1,0:T(8,128)(2,1)S(1)}, bf16[264,128]{1,0:T(8,128)(2,1)S(1)}, u32[]{:S(2)}, u32[]{:S(2)}) %collective-permute-start.6) | collective-permute-done | bytes 67616 | tf_op jit(solution)/shard_map/ppermute | solution.py:294
  28.3 0.1 combine.5
  28.4 2.8 %collective-permute-start.10 = (bf16[264,128]{1,0:T(8,128)(2,1)S(1)}, bf16[264,128]{1,0:T(8,128)(2,1)S(1)}, u32[]{:S(2)}, u32[]{:S(2)}) collective-permute-start(bf16[264,128]{1,0:T(8,128)(2,1)S(1)} %get-tuple-element.57), channel_id=1, source_target_pairs={{0,128},{2,130},{4,132},{6,134},{8,136},{10,138},{12,140},{14,142}... | collective-permute-start | bytes 202760 | tf_op jit(solution)/shard_map/ppermute | solution.py:294
  31.2 0.8 %collective-permute-start.9 = (bf16[264,128]{1,0:T(8,128)(2,1)S(1)}, bf16[264,128]{1,0:T(8,128)(2,1)S(1)}, u32[]{:S(2)}, u32[]{:S(2)}) collective-permute-start(bf16[264,128]{1,0:T(8,128)(2,1)S(1)} %get-tuple-element.57), channel_id=1, source_target_pairs={{0,192},{2,194},{4,196},{6,198},{8,200},{10,202},{12,204},{14,206}... | collective-permute-start | bytes 202760 | tf_op jit(solution)/shard_map/ppermute | solution.py:294
  32.0 0.0 collective-permute-start.8
  32.0 2.8 %intra_1.1 = (bf16[512,512]{1,0:T(8,128)(2,1)S(1)}, f32[512,512]{1,0:T(8,128)S(1)}) custom-call(s32[1]{0:T(128)} %bitcast.core_ref.refs_0_, bf16[512,1024]{1,0:T(8,128)(2,1)S(1)} %get-tuple-element.49.own_ref, bf16[512,1024]{1,0:T(8,128)(2,1)S(1)} %collective-permute-done.other_ref, bf16[2048,1024]{1,0:T(8,128)(2,1)S(1)} %stage.1.wq_ref, ...), custom_call_target="tpu_custom_call" | custom-call | tf_op jit(solution)/shard_map/intra_1/pallas_call | solution.py:271
  34.8 0.8 %collective-permute-done.9.refs_4_ = bf16[264,128]{1,0:T(8,128)(2,1)S(1)} collective-permute-done((bf16[264,128]{1,0:T(8,128)(2,1)S(1)}, bf16[264,128]{1,0:T(8,128)(2,1)S(1)}, u32[]{:S(2)}, u32[]{:S(2)}) %collective-permute-start.9) | collective-permute-done | bytes 67616 | tf_op jit(solution)/shard_map/ppermute | solution.py:294
  35.6 1.8 %norm.1 = (bf16[512,1024]{1,0:T(8,128)(2,1)S(1)}, bf16[256,1024]{1,0:T(8,128)(2,1)S(1)}, bf16[256,1024]{1,0:T(8,128)(2,1)S(1)}) custom-call(s32[1]{0:T(128)} %bitcast.core_ref.refs_0_, s32[1]{0:T(128)} %bitcast.1.refs_0_.refs_1_, f32[256,128]{1,0:T(8,128)S(1)} %get-tuple-element.47.refs_2_, bf16[264,128]{1,0:T(8,128)(2,1)S(1)} %collective-permute-done.8.refs_3_, ...), custom_call_target="tpu_custom_call" | custom-call | tf_op jit(solution)/shard_map/norm/pallas_call | solution.py:326
  37.4 4.6 %collective-permute-start.12 = (bf16[256,1024]{1,0:T(8,128)(2,1)S(1)}, bf16[256,1024]{1,0:T(8,128)(2,1)S(1)}, u32[]{:S(2)}, u32[]{:S(2)}) collective-permute-start(bf16[256,1024]{1,0:T(8,128)(2,1)S(1)} %get-tuple-element.66), channel_id=1, source_target_pairs={{0,1},{1,0},{2,3},{3,2},{4,5},{5,4},{6,7},{7,6},{8,9},{9,8},{10,11... | collective-permute-start | bytes 1572872 | tf_op jit(solution)/shard_map/ppermute | solution.py:224
  41.9 0.1 collective-permute-start.11
  42.0 1.3 %own.1.mine_ref = f32[512,1024]{1,0:T(8,128)S(1)} custom-call(s32[1]{0:T(128)} %bitcast.core_ref.refs_0_, bf16[512,1024]{1,0:T(8,128)(2,1)S(1)} %get-tuple-element.64.normed_ref, bf16[1024,2048]{1,0:T(8,128)(2,1)S(1)} %copy-done), custom_call_target="tpu_custom_call" | custom-call | tf_op jit(solution)/shard_map/own/pallas_call | solution.py:335
  43.3 0.2 collective-permute-done.12.theirs_ref
  43.5 0.9 %add_0.1.refs_0_ = bf16[512,1024]{1,0:T(8,128)(2,1)} custom-call(f32[512,1024]{1,0:T(8,128)S(1)} %own.1.mine_ref, bf16[256,1024]{1,0:T(8,128)(2,1)S(1)} %collective-permute-done.12.theirs_ref), custom_call_target="tpu_custom_call" | custom-call | tf_op jit(solution)/shard_map/add_0/pallas_call | solution.py:346
  44.4 0.9 %add_1.1 = bf16[512,1024]{1,0:T(8,128)(2,1)} custom-call(f32[512,1024]{1,0:T(8,128)S(1)} %own.1.mine_ref, bf16[256,1024]{1,0:T(8,128)(2,1)S(1)} %collective-permute-done.11.theirs_ref, bf16[512,1024]{1,0:T(8,128)(2,1)} %add_0.1.refs_0_), custom_call_target="tpu_custom_call", output_to_operand_aliasing={{}: (2, {})} | custom-call | tf_op jit(solution)/shard_map/add_1/pallas_call | solution.py:346
  (10 shorter events, 0.1 us)
Async XLA Ops:
  0.0 5.7 %collective-permute-start = (bf16[512,1024]{1,0:T(8,128)(2,1)}, bf16[512,1024]{1,0:T(8,128)(2,1)S(1)}, u32[]{:S(2)}, u32[]{:S(2)}) collective-permute-start(bf16[512,1024]{1,0:T(8,128)(2,1)} %own_hbm.1), channel_id=1, source_target_pairs={{0,1},{1,0},{2,3},{3,2},{4,5},{5,4},{6,7},{7,6},{8,9},{9,8},{10,11... | collective-permute-start | bytes 3145736 | tf_op jit(solution)/shard_map/ppermute | solution.py:224
  6.7 5.9 %collective-permute-start.3 = (bf16[264,128]{1,0:T(8,128)(2,1)S(1)}, bf16[264,128]{1,0:T(8,128)(2,1)S(1)}, u32[]{:S(2)}, u32[]{:S(2)}) collective-permute-start(bf16[264,128]{1,0:T(8,128)(2,1)S(1)} %get-tuple-element.41.refs_2_.after_ref), channel_id=1, source_target_pairs={{0,6},{2,4},{4,2},{6,0},{8,14},{10,12},{12,10},{14,8},{16,22},{18,... | collective-permute-start | bytes 202760 | tf_op jit(solution)/shard_map/ppermute | solution.py:294
  9.4 6.1 %collective-permute-start.2 = (bf16[264,128]{1,0:T(8,128)(2,1)S(1)}, bf16[264,128]{1,0:T(8,128)(2,1)S(1)}, u32[]{:S(2)}, u32[]{:S(2)}) collective-permute-start(bf16[264,128]{1,0:T(8,128)(2,1)S(1)} %get-tuple-element.41.refs_2_.after_ref), channel_id=1, source_target_pairs={{0,4},{2,6},{4,0},{6,2},{8,12},{10,14},{12,8},{14,10},{16,20},{18,... | collective-permute-start | bytes 202760 | tf_op jit(solution)/shard_map/ppermute | solution.py:294
  9.4 6.1 %collective-permute-start.1 = (bf16[264,128]{1,0:T(8,128)(2,1)S(1)}, bf16[264,128]{1,0:T(8,128)(2,1)S(1)}, u32[]{:S(2)}, u32[]{:S(2)}) collective-permute-start(bf16[264,128]{1,0:T(8,128)(2,1)S(1)} %get-tuple-element.41.refs_2_.after_ref), channel_id=1, source_target_pairs={{0,2},{2,0},{4,6},{6,4},{8,10},{10,8},{12,14},{14,12},{16,18},{18,... | collective-permute-start | bytes 202760 | tf_op jit(solution)/shard_map/ppermute | solution.py:294
  15.7 5.4 %collective-permute-start.4 = (bf16[264,128]{1,0:T(8,128)(2,1)S(1)}, bf16[264,128]{1,0:T(8,128)(2,1)S(1)}, u32[]{:S(2)}, u32[]{:S(2)}) collective-permute-start(bf16[264,128]{1,0:T(8,128)(2,1)S(1)} %get-tuple-element.43.refs_2_), channel_id=1, source_target_pairs={{0,12},{2,14},{4,8},{6,10},{8,4},{10,6},{12,0},{14,2},{16,28},{18,... | collective-permute-start | bytes 202760 | tf_op jit(solution)/shard_map/ppermute | solution.py:294
  21.1 5.6 %collective-permute-start.7 = (bf16[264,128]{1,0:T(8,128)(2,1)S(1)}, bf16[264,128]{1,0:T(8,128)(2,1)S(1)}, u32[]{:S(2)}, u32[]{:S(2)}) collective-permute-start(bf16[264,128]{1,0:T(8,128)(2,1)S(1)} %get-tuple-element.45.refs_2_), channel_id=1, source_target_pairs={{0,32},{2,34},{4,36},{6,38},{8,40},{10,42},{12,44},{14,46},{16,48}... | collective-permute-start | bytes 202760 | tf_op jit(solution)/shard_map/ppermute | solution.py:294
  23.0 5.3 %collective-permute-start.6 = (bf16[264,128]{1,0:T(8,128)(2,1)S(1)}, bf16[264,128]{1,0:T(8,128)(2,1)S(1)}, u32[]{:S(2)}, u32[]{:S(2)}) collective-permute-start(bf16[264,128]{1,0:T(8,128)(2,1)S(1)} %get-tuple-element.45.refs_2_), channel_id=1, source_target_pairs={{0,48},{2,50},{4,52},{6,54},{8,56},{10,58},{12,60},{14,62},{16,32}... | collective-permute-start | bytes 202760 | tf_op jit(solution)/shard_map/ppermute | solution.py:294
  23.9 4.4 %collective-permute-start.5 = (bf16[264,128]{1,0:T(8,128)(2,1)S(1)}, bf16[264,128]{1,0:T(8,128)(2,1)S(1)}, u32[]{:S(2)}, u32[]{:S(2)}) collective-permute-start(bf16[264,128]{1,0:T(8,128)(2,1)S(1)} %get-tuple-element.45.refs_2_), channel_id=1, source_target_pairs={{0,16},{2,18},{4,20},{6,22},{8,24},{10,26},{12,28},{14,30},{16,0},... | collective-permute-start | bytes 202760 | tf_op jit(solution)/shard_map/ppermute | solution.py:294
  26.7 8.9 %copy-start = (bf16[1024,2048]{1,0:T(8,128)(2,1)S(1)}, bf16[1024,2048]{1,0:T(8,128)(2,1)}, u32[]{:S(2)}) copy-start(bf16[1024,2048]{1,0:T(8,128)(2,1)} %weight_ref.1) | copy-start | bytes 12582916
  26.7 8.9 %copy-start.1 = (f32[1024]{0:T(1024)S(1)}, f32[1024]{0:T(1024)}, u32[]{:S(2)}) copy-start(f32[1024]{0:T(1024)} %param.11) | copy-start | bytes 12292
  28.4 6.4 %collective-permute-start.10 = (bf16[264,128]{1,0:T(8,128)(2,1)S(1)}, bf16[264,128]{1,0:T(8,128)(2,1)S(1)}, u32[]{:S(2)}, u32[]{:S(2)}) collective-permute-start(bf16[264,128]{1,0:T(8,128)(2,1)S(1)} %get-tuple-element.57), channel_id=1, source_target_pairs={{0,128},{2,130},{4,132},{6,134},{8,136},{10,138},{12,140},{14,142}... | collective-permute-start | bytes 202760 | tf_op jit(solution)/shard_map/ppermute | solution.py:294
  31.2 4.3 %collective-permute-start.9 = (bf16[264,128]{1,0:T(8,128)(2,1)S(1)}, bf16[264,128]{1,0:T(8,128)(2,1)S(1)}, u32[]{:S(2)}, u32[]{:S(2)}) collective-permute-start(bf16[264,128]{1,0:T(8,128)(2,1)S(1)} %get-tuple-element.57), channel_id=1, source_target_pairs={{0,192},{2,194},{4,196},{6,198},{8,200},{10,202},{12,204},{14,206}... | collective-permute-start | bytes 202760 | tf_op jit(solution)/shard_map/ppermute | solution.py:294
  32.0 3.6 %collective-permute-start.8 = (bf16[264,128]{1,0:T(8,128)(2,1)S(1)}, bf16[264,128]{1,0:T(8,128)(2,1)S(1)}, u32[]{:S(2)}, u32[]{:S(2)}) collective-permute-start(bf16[264,128]{1,0:T(8,128)(2,1)S(1)} %get-tuple-element.57), channel_id=1, source_target_pairs={{0,64},{2,66},{4,68},{6,70},{8,72},{10,74},{12,76},{14,78},{16,80}... | collective-permute-start | bytes 202760 | tf_op jit(solution)/shard_map/ppermute | solution.py:294
  37.4 6.1 %collective-permute-start.12 = (bf16[256,1024]{1,0:T(8,128)(2,1)S(1)}, bf16[256,1024]{1,0:T(8,128)(2,1)S(1)}, u32[]{:S(2)}, u32[]{:S(2)}) collective-permute-start(bf16[256,1024]{1,0:T(8,128)(2,1)S(1)} %get-tuple-element.66), channel_id=1, source_target_pairs={{0,1},{1,0},{2,3},{3,2},{4,5},{5,4},{6,7},{7,6},{8,9},{9,8},{10,11... | collective-permute-start | bytes 1572872 | tf_op jit(solution)/shard_map/ppermute | solution.py:224
  41.9 2.5 %collective-permute-start.11 = (bf16[256,1024]{1,0:T(8,128)(2,1)S(1)}, bf16[256,1024]{1,0:T(8,128)(2,1)S(1)}, u32[]{:S(2)}, u32[]{:S(2)}) collective-permute-start(bf16[256,1024]{1,0:T(8,128)(2,1)S(1)} %get-tuple-element.65), channel_id=1, source_target_pairs={{0,1},{1,0},{2,3},{3,2},{4,5},{5,4},{6,7},{7,6},{8,9},{9,8},{10,11... | collective-permute-start | bytes 1572872 | tf_op jit(solution)/shard_map/ppermute | solution.py:224
